TPU v7x, 128 devices: a whole 4x4x4 slice. The times are simulated.
128 devices in a mesh: img: 16 (over x_hi, y, core), pose: 8 (over z, x_lo).
Axes of the slice: x: 4 (x_hi: 2, x_lo: 2; x = x_hi * 2 + x_lo), y: 4, z: 4, core: 2. Of those that a mesh axis runs over, the one named last changes fastest.
Arguments:
- images: bfloat16 [2048, 8192], P('img'), may hold values from -240 to 240
- shift_phase: float32 [8, 4096], replicated, may hold values from -3.140625 to 3.140625
- noise_weight: float32 [8192], replicated, may hold values from 0.005 to 0.05
- refs: bfloat16 [3072, 8192], P('pose', 'img'), may hold values from -6 to 6
- routing: int32 [98304, 1], P(('pose', 'img')), may hold values from 0 to 127; in each aligned block of 768 rows (0 to 767, 768 to 1535, ...) at most 12 rows name the same one
- stencil: int32 [98304], P(('pose', 'img')), may hold values from 0 to 7
- interp: bfloat16 [128, 8, 256, 512], P(('img', 'pose')), may hold values from -48 to 48
Outputs:
- volume: float32 [128, 512], P(('img', 'pose'))
- evidence: float32 [2048], P('img')
Inputs may be any that keep to these rules, and one draw needn't show every extreme that they name: `routing`: among the rows of one device no brick is named more than 12 times, a bound that some block reaches there.
All inputs are finite; a program needn't handle non-finite values.
Results may differ from a plain program's by a relative error of at most 0.0052.
Values may be sent and summed in bfloat16 or wider, within the bound.
No kernel may reach another device: no remote copies, remote signals or barrier semaphores. Data moves between devices by JAX's collectives and lax.ppermute only.
A program may use at most 192 MiB of HBM per device.

v0:
```python
import jax
import jax.numpy as jnp
from jax import lax
from jax.sharding import Mesh
from jax.sharding import PartitionSpec as P

PIX = 4096
TRANS = 8
BLOCK = 128
STENCILS = 8
IMG = ("img_0", "img_1", "img_2")
IMG_POSE = ("img_0", "img_1", "img_2", "pose")
POSE_IMG = ("pose", "img_0", "img_1", "img_2")


def from_everyone(x, axis):
    size = lax.axis_size(axis)
    return lax.all_to_all(jnp.broadcast_to(x[None], (size, *x.shape)), axis, 0, 0, tiled=True)


def all_in_one(x, axis):
    leaves = jax.tree.leaves(x)
    turns = sorted(range(len(leaves)), key=lambda k: -leaves[k].size)
    width = (1, *leaves[turns[0]].shape)[-1]
    lines = [
        jnp.pad(leaves[k].reshape(-1), (0, -leaves[k].size % width)).reshape(-1, width)
        for k in turns
    ]
    both, at, found = (from_everyone(jnp.concatenate(lines), axis), 0, {})
    for k, line in zip(turns, lines):
        piece = both[:, at : at + len(line)].reshape(len(both), -1)
        found[k] = piece[:, : leaves[k].size].reshape(-1, *leaves[k].shape)
        at += len(line)
    numbers = iter(range(len(leaves)))
    return jax.tree.map(lambda _: found[next(numbers)], x)


def combined_pairwise(pieces, combine):
    while len(jax.tree.leaves(pieces)[0]) > 1:
        pieces = jax.vmap(combine)(
            *(jax.tree.map(lambda part: part[side::2], pieces) for side in (0, 1))
        )
    return jax.tree.map(lambda part: part[0], pieces)


def combined_all(x, axis, combine):
    pieces = all_in_one(x, axis)
    return combined_pairwise(pieces, combine)


def in_blocks(x, dim, size):
    before, after = (x.shape[:dim], x.shape[dim + 1 :])
    return jnp.moveaxis(x.reshape(*before, size, -1, *after), dim, 0)


def summed_rows_2(x, chips, core, dim):
    sizes = (lax.axis_size(chips), lax.axis_size(core))
    tiles = in_blocks(x, dim, sizes[0] * sizes[1])
    inside = tiles.shape[1:]
    tiles = tiles.reshape(*sizes, *inside).swapaxes(0, 1).reshape(-1, *inside)
    tiles = lax.psum_scatter(tiles, core, scatter_dimension=0, tiled=True)
    return lax.psum_scatter(tiles, chips, scatter_dimension=0, tiled=True)[0]


def joined_along(tiles, dim):
    tiles = jnp.moveaxis(tiles, 0, dim)
    dims = tiles.shape
    return tiles.reshape(*dims[:dim], dims[dim] * dims[dim + 1], *dims[dim + 2 :])


def joined_exchange(x, axis, axes, splits, concats):
    sizes = [lax.axis_size(a) for a in axes]
    tiles = in_blocks(x, splits[0], sizes[0])
    tiles = jnp.moveaxis(in_blocks(tiles, splits[1] + 1, sizes[1]), 0, 1)
    inside = tiles.shape[2:]
    tiles = tiles.reshape(-1, *inside)
    tiles = lax.all_to_all(tiles, axis, split_axis=0, concat_axis=0, tiled=True)
    tiles = joined_along(tiles.reshape(*sizes, *inside), concats[0] + 1)
    return joined_along(tiles, concats[1])


def translated(images, shift_phase, noise_weight):
    count = images.shape[0]
    blocks = images.astype(jnp.float32).reshape(count, 1, PIX // BLOCK, 2, BLOCK)
    real_part = blocks[:, :, :, 0, :]
    imag_part = blocks[:, :, :, 1, :]
    angles = shift_phase.reshape(1, TRANS, PIX // BLOCK, BLOCK)
    cosine = jnp.cos(angles)
    sine = jnp.sin(angles)
    new_real = real_part * cosine + imag_part * sine
    new_imag = imag_part * cosine - real_part * sine
    stacked = jnp.stack([new_real, new_imag], axis=3).reshape(count * TRANS, 2 * PIX)
    return (stacked * noise_weight[None, :]).astype(jnp.bfloat16)


def combine_parts(earlier, later):
    peak_first, total_first = earlier
    peak_second, total_second = later
    highest = jnp.maximum(peak_first, peak_second)
    joined = total_first * jnp.exp(peak_first - highest) + total_second * jnp.exp(
        peak_second - highest
    )
    return (highest, joined)


def body(images, shift_phase, noise_weight, refs, routing, stencil, interp):
    weighted = translated(images, shift_phase, noise_weight)
    image_rows = weighted.shape[0]
    image_count = images.shape[0]
    pose_count = refs.shape[0]
    columns = lax.all_gather(refs, IMG, axis=1, tiled=True)
    partial_scores = lax.dot_general(
        weighted, columns, (((1,), (1,)), ((), ())), preferred_element_type=jnp.float32
    )
    columns_wide = columns.astype(jnp.float32)
    half_norm = 0.5 * jnp.sum(columns_wide * columns_wide * noise_weight[None, :], axis=1)
    scores, half_norm = (partial_scores, half_norm)
    grouped = (scores - half_norm[None, :]).reshape(image_count, TRANS * pose_count)
    local_peak = jnp.max(grouped, axis=1)
    local_expo = jnp.exp(grouped - local_peak[:, None])
    local_total = jnp.sum(local_expo, axis=1)
    peak, total = combined_all((local_peak, local_total), "pose", combine_parts)
    expo = jnp.exp(grouped - peak[:, None])
    evidence = peak + jnp.log(total)
    posterior = (expo / total[:, None]).astype(jnp.bfloat16).reshape(image_rows, pose_count)
    img_count = lax.axis_size(IMG)
    share = pose_count // img_count
    accum = summed_rows_2(
        lax.dot_general(
            posterior, weighted, (((0,), (0,)), ((), ())), preferred_element_type=jnp.float32
        ),
        ("img_0", "img_1"),
        "img_2",
        0,
    )
    block_rows = accum.astype(jnp.bfloat16).reshape(share * (PIX // BLOCK), 2 * BLOCK)
    pose_axis = lax.axis_size("pose")
    devices = img_count * pose_axis
    row_count = block_rows.shape[0]
    capacity = max(2, 2 * row_count // devices)
    target = routing[:, 0]
    one_hot = (target[:, None] == jnp.arange(devices, dtype=jnp.int32)[None, :]).astype(jnp.int32)
    before = jnp.cumsum(one_hot, axis=0) - one_hot
    slot_index = jnp.sum(before * one_hot, axis=1)
    rows_buffer = (
        jnp.zeros((devices, capacity, 2 * BLOCK), jnp.bfloat16)
        .at[target, slot_index]
        .set(block_rows)
    )
    stencil_buffer = (
        jnp.full((devices, capacity), STENCILS, jnp.int32).at[target, slot_index].set(stencil)
    )
    split_rows = rows_buffer.reshape(img_count, pose_axis, capacity, 2 * BLOCK)
    split_stencil = stencil_buffer.reshape(img_count, pose_axis, capacity)
    got_rows, got_stencil = (
        joined_exchange(split_rows, IMG_POSE, (IMG, "pose"), (0, 1), (0, 1)),
        joined_exchange(split_stencil, IMG_POSE, (IMG, "pose"), (0, 1), (0, 1)),
    )
    flat_rows = got_rows.reshape(devices * capacity, 2 * BLOCK)
    flat_stencil = got_stencil.reshape(devices * capacity)
    selector = (jnp.arange(STENCILS, dtype=jnp.int32)[:, None] == flat_stencil[None, :]).astype(
        jnp.bfloat16
    )
    gathered = jnp.dot(selector, flat_rows, preferred_element_type=jnp.float32).astype(jnp.bfloat16)
    gathered = gathered.reshape(1, STENCILS * 2 * BLOCK)
    matrices = interp.reshape(STENCILS * 2 * BLOCK, interp.shape[3])
    summed_volume = jnp.dot(gathered, matrices, preferred_element_type=jnp.float32)
    received = jnp.sum((flat_stencil < STENCILS).astype(jnp.float32))
    volume = summed_volume * lax.rsqrt(1.0 + received)
    return (volume, evidence)


def solution(mesh):
    finer = Mesh(
        mesh.devices.reshape(2, 4, 2, mesh.shape["pose"]), ("img_0", "img_1", "img_2", "pose")
    )
    return jax.shard_map(
        body,
        mesh=finer,
        in_specs=(
            P(IMG, None),
            P(),
            P(),
            P("pose", IMG),
            P(POSE_IMG, None),
            P(POSE_IMG),
            P(IMG_POSE, None, None, None),
        ),
        out_specs=(P(IMG_POSE, None), P(IMG)),
        check_vma=False,
    )
```

profile of v0, /device:TPU:0, one launch (start us, length us, event | category | flops | bytes accessed | tf_op | source)
XLA Modules:
  0.0 343.7 jit_solution(1104705088797828917)
XLA Ops:
  7.2 0.7 all-gather.2.cloned.1.call-update
  8.0 6.6 %reshape.184 = f32[128,1,32,2,128]{4,3,2,0,1:T(2,128)} reshape(bf16[128,8192]{1,0:T(8,128)(2,1)} %param.7) | data formatting | bytes 6291456 | tf_op jit(solution)/shard_map/reshape | solution.py:84
  14.5 1.4 cosine_bitcast_fusion
  15.9 7.9 %fusion.12 = (f32[128,1,32,1,128]{4,3,2,0,1:T(1,128)S(1)}, f32[128,1,32,1,128]{4,3,2,0,1:T(1,128)S(1)}) fusion(f32[128,1,32,2,128]{4,3,2,0,1:T(2,128)} %reshape.184), kind=kLoop, calls=%fused_computation.46 | loop fusion | bytes 8388608 | tf_op jit(solution)/shard_map/slice | solution.py:85
  23.8 7.7 %multiply_add_fusion = (f32[128,8,32,1,128]{4,1,3,2,0:T(8,128)S(1)}, f32[128,8,32,1,128]{4,1,3,2,0:T(8,128)}) fusion(f32[8,32,128]{2,0,1:T(8,128)S(1)} %get-tuple-element.16, f32[128,32,128]{2,1,0:T(8,128)S(1)} %bitcast.86, f32[8,32,128]{2,0,1:T(8,128)S(1)} %get-tuple-element.15, f32[128,32,128]{2,1,0:T(8,128)S(1)} %bitcast.85), kind=kLoop, calls=%fused_computation.8 | loop fusion | flops 25165824 | bytes 38010880 | tf_op jit(solution)/shard_map/add | solution.py:90
  31.5 23.5 %multiply_convert_fusion = (bf16[128,8,32,2,128]{4,1,3,2,0:T(8,128)(2,1)}, f32[128,8,32,2,128]{4,1,3,2,0:T(8,128)}) fusion(f32[32,2,128]{2,1,0:T(2,128)S(1)} %bitcast.91, f32[128,8,32,1,128]{4,1,3,2,0:T(8,128)} %get-tuple-element.12, f32[128,8,32,1,128]{4,1,3,2,0:T(8,128)S(1)} %get-tuple-element.11), kind=kLoop, calls=%fused_computation.3 | loop fusion | flops 25165824 | bytes 83918848 | tf_op jit(solution)/shard_map/convert_element_type | solution.py:93
  55.1 23.9 %all-gather.2.cloned.1.call-done = bf16[384,8192]{1,0:T(8,128)(2,1)} async-done(((bf16[384,512]{1,0:T(8,128)(2,1)}), bf16[384,8192]{1,0:T(8,128)(2,1)}) %all-gather.2.cloned.1.call-update) | async-done | bytes 6291472 | tf_op jit(solution)/shard_map/all_gather | solution.py:111
  78.9 4.5 %multiply_reduce_fusion = f32[384]{0:T(512)S(1)} fusion(bf16[384,8192]{1,0:T(8,128)(2,1)} %all-gather.2.cloned.1.call-done, f32[8192]{0:T(1024)S(1)} %copy-done.1), kind=kLoop, calls=%fused_computation.9 | loop fusion | flops 12582528 | bytes 6325760 | tf_op jit(solution)/shard_map/reduce_sum | solution.py:116
  83.5 17.2 %fusion.14 = (f32[1024]{0:T(1024)S(1)}, f32[1024,384]{0,1:T(8,128)}) fusion(f32[384]{0:T(512)S(1)} %broadcast_multiply_fusion.1, bf16[384,8192]{1,0:T(8,128)(2,1)} %all-gather.2.cloned.1.call-done, f32[1024,8192]{1,0:T(8,128)} %bitcast.82, f32[8192]{0:T(1024)S(1)} %copy-done.1), kind=kOutput, calls=%fused_computation.48 | convolution fusion | flops 6460013568 | bytes 41457152 | tf_op jit(solution)/shard_map/dot_general | solution.py:112
  100.6 0.1 reduce_max.14
  100.7 0.1 reduce_max.18
  100.8 0.1 sub.75
  100.9 0.1 sub.76
  101.0 1.6 exponential_reduce_fusion
  102.7 0.1 reduce_sum.49
  102.7 0.1 reduce_sum.50
  102.9 10.4 %all_to_all.15 = f32[8,2,128]{2,1,0:T(2,128)S(1)} all-to-all(f32[8,2,128]{2,1,0:T(2,128)S(1)} %broadcast_in_dim.8), channel_id=1, replica_groups=mesh['img_0'=2,'img_1'=4,'img_2'=2,'pose'=8] {'pose'}, dimensions={0} | all-to-all | bytes 16384 | tf_op jit(solution)/shard_map/all_to_all | solution.py:18
  113.5 0.5 log_add_fusion
  114.1 0.1 div.20
  114.1 0.1 div.21
  114.2 0.1 sub.80
  114.3 0.1 sub.81
  114.4 1.7 divide_convert_fusion
  116.1 14.9 %convolution_bitcast_fusion = f32[2,8,24,8192]{3,2,0,1:T(8,128)} fusion(bf16[8,2,24,1024]{3,2,1,0:T(8,128)(2,1)S(1)} %bitcast.89, bf16[1024,8192,1,1]{1,0,3,2:T(8,128)(2,1)} %bitcast.84), kind=kOutput, calls=%fused_computation.10 | convolution fusion | flops 6442450944 | bytes 30146560 | tf_op jit(solution)/shard_map/dot_general | solution.py:129
  131.0 10.5 %copy.21 = f32[2,8,24,8192]{3,2,1,0:T(8,128)} copy(f32[2,8,24,8192]{3,2,0,1:T(8,128)} %convolution_bitcast_fusion) | data formatting | bytes 25165824 | tf_op jit(solution)/shard_map/transpose | solution.py:60
  141.5 21.3 %reduce-scatter.3.cloned.1.call-done = f32[8,24,8192]{2,1,0:T(8,128)} async-done(((f32[16,24,8192]{2,1,0:T(8,128)}), f32[8,24,8192]{2,1,0:T(8,128)}) %reduce-scatter.3.cloned.1.call-update) | async-done | bytes 6291472 | tf_op jit(solution)/shard_map/reduce_scatter | solution.py:61
  162.9 0.1 copy.15
  163.0 0.2 fusion.4
  163.3 0.1 copy.16
  163.4 0.3 fusion.7
  163.7 36.6 %scatter_fusion = s32[128,12]{0,1:T(8,128)S(1)} fusion(s32[128,12]{0,1:T(8,128)S(1)} %broadcast_in_dim.6, s32[768]{0:T(1024)S(1)} %fusion.11, s32[768]{0:T(1024)S(1)} %copy-done.3), kind=kCustom, calls=%fused_computation | custom fusion | bytes 15360 | tf_op jit(solution)/shard_map/scatter | solution.py:151
  200.3 0.7 copy.17
  201.0 10.1 %all-to-all-start = ((s32[128,1,1,12]{3,2,1,0:T(1,128)}), s32[128,1,1,12]{3,2,1,0:T(1,128)S(1)}, u32[]{:S(2)}, u32[]{:S(2)}) async-start(s32[128,1,1,12]{3,2,1,0:T(1,128)} %copy.17), calls=%async_computation | async-start | bytes 131072 | tf_op jit(solution)/shard_map/all_to_all | solution.py:77
  211.1 56.0 %reduce-scatter.5.cloned.1.call-done = f32[1,24,8192]{2,1,0:T(8,128)} async-done(((f32[8,24,8192]{2,1,0:T(8,128)}), f32[1,24,8192]{2,1,0:T(8,128)}) %reduce-scatter.5.cloned.1.call-update) | async-done | bytes 786448 | tf_op jit(solution)/shard_map/reduce_scatter | solution.py:62
  267.1 1.2 convert_element_type.49
  268.3 0.2 reshape.193
  268.6 37.6 %scatter_fusion.1 = bf16[128,12,256]{2,0,1:T(8,128)(2,1)S(1)} fusion(bf16[128,12,256]{2,0,1:T(8,128)(2,1)S(1)} %broadcast_in_dim.7, s32[768]{0:T(1024)S(1)} %fusion.11, bf16[768,256]{1,0:T(8,128)(2,1)S(1)} %reshape.193), kind=kCustom, calls=%fused_computation.1 | custom fusion | bytes 1185792 | tf_op jit(solution)/shard_map/scatter | solution.py:148
  306.2 1.4 copy.22
  307.6 7.3 %all-to-all-start.2 = ((bf16[128,1,1,12,256]{4,3,2,1,0:T(8,128)(2,1)}), bf16[128,1,1,12,256]{4,3,2,1,0:T(8,128)(2,1)S(1)}, u32[]{:S(2)}, u32[]{:S(2)}) async-start(bf16[128,1,1,12,256]{4,3,2,1,0:T(8,128)(2,1)} %copy.22), calls=%async_computation.4 | async-start | bytes 2097152 | tf_op jit(solution)/shard_map/all_to_all | solution.py:77
  314.9 0.2 copy.24
  315.1 0.2 copy.19
  315.3 0.1 eq.49
  315.4 0.6 convert_reduce_fusion
  316.7 17.1 %all-to-all-done.2 = bf16[128,1,1,12,256]{4,3,2,1,0:T(8,128)(2,1)S(1)} async-done(((bf16[128,1,1,12,256]{4,3,2,1,0:T(8,128)(2,1)}), bf16[128,1,1,12,256]{4,3,2,1,0:T(8,128)(2,1)S(1)}, u32[]{:S(2)}, u32[]{:S(2)}) %all-to-all-start.2) | async-done | bytes 786464 | tf_op jit(solution)/shard_map/all_to_all | solution.py:77
  333.8 1.0 reshape_reshape.2
  334.8 1.3 fusion.3
  336.2 0.4 fusion.15
  336.6 0.6 broadcast_multiply_fusion
  (36 shorter events, 0.6 us)
Async XLA Ops:
  7.2 329.0 %copy-start = (bf16[1,8,256,512]{3,2,1,0:T(8,128)(2,1)S(1)}, bf16[1,8,256,512]{3,2,1,0:T(8,128)(2,1)}, u32[]{:S(2)}) copy-start(bf16[1,8,256,512]{3,2,1,0:T(8,128)(2,1)} %param.13) | copy-start | bytes 6291460
  7.2 71.8 %all-gather.2.cloned.1.call-start = ((), (), s32[]{:S(2)}) async-start(), calls=%async_computation.5 | async-start | bytes 6684672 | tf_op jit(solution)/shard_map/all_gather | solution.py:111
  7.9 154.9 %reduce-scatter.3.cloned.1.call-start = ((), (), s32[]{:S(2)}) async-start(), calls=%async_computation.6 | async-start | bytes 18874368 | tf_op jit(solution)/shard_map/reduce_scatter | solution.py:61
  23.8 7.7 %copy-start.1 = (f32[8192]{0:T(1024)S(1)}, f32[8192]{0:T(1024)}, u32[]{:S(2)}) copy-start(f32[8192]{0:T(1024)} %param.9) | copy-start | bytes 98308
  141.5 21.4 %copy-start.2 = (s32[768,1]{0,1:T(1,128)S(1)}, s32[768,1]{0,1:T(1,128)}, u32[]{:S(2)}) copy-start(s32[768,1]{0,1:T(1,128)} %param.11) | copy-start | bytes 9220
  141.5 22.3 %copy-start.3 = (s32[768]{0:T(1024)S(1)}, s32[768]{0:T(1024)}, u32[]{:S(2)}) copy-start(s32[768]{0:T(1024)} %param.12) | copy-start | bytes 9220
  141.5 125.6 %reduce-scatter.5.cloned.1.call-start = ((), (), s32[]{:S(2)}) async-start(), calls=%async_computation.7 | async-start | bytes 7077888 | tf_op jit(solution)/shard_map/reduce_scatter | solution.py:62
  201.0 106.6 %all-to-all-start = ((s32[128,1,1,12]{3,2,1,0:T(1,128)}), s32[128,1,1,12]{3,2,1,0:T(1,128)S(1)}, u32[]{:S(2)}, u32[]{:S(2)}) async-start(s32[128,1,1,12]{3,2,1,0:T(1,128)} %copy.17), calls=%async_computation | async-start | bytes 131072 | tf_op jit(solution)/shard_map/all_to_all | solution.py:77
  307.6 26.1 %all-to-all-start.2 = ((bf16[128,1,1,12,256]{4,3,2,1,0:T(8,128)(2,1)}), bf16[128,1,1,12,256]{4,3,2,1,0:T(8,128)(2,1)S(1)}, u32[]{:S(2)}, u32[]{:S(2)}) async-start(bf16[128,1,1,12,256]{4,3,2,1,0:T(8,128)(2,1)} %copy.22), calls=%async_computation.4 | async-start | bytes 2097152 | tf_op jit(solution)/shard_map/all_to_all | solution.py:77
Sparse Core Ops, SparseCore 0:
  10.3 68.6 all-gather.1
  141.6 21.1 reduce-scatter.2
  166.7 100.4 reduce-scatter.4
where the time goes:
time: 345 us; the launch traced here: 344 us
  waiting for transfers between devices  119 us (34%)
  local copies, waits for them, and re-layouts  106 us (31%)
  other arithmetic  42.8 us (12%)
  matrix products  33.8 us (10%)
  starting transfers between devices  17.5 us (5%)
  between operations  14.7 us (4%)
  blocking collectives  10.4 us (3%)
    reduce_scatter x1, waiting for transfers between devices, summed_rows_2(): return lax.psum_scatter(tiles, chips, scatter_dimension=0, tiled=True)[0]  56 us
    scatter x1, local copies, waits for them, and re-layouts, body(): rows_buffer = jnp.zeros((devices, capacity, 2 * BLOCK), jnp.bfloat16).at[...  37.6 us
    scatter x1, local copies, waits for them, and re-layouts, body(): jnp.full((devices, capacity), STENCILS, jnp.int32).at[target, slot_index]  36.6 us
    all_gather x1, waiting for transfers between devices, body(): columns = lax.all_gather(refs, IMG, axis=1, tiled=True)  23.9 us
    convert_element_type x1, other arithmetic, translated(): return (stacked * noise_weight[None, :]).astype(jnp.bfloat16)  23.5 us
    reduce_scatter x1, waiting for transfers between devices, summed_rows_2(): tiles = lax.psum_scatter(tiles, core, scatter_dimension=0, tiled=True)  21.3 us
    all_to_all x2, starting transfers between devices, joined_exchange(): tiles = lax.all_to_all(tiles, axis, split_axis=0, concat_axis=0, tiled=True)  17.4 us
    dot_general x1, matrix products, body(): lax.dot_general(weighted, columns, (((1,), (1,)), ((), ())), preferred_el...  17.2 us
  transfers between devices with their start and end apart: 5, of which 4 were waited for; matrix products, arithmetic and copies ran while one was open for 37% of the time, Pallas kernels for 0%

commit v1 on v0

v1 whole, which is shorter than its diff:
```python
import jax
import jax.numpy as jnp
from jax import lax
from jax.experimental import pallas as pl
from jax.experimental.pallas import tpu as pltpu
from jax.sharding import Mesh
from jax.sharding import PartitionSpec as P

PIX = 4096
TRANS = 8
BLOCK = 128
STENCILS = 8
NBLK = 32
BRICKS = 128
CELLS = 512
SLICE = 512
IMG = ("xh", "y", "c")
POSE = ("z", "xl")
IMG_POSE = ("xh", "y", "c", "z", "xl")
POSE_IMG = ("z", "xl", "xh", "y", "c")
F32 = jnp.float32
BF16 = jnp.bfloat16


def weight_kernel(img, cos, sin, out):
    x = img[...].astype(F32)
    n = x.shape[0]
    parts = []
    for b in range(x.shape[1] // 256):
        parts.append(x[:, b * 256 + 128 : b * 256 + 256])
        parts.append(x[:, b * 256 : b * 256 + 128])
    swapped = jnp.concatenate(parts, axis=1)
    for t in range(TRANS):
        w = x * cos[t : t + 1, :] + swapped * sin[t : t + 1, :]
        out[t * n : (t + 1) * n, :] = w.astype(BF16)


def weight_rows(images, cos, sin):
    n, width = images.shape
    step = 512
    return pl.pallas_call(
        weight_kernel,
        grid=(width // step,),
        in_specs=[
            pl.BlockSpec((n, step), lambda i: (0, i)),
            pl.BlockSpec((TRANS, step), lambda i: (0, i)),
            pl.BlockSpec((TRANS, step), lambda i: (0, i)),
        ],
        out_specs=pl.BlockSpec((n * TRANS, step), lambda i: (0, i)),
        out_shape=jax.ShapeDtypeStruct((n * TRANS, width), BF16),
        name="weigh",
    )(images, cos, sin)


def scores_call(chunks, index, weighted, noise, carried, last):
    count = len(chunks)
    arrays = [c[0] for c in chunks]
    offsets = [c[1] for c in chunks]
    rows = weighted.shape[0]
    imgs = rows // TRANS
    poses = 384

    def kernel(idx, *refs):
        del idx
        parts = refs[:count]
        w, nz = refs[count : count + 2]
        rest = refs[count + 2 :]
        if carried is not None:
            s_in, p_in = rest[:2]
            rest = rest[2:]
        if last:
            e_out, st_out, s_acc, p_acc = rest
        else:
            s_acc, p_acc = rest
        step = pl.program_id(0)

        @pl.when(step == 0)
        def _():
            if carried is None:
                s_acc[...] = jnp.zeros(s_acc.shape, F32)
                p_acc[...] = jnp.zeros(p_acc.shape, F32)
            else:
                s_acc[...] = s_in[...]
                p_acc[...] = p_in[...]

        for j in range(count):

            @pl.when(step == j)
            def _(j=j):
                a = parts[j][...]
                lo, n = offsets[j], a.shape[0]
                s_acc[lo : lo + n, :] += lax.dot_general(
                    a, w[...], (((1,), (1,)), ((), ())), preferred_element_type=F32
                )
                wide = a.astype(F32)
                q = wide * wide * nz[...]
                p_acc[lo : lo + n, :] += (
                    q[:, :128] + q[:, 128:256] + (q[:, 256:384] + q[:, 384:])
                )

        if last:

            @pl.when(step == count - 1)
            def _():
                half = 0.5 * jnp.sum(p_acc[...], axis=1, keepdims=True)
                s_acc[...] = s_acc[...] - half
                m = jnp.max(s_acc[...], axis=0, keepdims=True)
                top = m[:, :imgs]
                for t in range(1, TRANS):
                    top = jnp.maximum(top, m[:, t * imgs : (t + 1) * imgs])
                total = jnp.zeros((1, imgs), F32)
                for t in range(TRANS):
                    e = jnp.exp(s_acc[:, t * imgs : (t + 1) * imgs] - top)
                    e_out[:, t * imgs : (t + 1) * imgs] = e
                    total = total + jnp.sum(e, axis=0, keepdims=True)
                st_out[0:1, :] = top
                st_out[1:2, :] = total

    def whole(shape):
        return pl.BlockSpec(shape, lambda i, idx: (0,) * len(shape))

    in_specs = [whole(a.shape) for a in arrays]
    in_specs += [
        pl.BlockSpec((rows, SLICE), lambda i, idx: (0, idx[i])),
        pl.BlockSpec((1, SLICE), lambda i, idx: (0, idx[i])),
    ]
    args = [*arrays, weighted, noise]
    acc_shapes = ((poses, rows), (poses, 128))
    if carried is not None:
        in_specs += [whole(s) for s in acc_shapes]
        args += list(carried)
    if last:
        out_shapes = ((poses, rows), (2, imgs))
        scratch = [pltpu.VMEM(s, F32) for s in acc_shapes]
    else:
        out_shapes = acc_shapes
        scratch = []
    return pl.pallas_call(
        kernel,
        grid_spec=pltpu.PrefetchScalarGridSpec(
            num_scalar_prefetch=1,
            grid=(count,),
            in_specs=in_specs,
            out_specs=[whole(s) for s in out_shapes],
            scratch_shapes=scratch,
        ),
        out_shape=[jax.ShapeDtypeStruct(s, F32) for s in out_shapes],
        name="scores",
    )(index, *args)


def gather_kernel(pieces, own, e, w, seg, g_out, ev_out, post, acc):
    step = pl.program_id(0)

    @pl.when(step == 0)
    def _():
        imgs = own.shape[1]
        peak = pieces[0, 0:1, :]
        for j in range(1, pieces.shape[0]):
            peak = jnp.maximum(peak, pieces[j, 0:1, :])
        total = jnp.zeros_like(peak)
        for j in range(pieces.shape[0]):
            total = total + pieces[j, 1:2, :] * jnp.exp(pieces[j, 0:1, :] - peak)
        ev_out[...] = peak + jnp.log(total)
        scale = jnp.exp(own[0:1, :] - peak) / total
        for t in range(TRANS):
            at = slice(t * imgs, (t + 1) * imgs)
            post[:, at] = (e[:, at] * scale).astype(BF16)
        acc[...] = jnp.zeros(acc.shape, F32)

    rows = jnp.dot(post[...], w[...], preferred_element_type=F32).astype(BF16)
    both = jnp.concatenate([rows[:, :256], rows[:, 256:]], axis=0)
    ids = seg[0]
    hot = lax.broadcasted_iota(jnp.int32, (acc.shape[0], ids.shape[1]), 0) == ids
    hot = jnp.where(hot, 1.0, 0.0).astype(BF16)
    acc[...] += jnp.dot(hot, both, preferred_element_type=F32)

    @pl.when(step == pl.num_programs(0) - 1)
    def _():
        g_out[...] = acc[...].astype(BF16)


def gather_call(pieces, own, e, weighted, seg):
    rows = weighted.shape[0]
    imgs = own.shape[1]
    segs = BRICKS * STENCILS
    return pl.pallas_call(
        gather_kernel,
        grid=(NBLK // 2,),
        in_specs=[
            pl.BlockSpec(pieces.shape, lambda i: (0, 0, 0)),
            pl.BlockSpec(own.shape, lambda i: (0, 0)),
            pl.BlockSpec(e.shape, lambda i: (0, 0)),
            pl.BlockSpec((rows, 512), lambda i: (0, i)),
            pl.BlockSpec((1, 1, seg.shape[2]), lambda i: (i, 0, 0)),
        ],
        out_specs=[
            pl.BlockSpec((segs, 256), lambda i: (0, 0)),
            pl.BlockSpec((1, imgs), lambda i: (0, 0)),
        ],
        out_shape=[
            jax.ShapeDtypeStruct((segs, 256), BF16),
            jax.ShapeDtypeStruct((1, imgs), F32),
        ],
        scratch_shapes=[pltpu.VMEM(e.shape, BF16), pltpu.VMEM((segs, 256), F32)],
        name="gather",
    )(pieces, own, e, weighted, seg)


def volume_kernel(got, interp, count, out):
    total = got[0].astype(F32)
    for j in range(1, got.shape[0]):
        total = total + got[j].astype(F32)
    mixed = total.astype(BF16)
    acc = jnp.zeros((STENCILS, CELLS), F32)
    for s in range(STENCILS):
        row = lax.broadcasted_iota(jnp.int32, mixed.shape, 0) == s
        only = jnp.where(row, total, 0.0).astype(BF16)
        acc = acc + jnp.dot(only, interp[0, s], preferred_element_type=F32)
    del mixed
    out[...] = jnp.sum(acc, axis=0, keepdims=True) * lax.rsqrt(1.0 + count[...])


def volume_call(got, interp, count):
    return pl.pallas_call(
        volume_kernel,
        out_shape=jax.ShapeDtypeStruct((1, CELLS), F32),
        name="volume",
    )(got, interp, count)


def shifted(x, axis, by):
    size = lax.axis_size(axis)
    return lax.ppermute(x, axis, [(i, (i + by) % size) for i in range(size)])


def flipped(x, axis, bit=1):
    size = lax.axis_size(axis)
    return lax.ppermute(x, axis, [(i, i ^ bit) for i in range(size)])


def doubled(x, axis, bit=1):
    other = flipped(x, axis, bit)
    upper = (lax.axis_index(axis) & bit) != 0
    return jnp.where(
        upper, jnp.concatenate([other, x], 0), jnp.concatenate([x, other], 0)
    )


def body(images, shift_phase, noise_weight, refs, routing, stencil, interp):
    xh, y, c = (lax.axis_index(a) for a in IMG)

    def at(fx, dy, fc):
        return (((xh ^ fx) * 4 + (y + dy) % 4) * 2 + (c ^ fc)).astype(jnp.int32)

    near = flipped(refs, "c")
    left = shifted(refs, "y", 1)
    right = shifted(refs, "y", -1)
    across = flipped(refs, "xh")
    low = slice(0, 192)
    high = slice(192, 384)
    far_low = shifted(left[low], "y", 1)
    far_high = shifted(right[high], "y", -1)
    aleft = shifted(across, "y", 1)
    aright = shifted(across, "y", -1)
    afar_low = shifted(aleft[low], "y", 1)
    afar_high = shifted(aright[high], "y", -1)
    place = [
        (refs, 0, (0, 0)),
        (left, 0, (0, -1)),
        (right, 0, (0, 1)),
        (across, 0, (1, 0)),
        (far_low, 0, (0, 2)),
        (far_high, 192, (0, 2)),
        (aleft, 0, (1, -1)),
        (aright, 0, (1, 1)),
        (afar_low, 0, (1, 2)),
        (afar_high, 192, (1, 2)),
    ]

    ids = (routing[:, 0] * STENCILS + stencil).reshape(1, 6, 128)
    ids = doubled(ids, "c")
    ids = doubled(ids, "xh")
    ids = doubled(ids, "y", 1)
    ids = doubled(ids, "y", 2)
    ids = ids.reshape(2, 2, 2, 2, 24, NBLK).transpose(2, 0, 1, 3, 4, 5).reshape(384, NBLK)
    counts = jnp.sum(
        (ids.reshape(1, -1) // STENCILS == jnp.arange(BRICKS, dtype=jnp.int32)[:, None]).astype(F32),
        axis=1,
    )
    seg = ids.T.reshape(NBLK // 2, 1, 768)

    noise = noise_weight.reshape(1, -1)
    by_block = noise_weight.reshape(1, NBLK, 2, BLOCK)
    angles = shift_phase.reshape(TRANS, NBLK, 1, BLOCK)
    cos = (jnp.cos(angles) * by_block).reshape(TRANS, 2 * PIX)
    sign = jnp.array([1.0, -1.0], F32).reshape(1, 1, 2, 1)
    sin = (jnp.sin(angles) * by_block * sign).reshape(TRANS, 2 * PIX)
    weighted = weight_rows(images, cos, sin)

    def group(picks):
        chunks = [(a, lo) for a, lo, _, _ in picks]
        index = jnp.stack([at(f[0], f[1], core) for _, _, f, core in picks])
        return chunks, index

    def mine(js):
        return [(*place[j], 0) for j in js]

    def theirs(js):
        return [(flipped(place[j][0], "c"), *place[j][1:], 1) for j in js]

    first = mine([0]) + [(near, 0, (0, 0), 1)]
    second = mine([1, 2, 3])
    third = theirs([1, 2, 3])
    fourth = mine([4, 5, 6, 7])
    fifth = theirs([4, 5, 6, 7]) + mine([8, 9]) + theirs([8, 9])
    carried = None
    turns = [first, second, third, fourth, fifth]
    for j, picks in enumerate(turns):
        chunks, index = group(picks)
        carried = scores_call(chunks, index, weighted, noise, carried, j == len(turns) - 1)
    e, own = carried

    sent = jnp.concatenate([own, counts.reshape(1, BRICKS)], axis=0)
    pieces = lax.all_to_all(
        jnp.broadcast_to(sent[None], (8, *sent.shape)), POSE, 0, 0, tiled=True
    )
    gathered, evidence = gather_call(pieces, own, e, weighted, seg)
    got = lax.all_to_all(
        gathered.reshape(BRICKS, STENCILS, 2 * BLOCK), IMG_POSE, 0, 0, tiled=True
    )
    brick = lax.axis_index(IMG_POSE)
    count = lax.dynamic_slice(jnp.sum(pieces[:, 2, :], axis=0), (brick,), (1,))
    volume = volume_call(got, interp, count.reshape(1, 1))
    return (volume, evidence.reshape(-1))


def solution(mesh):
    finer = Mesh(mesh.devices.reshape(2, 4, 2, 4, 2), ("xh", "y", "c", "z", "xl"))
    return jax.shard_map(
        body,
        mesh=finer,
        in_specs=(
            P(IMG, None),
            P(),
            P(),
            P(POSE, IMG),
            P(POSE_IMG, None),
            P(POSE_IMG),
            P(IMG_POSE, None, None, None),
        ),
        out_specs=(P(IMG_POSE, None), P(IMG)),
        check_vma=False,
    )
```

time: 345 us -> 163 us (0.47)
  local copies, waits for them, and re-layouts: 106 us -> 10.5 us
  waiting for transfers between devices: 119 us -> 30.2 us
  Pallas kernels: 0 us -> 74.9 us
  matrix products: 33.8 us -> 0 us
  other arithmetic: 42.8 us -> 9.21 us
  starting transfers between devices: 17.5 us -> 35.3 us
  between operations: 14.7 us -> 0.95 us
  blocking collectives: 10.4 us -> 0 us
    reduce_scatter x2 -> x0, waiting for transfers between devices: 77.3 us -> none  [the longest x1 56 us: summed_rows_2(): return lax.psum_scatter(tiles, chips, scatter_dimension=0, tiled=True)[0]]
    pallas_call x0 -> x8, Pallas kernels: none -> 74.9 us  [the longest x5 36.2 us: scores_call(): pl.pallas_call(kernel, grid_spec=pltpu.PrefetchScalarGridSpec(num_scalar_...]
    scatter x2 -> x0, local copies, waits for them, and re-layouts: 74.2 us -> none  [the longest x1 37.6 us: body(): rows_buffer = jnp.zeros((devices, capacity, 2 * BLOCK), jnp.bfloat16).at[...]
    dot_general x4 -> x0, matrix products: 33.8 us -> none  [the longest x1 17.2 us: body(): lax.dot_general(weighted, columns, (((1,), (1,)), ((), ())), preferred_el...]
    convert_element_type x2 -> x0, other arithmetic: 24.7 us -> none  [the longest x1 23.5 us: translated(): return (stacked * noise_weight[None, :]).astype(jnp.bfloat16)]
    all_gather x1 -> x0, waiting for transfers between devices: 23.9 us -> none  [body(): columns = lax.all_gather(refs, IMG, axis=1, tiled=True)]
    ppermute x0 -> x23, starting transfers between devices: none -> 21.8 us  [the longest x8 12.8 us: shifted(): return lax.ppermute(x, axis, [(i, (i + by) % size) for i in range(size)])]
    ppermute x0 -> x23, waiting for transfers between devices: none -> 13.1 us  [the longest x15 10.6 us: flipped(): return lax.ppermute(x, axis, [(i, i ^ bit) for i in range(size)])]
  transfers between devices with their start and end apart: 5 -> 25, of which waited for: 4 -> 6; matrix products, arithmetic and copies ran while one was open for 37% -> 9% of each run, Pallas kernels for 0% -> 24%
where the time goes in v1:
time: 163 us; the launch traced here: 161 us
  Pallas kernels  74.9 us (46%)
  starting transfers between devices  35.3 us (22%)
  waiting for transfers between devices  30.2 us (19%)
  local copies, waits for them, and re-layouts  10.5 us (6%)
  other arithmetic  9.21 us (6%)
    pallas_call x5, Pallas kernels, scores_call(): pl.pallas_call(kernel, grid_spec=pltpu.PrefetchScalarGridSpec(num_scalar_...  36.2 us
    pallas_call x1, Pallas kernels, gather_call(): pl.pallas_call(gather_kernel, grid=(NBLK // 2,), in_specs=[pl.BlockSpec(p...  21.8 us
    pallas_call x1, Pallas kernels, weight_rows(): pl.pallas_call(weight_kernel, grid=(width // step,), in_specs=[pl.BlockSp...  13.4 us
    ppermute x8, starting transfers between devices, shifted(): return lax.ppermute(x, axis, [(i, (i + by) % size) for i in range(size)])  12.8 us
    all_to_all x1, waiting for transfers between devices, body(): lax.all_to_all(gathered.reshape(BRICKS, STENCILS, 2 * BLOCK), IMG_POSE, 0...  12.2 us
    ppermute x15, waiting for transfers between devices, flipped(): return lax.ppermute(x, axis, [(i, i ^ bit) for i in range(size)])  10.6 us
    ppermute x15, starting transfers between devices, flipped(): return lax.ppermute(x, axis, [(i, i ^ bit) for i in range(size)])  9.05 us
    all_to_all x1, starting transfers between devices, body(): lax.all_to_all(gathered.reshape(BRICKS, STENCILS, 2 * BLOCK), IMG_POSE, 0...  7.28 us
  transfers between devices with their start and end apart: 25, of which 6 were waited for; matrix products, arithmetic and copies ran while one was open for 9% of the time, Pallas kernels for 24%

profile of v1, /device:TPU:0, one launch (start us, length us, event | category | flops | bytes accessed | tf_op | source)
XLA Modules:
  0.0 161.1 jit_solution(6931468574492140635)
XLA Ops:
  0.6 0.7 multiply_reduce_fusion
  1.3 0.7 add_bitcast_fusion
  2.0 3.1 %collective-permute-start.6 = (bf16[384,512]{1,0:T(8,128)(2,1)}, bf16[384,512]{1,0:T(8,128)(2,1)S(1)}, u32[]{:S(2)}, u32[]{:S(2)}) collective-permute-start(bf16[384,512]{1,0:T(8,128)(2,1)} %refs_0_.1), channel_id=1, source_target_pairs={{0,64},{64,0},{1,65},{65,1},{2,66},{66,2},{3,67},{67,3},{4,68},{68... | collective-permute-start | bytes 1179656 | tf_op jit(solution)/shard_map/ppermute | solution.py:239
  5.2 1.2 collective-permute-start.20
  6.3 1.6 collective-permute-start
  7.9 1.7 %collective-permute-start.3 = (bf16[384,512]{1,0:T(8,128)(2,1)}, bf16[384,512]{1,0:T(8,128)(2,1)S(1)}, u32[]{:S(2)}, u32[]{:S(2)}) collective-permute-start(bf16[384,512]{1,0:T(8,128)(2,1)} %refs_0_.1), channel_id=1, source_target_pairs={{0,48},{16,0},{32,16},{48,32},{1,49},{17,1},{33,17},{49,33},{2,50}... | collective-permute-start | bytes 1179656 | tf_op jit(solution)/shard_map/ppermute | solution.py:234
  9.6 5.9 %collective-permute-done.20 = s32[2,6,128]{2,1,0:T(8,128)S(1)} collective-permute-done((s32[2,6,128]{2,1,0:T(8,128)S(1)}, s32[2,6,128]{2,1,0:T(8,128)S(1)}, u32[]{:S(2)}, u32[]{:S(2)}) %collective-permute-start.20) | collective-permute-done | bytes 6176 | tf_op jit(solution)/shard_map/ppermute | solution.py:239
  15.4 1.7 %collective-permute-start.21 = (s32[4,6,128]{2,1,0:T(8,128)S(1)}, s32[4,6,128]{2,1,0:T(8,128)S(1)}, u32[]{:S(2)}, u32[]{:S(2)}) collective-permute-start(s32[4,6,128]{2,1,0:T(8,128)S(1)} %add_select_fusion.3), channel_id=1, source_target_pairs={{0,16},{16,0},{32,48},{48,32},{1,17},{17,1},{33,49},{49,33},{2,18}... | collective-permute-start | bytes 36872 | tf_op jit(solution)/shard_map/ppermute | solution.py:239
  17.1 1.4 sine_bitcast_fusion
  18.9 0.8 collective-permute-done.21
  19.7 2.6 %collective-permute-start.9 = (bf16[384,512]{1,0:T(8,128)(2,1)S(1)}, bf16[384,512]{1,0:T(8,128)(2,1)S(1)}, u32[]{:S(2)}, u32[]{:S(2)}) collective-permute-start(bf16[384,512]{1,0:T(8,128)(2,1)S(1)} %collective-permute-done.6.refs_2_), channel_id=1, source_target_pairs={{0,48},{16,0},{32,16},{48,32},{1,49},{17,1},{33,17},{49,33},{2,50}... | collective-permute-start | bytes 1179656 | tf_op jit(solution)/shard_map/ppermute | solution.py:234
  22.4 0.7 mul.137
  23.1 1.6 %multiply_multiply_fusion = (f32[8,8192]{1,0:T(8,128)}, f32[8,8192]{1,0:T(8,128)}) fusion(f32[8,8192]{1,0:T(8,128)S(1)} %bitcast.44, f32[8192]{0:T(1024)S(1)} %bitcast.47, f32[8192]{0:T(1024)} %param.10, f32[8,8192]{1,0:T(8,128)S(1)} %bitcast.43), kind=kLoop, calls=%fused_computation.2 | loop fusion | flops 196608 | bytes 1114112 | tf_op jit(solution)/shard_map/mul | solution.py:298
  24.8 1.3 collective-permute-start.22
  26.6 0.7 slice.20
  27.3 4.0 %collective-permute-done.22 = s32[8,6,128]{2,1,0:T(8,128)S(1)} collective-permute-done((s32[8,6,128]{2,1,0:T(8,128)S(1)}, s32[8,6,128]{2,1,0:T(8,128)S(1)}, u32[]{:S(2)}, u32[]{:S(2)}) %collective-permute-start.22) | collective-permute-done | bytes 24608 | tf_op jit(solution)/shard_map/ppermute | solution.py:239
  31.3 1.8 %collective-permute-start.1 = (bf16[192,512]{1,0:T(8,128)(2,1)}, bf16[192,512]{1,0:T(8,128)(2,1)}, u32[]{:S(2)}, u32[]{:S(2)}) collective-permute-start(bf16[192,512]{1,0:T(8,128)(2,1)} %slice.20), channel_id=1, source_target_pairs={{0,16},{16,32},{32,48},{48,0},{1,17},{17,33},{33,49},{49,1},{2,18}... | collective-permute-start | bytes 589832 | tf_op jit(solution)/shard_map/ppermute | solution.py:234
  33.1 1.5 collective-permute-start.4
  35.2 0.7 pad_add_fusion.2.idx
  35.8 13.4 %weigh.1.refs_2_.refs_3_.refs_4_.refs_8_.w = bf16[1024,8192]{1,0:T(8,128)(2,1)} custom-call(bf16[128,8192]{1,0:T(8,128)(2,1)} %img.1, f32[8,8192]{1,0:T(8,128)} %get-tuple-element.29.cos, f32[8,8192]{1,0:T(8,128)} %get-tuple-element.28.sin), custom_call_target="tpu_custom_call" | custom-call | tf_op jit(solution)/shard_map/weigh/pallas_call | solution.py:41
  50.4 0.7 slice.22
  51.1 0.7 slice.23
  51.9 0.6 collective-permute-start.11
  52.5 2.6 %collective-permute-start.12 = (bf16[192,512]{1,0:T(8,128)(2,1)}, bf16[192,512]{1,0:T(8,128)(2,1)}, u32[]{:S(2)}, u32[]{:S(2)}) collective-permute-start(bf16[192,512]{1,0:T(8,128)(2,1)} %slice.23), channel_id=1, source_target_pairs={{0,48},{16,0},{32,16},{48,32},{1,49},{17,1},{33,17},{49,33},{2,50}... | collective-permute-start | bytes 589832 | tf_op jit(solution)/shard_map/ppermute | solution.py:234
  55.2 0.6 pad_add_fusion.idx
  55.8 0.8 add_select_fusion.1
  56.8 0.7 reshape_reshape.3
  58.2 2.4 %collective-permute-done.11.refs_4_ = bf16[192,512]{1,0:T(8,128)(2,1)S(1)} collective-permute-done((bf16[192,512]{1,0:T(8,128)(2,1)}, bf16[192,512]{1,0:T(8,128)(2,1)S(1)}, u32[]{:S(2)}, u32[]{:S(2)}) %collective-permute-start.11) | collective-permute-done | bytes 196640 | tf_op jit(solution)/shard_map/ppermute | solution.py:234
  61.1 0.8 add_select_fusion
  61.9 0.7 convert_reduce_fusion
  62.6 4.7 %scores.5 = (f32[384,1024]{1,0:T(8,128)}, f32[384,128]{1,0:T(8,128)}) custom-call(s32[2]{0:T(128)} %pad_add_fusion.3.idx, bf16[384,512]{1,0:T(8,128)(2,1)} %refs_0_.1, bf16[384,512]{1,0:T(8,128)(2,1)} %copy-done.6, bf16[1024,8192]{1,0:T(8,128)(2,1)} %weigh.1.refs_2_.refs_3_.refs_4_.refs_8_.w, f32[1,8192]{1,0:T(1,128)} %bitcast.38), custom_call_target="tpu_custom_call" | custom-call | tf_op jit(solution)/shard_map/scores/pallas_call | solution.py:138
  67.3 6.5 %scores.6 = (f32[384,1024]{1,0:T(8,128)}, f32[384,128]{1,0:T(8,128)}) custom-call(s32[3]{0:T(128)} %pad_add_fusion.2.idx, bf16[384,512]{1,0:T(8,128)(2,1)} %copy-done.2, bf16[384,512]{1,0:T(8,128)(2,1)} %copy-done.3, bf16[384,512]{1,0:T(8,128)(2,1)} %copy-done.5, bf16[1024,8192]{1,0:T(8,128)(2,1)} %weigh.1.refs_2_.refs_3_.refs_4_.refs_8_.w, ...), custom_call_target="tpu_custom_call" | custom-call | tf_op jit(solution)/shard_map/scores/pallas_call | solution.py:138
  73.8 6.5 %scores.7 = (f32[384,1024]{1,0:T(8,128)}, f32[384,128]{1,0:T(8,128)}) custom-call(s32[3]{0:T(128)} %pad_add_fusion.1.idx, bf16[384,512]{1,0:T(8,128)(2,1)} %copy-done.8, bf16[384,512]{1,0:T(8,128)(2,1)} %collective-permute-done.16.refs_1_, bf16[384,512]{1,0:T(8,128)(2,1)} %copy-done.7, bf16[1024,8192]{1,0:T(8,128)(2,1)} %weigh.1.refs_2_.refs_3_.refs_4_.refs_8_.w, ...), custom_call_target="tpu_custom_call" | custom-call | tf_op jit(solution)/shard_map/scores/pallas_call | solution.py:138
  80.4 7.2 %scores.8 = (f32[384,1024]{1,0:T(8,128)}, f32[384,128]{1,0:T(8,128)}) custom-call(s32[4]{0:T(128)} %pad_add_fusion.idx, bf16[192,512]{1,0:T(8,128)(2,1)} %collective-permute-done.1.refs_0_, bf16[192,512]{1,0:T(8,128)(2,1)} %copy-done.11, bf16[384,512]{1,0:T(8,128)(2,1)} %copy-done.1, bf16[384,512]{1,0:T(8,128)(2,1)} %copy-done.4, ...), custom_call_target="tpu_custom_call" | custom-call | tf_op jit(solution)/shard_map/scores/pallas_call | solution.py:138
  87.7 0.6 copy-done.14
  88.6 11.3 %scores.9 = (f32[384,1024]{1,0:T(8,128)}, f32[2,128]{1,0:T(2,128)}) custom-call(s32[8]{0:T(128)} %stack.72.idx, bf16[192,512]{1,0:T(8,128)(2,1)} %copy-done.12, bf16[192,512]{1,0:T(8,128)(2,1)} %copy-done.14, bf16[384,512]{1,0:T(8,128)(2,1)} %copy-done.10, bf16[384,512]{1,0:T(8,128)(2,1)} %copy-done.9, bf16[192,512]{1,0:T(8,128)(2,1)} %copy-done.13, ...), custom_call_target="tpu_custom_call" | custom-call | tf_op jit(solution)/shard_map/scores/pallas_call | solution.py:138
  99.9 0.7 pad_maximum_fusion
  100.6 0.6 broadcast_in_dim.2
  101.2 6.2 %all-to-all-start = ((f32[8,3,128]{2,1,0:T(4,128)}), f32[8,3,128]{2,1,0:T(4,128)S(1)}, u32[]{:S(2)}, u32[]{:S(2)}) async-start(f32[8,3,128]{2,1,0:T(4,128)} %broadcast_in_dim.2), calls=%async_computation | async-start | bytes 32768 | tf_op jit(solution)/shard_map/all_to_all | solution.py:325
  108.1 0.7 reshape.129.seg
  108.7 5.0 %all-to-all-done.pieces = f32[8,3,128]{2,1,0:T(4,128)S(1)} async-done(((f32[8,3,128]{2,1,0:T(4,128)}), f32[8,3,128]{2,1,0:T(4,128)S(1)}, u32[]{:S(2)}, u32[]{:S(2)}) %all-to-all-start) | async-done | bytes 12320 | tf_op jit(solution)/shard_map/all_to_all | solution.py:325
  113.7 0.6 copy-done.17
  114.3 21.8 %gather.1 = (bf16[1024,256]{1,0:T(8,128)(2,1)}, f32[1,128]{1,0:T(1,128)}) custom-call(f32[8,3,128]{2,1,0:T(4,128)} %copy-done.17, f32[2,128]{1,0:T(2,128)} %get-tuple-element.22.own, f32[384,1024]{1,0:T(8,128)} %get-tuple-element.23.e, bf16[1024,8192]{1,0:T(8,128)(2,1)} %weigh.1.refs_2_.refs_3_.refs_4_.refs_8_.w, s32[16,1,768]{2,1,0:T(1,128)} %reshape.129.seg), custom_call_target="tpu_custom_call" | custom-call | tf_op jit(solution)/shard_map/gather/pallas_call | solution.py:187
  136.1 7.3 %all-to-all-start.1 = ((bf16[128,8,256]{2,1,0:T(8,128)(2,1)}), bf16[128,8,256]{2,1,0:T(8,128)(2,1)S(1)}, u32[]{:S(2)}, u32[]{:S(2)}) async-start(bf16[128,8,256]{2,1,0:T(8,128)(2,1)} %bitcast.45), calls=%async_computation.1 | async-start | bytes 1048576 | tf_op jit(solution)/shard_map/all_to_all | solution.py:329
  143.4 0.7 slice_reduce_fusion
  144.7 12.2 %all-to-all-done.1.got = bf16[128,8,256]{2,1,0:T(8,128)(2,1)S(1)} async-done(((bf16[128,8,256]{2,1,0:T(8,128)(2,1)}), bf16[128,8,256]{2,1,0:T(8,128)(2,1)S(1)}, u32[]{:S(2)}, u32[]{:S(2)}) %all-to-all-start.1) | async-done | bytes 524320 | tf_op jit(solution)/shard_map/all_to_all | solution.py:329
  156.9 0.8 copy-done
  157.7 3.4 %volume.1 = f32[1,512]{1,0:T(1,128)} custom-call(bf16[128,8,256]{2,1,0:T(8,128)(2,1)} %copy-done, bf16[1,8,256,512]{3,2,1,0:T(8,128)(2,1)} %interp.1, f32[1,1]{1,0:T(1,128)} %bitcast.27.count), custom_call_target="tpu_custom_call" | custom-call | tf_op jit(solution)/shard_map/volume/pallas_call | solution.py:225
  (80 shorter events, 5.7 us)
Async XLA Ops:
  2.0 3.1 %collective-permute-start.19 = (s32[1,6,128]{2,1,0:T(8,128)S(1)}, s32[1,6,128]{2,1,0:T(8,128)S(1)}, u32[]{:S(2)}, u32[]{:S(2)}) collective-permute-start(s32[1,6,128]{2,1,0:T(8,128)S(1)} %add_bitcast_fusion), channel_id=1, source_target_pairs={{0,8},{8,0},{1,9},{9,1},{2,10},{10,2},{3,11},{11,3},{4,12},{12,4},... | collective-permute-start | bytes 9224 | tf_op jit(solution)/shard_map/ppermute | solution.py:239
  2.0 16.5 %collective-permute-start.6 = (bf16[384,512]{1,0:T(8,128)(2,1)}, bf16[384,512]{1,0:T(8,128)(2,1)S(1)}, u32[]{:S(2)}, u32[]{:S(2)}) collective-permute-start(bf16[384,512]{1,0:T(8,128)(2,1)} %refs_0_.1), channel_id=1, source_target_pairs={{0,64},{64,0},{1,65},{65,1},{2,66},{66,2},{3,67},{67,3},{4,68},{68... | collective-permute-start | bytes 1179656 | tf_op jit(solution)/shard_map/ppermute | solution.py:239
  5.2 10.3 %collective-permute-start.20 = (s32[2,6,128]{2,1,0:T(8,128)S(1)}, s32[2,6,128]{2,1,0:T(8,128)S(1)}, u32[]{:S(2)}, u32[]{:S(2)}) collective-permute-start(s32[2,6,128]{2,1,0:T(8,128)S(1)} %add_select_fusion.4), channel_id=1, source_target_pairs={{0,64},{64,0},{1,65},{65,1},{2,66},{66,2},{3,67},{67,3},{4,68},{68... | collective-permute-start | bytes 18440 | tf_op jit(solution)/shard_map/ppermute | solution.py:239
  6.3 26.8 %collective-permute-start.18 = (bf16[384,512]{1,0:T(8,128)(2,1)}, bf16[384,512]{1,0:T(8,128)(2,1)S(1)}, u32[]{:S(2)}, u32[]{:S(2)}) collective-permute-start(bf16[384,512]{1,0:T(8,128)(2,1)} %refs_0_.1), channel_id=1, source_target_pairs={{0,8},{8,0},{1,9},{9,1},{2,10},{10,2},{3,11},{11,3},{4,12},{12,4},... | collective-permute-start | bytes 1179656 | tf_op jit(solution)/shard_map/ppermute | solution.py:239
  6.3 18.4 %collective-permute-start = (bf16[384,512]{1,0:T(8,128)(2,1)}, bf16[384,512]{1,0:T(8,128)(2,1)S(1)}, u32[]{:S(2)}, u32[]{:S(2)}) collective-permute-start(bf16[384,512]{1,0:T(8,128)(2,1)} %refs_0_.1), channel_id=1, source_target_pairs={{0,16},{16,32},{32,48},{48,0},{1,17},{17,33},{33,49},{49,1},{2,18}... | collective-permute-start | bytes 1179656 | tf_op jit(solution)/shard_map/ppermute | solution.py:234
  7.9 16.9 %collective-permute-start.3 = (bf16[384,512]{1,0:T(8,128)(2,1)}, bf16[384,512]{1,0:T(8,128)(2,1)S(1)}, u32[]{:S(2)}, u32[]{:S(2)}) collective-permute-start(bf16[384,512]{1,0:T(8,128)(2,1)} %refs_0_.1), channel_id=1, source_target_pairs={{0,48},{16,0},{32,16},{48,32},{1,49},{17,1},{33,17},{49,33},{2,50}... | collective-permute-start | bytes 1179656 | tf_op jit(solution)/shard_map/ppermute | solution.py:234
  15.4 4.3 %collective-permute-start.21 = (s32[4,6,128]{2,1,0:T(8,128)S(1)}, s32[4,6,128]{2,1,0:T(8,128)S(1)}, u32[]{:S(2)}, u32[]{:S(2)}) collective-permute-start(s32[4,6,128]{2,1,0:T(8,128)S(1)} %add_select_fusion.3), channel_id=1, source_target_pairs={{0,16},{16,0},{32,48},{48,32},{1,17},{17,1},{33,49},{49,33},{2,18}... | collective-permute-start | bytes 36872 | tf_op jit(solution)/shard_map/ppermute | solution.py:239
  18.5 30.7 %copy-start.5 = (bf16[384,512]{1,0:T(8,128)(2,1)}, bf16[384,512]{1,0:T(8,128)(2,1)S(1)}, u32[]{:S(2)}) copy-start(bf16[384,512]{1,0:T(8,128)(2,1)S(1)} %collective-permute-done.6.refs_2_) | copy-start | bytes 1179652
  18.5 16.1 %collective-permute-start.7 = (bf16[384,512]{1,0:T(8,128)(2,1)S(1)}, bf16[384,512]{1,0:T(8,128)(2,1)S(1)}, u32[]{:S(2)}, u32[]{:S(2)}) collective-permute-start(bf16[384,512]{1,0:T(8,128)(2,1)S(1)} %collective-permute-done.6.refs_2_), channel_id=1, source_target_pairs={{0,16},{16,32},{32,48},{48,0},{1,17},{17,33},{33,49},{49,1},{2,18}... | collective-permute-start | bytes 1179656 | tf_op jit(solution)/shard_map/ppermute | solution.py:234
  19.7 14.9 %collective-permute-start.9 = (bf16[384,512]{1,0:T(8,128)(2,1)S(1)}, bf16[384,512]{1,0:T(8,128)(2,1)S(1)}, u32[]{:S(2)}, u32[]{:S(2)}) collective-permute-start(bf16[384,512]{1,0:T(8,128)(2,1)S(1)} %collective-permute-done.6.refs_2_), channel_id=1, source_target_pairs={{0,48},{16,0},{32,16},{48,32},{1,49},{17,1},{33,17},{49,33},{2,50}... | collective-permute-start | bytes 1179656 | tf_op jit(solution)/shard_map/ppermute | solution.py:234
  24.7 24.5 %copy-start.2 = (bf16[384,512]{1,0:T(8,128)(2,1)}, bf16[384,512]{1,0:T(8,128)(2,1)S(1)}, u32[]{:S(2)}) copy-start(bf16[384,512]{1,0:T(8,128)(2,1)S(1)} %collective-permute-done.refs_0_) | copy-start | bytes 1179652
  24.7 27.8 %collective-permute-start.17 = (bf16[384,512]{1,0:T(8,128)(2,1)S(1)}, bf16[384,512]{1,0:T(8,128)(2,1)S(1)}, u32[]{:S(2)}, u32[]{:S(2)}) collective-permute-start(bf16[384,512]{1,0:T(8,128)(2,1)S(1)} %collective-permute-done.6.refs_2_), channel_id=1, source_target_pairs={{0,8},{8,0},{1,9},{9,1},{2,10},{10,2},{3,11},{11,3},{4,12},{12,4},... | collective-permute-start | bytes 1179656 | tf_op jit(solution)/shard_map/ppermute | solution.py:239
  24.8 8.4 %copy-start.16 = (s32[8,6,128]{2,1,0:T(8,128)}, s32[8,6,128]{2,1,0:T(8,128)S(1)}, u32[]{:S(2)}) copy-start(s32[8,6,128]{2,1,0:T(8,128)S(1)} %add_select_fusion.2) | copy-start | bytes 73732
  24.8 24.5 %copy-start.3 = (bf16[384,512]{1,0:T(8,128)(2,1)}, bf16[384,512]{1,0:T(8,128)(2,1)S(1)}, u32[]{:S(2)}) copy-start(bf16[384,512]{1,0:T(8,128)(2,1)S(1)} %collective-permute-done.3.refs_1_) | copy-start | bytes 1179652
  24.8 6.5 %collective-permute-start.22 = (s32[8,6,128]{2,1,0:T(8,128)S(1)}, s32[8,6,128]{2,1,0:T(8,128)S(1)}, u32[]{:S(2)}, u32[]{:S(2)}) collective-permute-start(s32[8,6,128]{2,1,0:T(8,128)S(1)} %add_select_fusion.2), channel_id=1, source_target_pairs={{0,32},{16,48},{32,0},{48,16},{1,33},{17,49},{33,1},{49,17},{2,34}... | collective-permute-start | bytes 73736 | tf_op jit(solution)/shard_map/ppermute | solution.py:239
  31.3 1.8 %copy-start.18 = (s32[8,6,128]{2,1,0:T(8,128)}, s32[8,6,128]{2,1,0:T(8,128)S(1)}, u32[]{:S(2)}) copy-start(s32[8,6,128]{2,1,0:T(8,128)S(1)} %collective-permute-done.22) | copy-start | bytes 73732
  31.3 20.5 %collective-permute-start.1 = (bf16[192,512]{1,0:T(8,128)(2,1)}, bf16[192,512]{1,0:T(8,128)(2,1)}, u32[]{:S(2)}, u32[]{:S(2)}) collective-permute-start(bf16[192,512]{1,0:T(8,128)(2,1)} %slice.20), channel_id=1, source_target_pairs={{0,16},{16,32},{32,48},{48,0},{1,17},{17,33},{33,49},{49,1},{2,18}... | collective-permute-start | bytes 589832 | tf_op jit(solution)/shard_map/ppermute | solution.py:234
  33.1 16.1 %copy-start.6 = (bf16[384,512]{1,0:T(8,128)(2,1)}, bf16[384,512]{1,0:T(8,128)(2,1)S(1)}, u32[]{:S(2)}) copy-start(bf16[384,512]{1,0:T(8,128)(2,1)S(1)} %collective-permute-done.18.refs_1_) | copy-start | bytes 1179652
  33.1 18.8 %collective-permute-start.4 = (bf16[192,512]{1,0:T(8,128)(2,1)S(1)}, bf16[192,512]{1,0:T(8,128)(2,1)S(1)}, u32[]{:S(2)}, u32[]{:S(2)}) collective-permute-start(bf16[192,512]{1,0:T(8,128)(2,1)S(1)} %slice.21), channel_id=1, source_target_pairs={{0,48},{16,0},{32,16},{48,32},{1,49},{17,1},{33,17},{49,33},{2,50}... | collective-permute-start | bytes 589832 | tf_op jit(solution)/shard_map/ppermute | solution.py:234
  34.6 23.4 %copy-start.1 = (bf16[384,512]{1,0:T(8,128)(2,1)}, bf16[384,512]{1,0:T(8,128)(2,1)S(1)}, u32[]{:S(2)}) copy-start(bf16[384,512]{1,0:T(8,128)(2,1)S(1)} %collective-permute-done.7.refs_2_) | copy-start | bytes 1179652
  34.6 22.8 %collective-permute-start.15 = (bf16[384,512]{1,0:T(8,128)(2,1)S(1)}, bf16[384,512]{1,0:T(8,128)(2,1)S(1)}, u32[]{:S(2)}, u32[]{:S(2)}) collective-permute-start(bf16[384,512]{1,0:T(8,128)(2,1)S(1)} %collective-permute-done.refs_0_), channel_id=1, source_target_pairs={{0,8},{8,0},{1,9},{9,1},{2,10},{10,2},{3,11},{11,3},{4,12},{12,4},... | collective-permute-start | bytes 1179656 | tf_op jit(solution)/shard_map/ppermute | solution.py:239
  34.7 22.8 %copy-start.4 = (bf16[384,512]{1,0:T(8,128)(2,1)}, bf16[384,512]{1,0:T(8,128)(2,1)S(1)}, u32[]{:S(2)}) copy-start(bf16[384,512]{1,0:T(8,128)(2,1)S(1)} %collective-permute-done.9.refs_3_) | copy-start | bytes 1179652
  34.7 22.8 %collective-permute-start.16 = (bf16[384,512]{1,0:T(8,128)(2,1)S(1)}, bf16[384,512]{1,0:T(8,128)(2,1)}, u32[]{:S(2)}, u32[]{:S(2)}) collective-permute-start(bf16[384,512]{1,0:T(8,128)(2,1)S(1)} %collective-permute-done.3.refs_1_), channel_id=1, source_target_pairs={{0,8},{8,0},{1,9},{9,1},{2,10},{10,2},{3,11},{11,3},{4,12},{12,4},... | collective-permute-start | bytes 1179656 | tf_op jit(solution)/shard_map/ppermute | solution.py:239
  51.8 6.2 %collective-permute-start.2 = (bf16[192,512]{1,0:T(8,128)(2,1)}, bf16[192,512]{1,0:T(8,128)(2,1)S(1)}, u32[]{:S(2)}, u32[]{:S(2)}) collective-permute-start(bf16[192,512]{1,0:T(8,128)(2,1)} %collective-permute-done.1.refs_0_), channel_id=1, source_target_pairs={{0,8},{8,0},{1,9},{9,1},{2,10},{10,2},{3,11},{11,3},{4,12},{12,4},... | collective-permute-start | bytes 589832 | tf_op jit(solution)/shard_map/ppermute | solution.py:239
  51.9 15.3 %copy-start.11 = (bf16[192,512]{1,0:T(8,128)(2,1)}, bf16[192,512]{1,0:T(8,128)(2,1)S(1)}, u32[]{:S(2)}) copy-start(bf16[192,512]{1,0:T(8,128)(2,1)S(1)} %collective-permute-done.4.refs_1_) | copy-start | bytes 589828
  51.9 8.6 %collective-permute-start.11 = (bf16[192,512]{1,0:T(8,128)(2,1)}, bf16[192,512]{1,0:T(8,128)(2,1)S(1)}, u32[]{:S(2)}, u32[]{:S(2)}) collective-permute-start(bf16[192,512]{1,0:T(8,128)(2,1)} %slice.22), channel_id=1, source_target_pairs={{0,16},{16,32},{32,48},{48,0},{1,17},{17,33},{33,49},{49,1},{2,18}... | collective-permute-start | bytes 589832 | tf_op jit(solution)/shard_map/ppermute | solution.py:234
  52.5 14.7 %copy-start.7 = (bf16[384,512]{1,0:T(8,128)(2,1)}, bf16[384,512]{1,0:T(8,128)(2,1)S(1)}, u32[]{:S(2)}) copy-start(bf16[384,512]{1,0:T(8,128)(2,1)S(1)} %collective-permute-done.17.refs_2_) | copy-start | bytes 1179652
  52.5 8.0 %collective-permute-start.12 = (bf16[192,512]{1,0:T(8,128)(2,1)}, bf16[192,512]{1,0:T(8,128)(2,1)}, u32[]{:S(2)}, u32[]{:S(2)}) collective-permute-start(bf16[192,512]{1,0:T(8,128)(2,1)} %slice.23), channel_id=1, source_target_pairs={{0,48},{16,0},{32,16},{48,32},{1,49},{17,1},{33,17},{49,33},{2,50}... | collective-permute-start | bytes 589832 | tf_op jit(solution)/shard_map/ppermute | solution.py:234
  57.5 9.8 %copy-start.8 = (bf16[384,512]{1,0:T(8,128)(2,1)}, bf16[384,512]{1,0:T(8,128)(2,1)S(1)}, u32[]{:S(2)}) copy-start(bf16[384,512]{1,0:T(8,128)(2,1)S(1)} %collective-permute-done.15.refs_0_) | copy-start | bytes 1179652
  57.5 30.1 %collective-permute-start.5 = (bf16[192,512]{1,0:T(8,128)(2,1)S(1)}, bf16[192,512]{1,0:T(8,128)(2,1)S(1)}, u32[]{:S(2)}, u32[]{:S(2)}) collective-permute-start(bf16[192,512]{1,0:T(8,128)(2,1)S(1)} %collective-permute-done.4.refs_1_), channel_id=1, source_target_pairs={{0,8},{8,0},{1,9},{9,1},{2,10},{10,2},{3,11},{11,3},{4,12},{12,4},... | collective-permute-start | bytes 589832 | tf_op jit(solution)/shard_map/ppermute | solution.py:239
  57.5 30.1 %collective-permute-start.10 = (bf16[384,512]{1,0:T(8,128)(2,1)S(1)}, bf16[384,512]{1,0:T(8,128)(2,1)S(1)}, u32[]{:S(2)}, u32[]{:S(2)}) collective-permute-start(bf16[384,512]{1,0:T(8,128)(2,1)S(1)} %collective-permute-done.9.refs_3_), channel_id=1, source_target_pairs={{0,8},{8,0},{1,9},{9,1},{2,10},{10,2},{3,11},{11,3},{4,12},{12,4},... | collective-permute-start | bytes 1179656 | tf_op jit(solution)/shard_map/ppermute | solution.py:239
  58.0 9.3 %copy-start.12 = (bf16[192,512]{1,0:T(8,128)(2,1)}, bf16[192,512]{1,0:T(8,128)(2,1)S(1)}, u32[]{:S(2)}) copy-start(bf16[192,512]{1,0:T(8,128)(2,1)S(1)} %collective-permute-done.2.refs_0_) | copy-start | bytes 589828
  58.0 29.7 %collective-permute-start.8 = (bf16[384,512]{1,0:T(8,128)(2,1)S(1)}, bf16[384,512]{1,0:T(8,128)(2,1)S(1)}, u32[]{:S(2)}, u32[]{:S(2)}) collective-permute-start(bf16[384,512]{1,0:T(8,128)(2,1)S(1)} %collective-permute-done.7.refs_2_), channel_id=1, source_target_pairs={{0,8},{8,0},{1,9},{9,1},{2,10},{10,2},{3,11},{11,3},{4,12},{12,4},... | collective-permute-start | bytes 1179656 | tf_op jit(solution)/shard_map/ppermute | solution.py:239
  60.6 6.7 %copy-start.13 = (bf16[192,512]{1,0:T(8,128)(2,1)}, bf16[192,512]{1,0:T(8,128)(2,1)S(1)}, u32[]{:S(2)}) copy-start(bf16[192,512]{1,0:T(8,128)(2,1)S(1)} %collective-permute-done.11.refs_4_) | copy-start | bytes 589828
  60.6 27.0 %collective-permute-start.13 = (bf16[192,512]{1,0:T(8,128)(2,1)S(1)}, bf16[192,512]{1,0:T(8,128)(2,1)S(1)}, u32[]{:S(2)}, u32[]{:S(2)}) collective-permute-start(bf16[192,512]{1,0:T(8,128)(2,1)S(1)} %collective-permute-done.11.refs_4_), channel_id=1, source_target_pairs={{0,8},{8,0},{1,9},{9,1},{2,10},{10,2},{3,11},{11,3},{4,12},{12,4},... | collective-permute-start | bytes 589832 | tf_op jit(solution)/shard_map/ppermute | solution.py:239
  60.6 27.0 %collective-permute-start.14 = (bf16[192,512]{1,0:T(8,128)(2,1)}, bf16[192,512]{1,0:T(8,128)(2,1)}, u32[]{:S(2)}, u32[]{:S(2)}) collective-permute-start(bf16[192,512]{1,0:T(8,128)(2,1)} %collective-permute-done.12.refs_5_), channel_id=1, source_target_pairs={{0,8},{8,0},{1,9},{9,1},{2,10},{10,2},{3,11},{11,3},{4,12},{12,4},... | collective-permute-start | bytes 589832 | tf_op jit(solution)/shard_map/ppermute | solution.py:239
  87.6 0.7 copy-start.14
  87.6 0.7 copy-start.15
  87.6 0.8 copy-start.9
  87.7 0.9 copy-start.10
  101.2 12.5 %all-to-all-start = ((f32[8,3,128]{2,1,0:T(4,128)}), f32[8,3,128]{2,1,0:T(4,128)S(1)}, u32[]{:S(2)}, u32[]{:S(2)}) async-start(f32[8,3,128]{2,1,0:T(4,128)} %broadcast_in_dim.2), calls=%async_computation | async-start | bytes 32768 | tf_op jit(solution)/shard_map/all_to_all | solution.py:325
  113.7 0.6 copy-start.17
  136.1 20.8 %all-to-all-start.1 = ((bf16[128,8,256]{2,1,0:T(8,128)(2,1)}), bf16[128,8,256]{2,1,0:T(8,128)(2,1)S(1)}, u32[]{:S(2)}, u32[]{:S(2)}) async-start(bf16[128,8,256]{2,1,0:T(8,128)(2,1)} %bitcast.45), calls=%async_computation.1 | async-start | bytes 1048576 | tf_op jit(solution)/shard_map/all_to_all | solution.py:329
  156.9 0.8 copy-start

commit v2 on v1

v2 whole, which is shorter than its diff:
```python
import jax
import jax.numpy as jnp
from jax import lax
from jax.experimental import pallas as pl
from jax.experimental.pallas import tpu as pltpu
from jax.sharding import Mesh
from jax.sharding import PartitionSpec as P

PIX = 4096
TRANS = 8
BLOCK = 128
STENCILS = 8
NBLK = 32
BRICKS = 128
CELLS = 512
SLICE = 512
IMG = ("xh", "y", "c")
POSE = ("z", "xl")
IMG_POSE = ("xh", "y", "c", "z", "xl")
POSE_IMG = ("z", "xl", "xh", "y", "c")
F32 = jnp.float32
BF16 = jnp.bfloat16


LIMIT = pltpu.CompilerParams(vmem_limit_bytes=24 << 20)
IDS = 16


def weight_kernel(img, cos, sin, out):
    step = pl.program_id(0)
    n = img.shape[0]
    for p in range(SLICE // 256):
        re_at = slice(p * 256, p * 256 + 128)
        im_at = slice(p * 256 + 128, p * 256 + 256)
        for g in range(0, n, 16):
            re = img[g : g + 16, re_at].astype(F32)
            im = img[g : g + 16, im_at].astype(F32)
            for t in range(TRANS):
                rows = slice(t * n + g, t * n + g + 16)
                new_re = re * cos[t : t + 1, re_at] + im * sin[t : t + 1, re_at]
                new_im = im * cos[t : t + 1, im_at] + re * sin[t : t + 1, im_at]
                out[step, rows, re_at] = new_re.astype(BF16)
                out[step, rows, im_at] = new_im.astype(BF16)


def weight_rows(images, cos, sin):
    n, width = images.shape
    slices = width // SLICE
    return pl.pallas_call(
        weight_kernel,
        grid=(slices,),
        in_specs=[
            pl.BlockSpec((n, SLICE), lambda i: (0, i)),
            pl.BlockSpec((TRANS, SLICE), lambda i: (0, i)),
            pl.BlockSpec((TRANS, SLICE), lambda i: (0, i)),
        ],
        out_specs=pl.BlockSpec(memory_space=pltpu.VMEM),
        out_shape=pltpu.VMEM((slices, n * TRANS, SLICE), BF16),
        compiler_params=LIMIT,
        cost_estimate=pl.CostEstimate(flops=0, bytes_accessed=16 << 20, transcendentals=0),
        name="weigh",
    )(images, cos, sin)


def scores_call(pairs, where, weighted, noise, carried, last):
    count = len(pairs)
    arrays = [a for pair in pairs for a in pair[:2]]
    rows = weighted.shape[1]
    imgs = rows // TRANS
    poses = 384

    def kernel(pos, *refs):
        parts = refs[: 2 * count]
        w, nz = refs[2 * count : 2 * count + 2]
        rest = refs[2 * count + 2 :]
        if carried is not None:
            s_in, p_in, n_in = rest[:3]
            rest = rest[4:]
        if last:
            h_acc, e_out, st_out, s_acc, p_acc = rest
        else:
            s_acc, p_acc, n_acc, h_acc = rest
        number = jnp.zeros((1, BRICKS), F32) if carried is None else n_in[...]
        for j, (_, _, lo, n, (fx, dy)) in enumerate(pairs):
            chip = jnp.bitwise_xor(pos[0], fx) * 4 + jnp.bitwise_and(pos[1] + dy + 4, 3)
            total = None
            norm = None
            for side in range(2):
                at = chip * 2 + jnp.bitwise_xor(pos[2], side)
                a = parts[2 * j + side][:n, :]
                if lo + n == poses:
                    tag = parts[2 * j + side][n : n + IDS, :].astype(F32)
                    number = number + tag[3:4, :BRICKS]
                    for u in range(12):
                        lanes = slice(u % 4 * 128, u % 4 * 128 + 128)
                        h_acc[u, pl.ds(at, 1), :] = tag[u // 4 : u // 4 + 1, lanes]
                d = lax.dot_general(
                    a, w[at], (((1,), (1,)), ((), ())), preferred_element_type=F32
                )
                wide = a.astype(F32)
                q = wide * wide * nz[at]
                q = q[:, :128] + q[:, 128:256] + (q[:, 256:384] + q[:, 384:])
                total = d if total is None else total + d
                norm = q if norm is None else norm + q
            at = slice(lo, lo + n)
            if carried is None:
                s_acc[at, :] = total
                p_acc[at, :] = norm
            else:
                s_acc[at, :] = s_in[at, :] + total
                p_acc[at, :] = p_in[at, :] + norm
        if not last:
            n_acc[...] = number
        if last:
            half = 0.5 * jnp.sum(p_acc[...], axis=1, keepdims=True)
            m = None
            for t in range(TRANS):
                at = slice(t * imgs, (t + 1) * imgs)
                s = s_acc[:, at] - half
                s_acc[:, at] = s
                s = jnp.max(s, axis=0, keepdims=True)
                m = s if m is None else jnp.maximum(m, s)
            total = jnp.zeros((1, imgs), F32)
            for t in range(TRANS):
                at = slice(t * imgs, (t + 1) * imgs)
                e = jnp.exp(s_acc[:, at] - m)
                e_out[:, at] = e
                total = total + jnp.sum(e, axis=0, keepdims=True)
            st_out[0, 0:1, :] = m
            st_out[0, 1:2, :] = total
            st_out[0, 2:3, :] = number

    vmem = pl.BlockSpec(memory_space=pltpu.VMEM)
    smem = pl.BlockSpec(memory_space=pltpu.SMEM)
    in_specs = [smem] + [vmem] * (2 * count + 2)
    args = [where, *arrays, weighted, noise]
    acc_shapes = ((poses, rows), (poses, 128), (1, BRICKS), (12, 16, 128))
    alias = {}
    if carried is not None:
        in_specs += [vmem] * 4
        alias = {len(args) + 3: 0} if last else {len(args) + j: j for j in range(4)}
        args += list(carried)
    if last:
        out_shape = [
            pltpu.VMEM(acc_shapes[3], F32),
            pltpu.VMEM((poses, rows), F32),
            jax.ShapeDtypeStruct((1, 3, imgs), F32),
        ]
        scratch = [pltpu.VMEM(s, F32) for s in acc_shapes[:2]]
    else:
        out_shape = [pltpu.VMEM(s, F32) for s in acc_shapes]
        scratch = []
    work = sum(2 * 2 * p[3] * SLICE * rows for p in pairs)
    return pl.pallas_call(
        kernel,
        in_specs=in_specs,
        out_specs=[vmem] * len(out_shape),
        scratch_shapes=scratch,
        out_shape=out_shape,
        input_output_aliases=alias,
        compiler_params=LIMIT,
        cost_estimate=pl.CostEstimate(flops=work, bytes_accessed=1 << 20, transcendentals=0),
        name="scores",
    )(*args)


def route_kernel(h, seg):
    ids = None
    for kind, scale in ((0, STENCILS), (1, 1)):
        flat = h[6 * kind : 6 * kind + 6].reshape(96, 128)
        turned = flat.T.astype(BF16)
        u = lax.broadcasted_iota(jnp.int32, (96, 384), 0)
        pose = (u & 15) * 24 + (u >> 4) * 4
        k = lax.broadcasted_iota(jnp.int32, (96, 384), 1)
        for j in range(4):
            put = jnp.where(k == pose + j, 1.0, 0.0).astype(BF16)
            part = jnp.dot(turned[j * 32 : j * 32 + 32, :], put, preferred_element_type=F32)
            part = part * float(scale)
            ids = part if ids is None else ids + part
    seg[...] = ids.astype(jnp.int32)


def route_call(h):
    return pl.pallas_call(
        route_kernel,
        in_specs=[pl.BlockSpec(memory_space=pltpu.VMEM)],
        out_specs=pl.BlockSpec(memory_space=pltpu.VMEM),
        out_shape=pltpu.VMEM((NBLK, 384), jnp.int32),
        compiler_params=LIMIT,
        cost_estimate=pl.CostEstimate(flops=1 << 26, bytes_accessed=1 << 20, transcendentals=0),
        name="route",
    )(h)


def gather_kernel(pos, pieces, e, w, seg, g_out, ev_out, num_out, post, acc):
    step = pl.program_id(0)

    @pl.when(step == 0)
    def _():
        imgs = pieces.shape[2]
        group = [pieces[jnp.bitwise_xor(pos[3], j)] for j in range(8)]
        peak = group[0][0:1, :]
        for g in group[1:]:
            peak = jnp.maximum(peak, g[0:1, :])
        total = jnp.zeros_like(peak)
        number = jnp.zeros_like(peak)
        for g in group:
            total = total + g[1:2, :] * jnp.exp(g[0:1, :] - peak)
            number = number + g[2:3, :]
        ev_out[...] = peak + jnp.log(total)
        here = lax.broadcasted_iota(jnp.int32, number.shape, 1) == pos[4]
        num_out[...] = jnp.sum(jnp.where(here, number, 0.0), axis=1, keepdims=True)
        scale = jnp.exp(pieces[0, 0:1, :] - peak) / total
        for t in range(TRANS):
            at = slice(t * imgs, (t + 1) * imgs)
            post[:, at] = (e[:, at] * scale).astype(BF16)
        acc[...] = jnp.zeros(acc.shape, F32)

    rows = jnp.dot(post[...], w[step], preferred_element_type=F32).astype(BF16)
    both = jnp.concatenate([rows[:, :256], rows[:, 256:]], axis=0)
    ids = jnp.concatenate([seg[pl.ds(2 * step, 1), :], seg[pl.ds(2 * step + 1, 1), :]], axis=1)
    hot = lax.broadcasted_iota(jnp.int32, (acc.shape[0], ids.shape[1]), 0) == ids
    hot = jnp.where(hot, 1.0, 0.0).astype(BF16)
    acc[...] += jnp.dot(hot, both, preferred_element_type=F32)

    @pl.when(step == pl.num_programs(0) - 1)
    def _():
        g_out[...] = acc[...].astype(BF16)


def gather_call(where, pieces, e, weighted, seg):
    segs = BRICKS * STENCILS
    vmem = pl.BlockSpec(memory_space=pltpu.VMEM)
    return pl.pallas_call(
        gather_kernel,
        grid=(weighted.shape[0],),
        in_specs=[pl.BlockSpec(memory_space=pltpu.SMEM)] + [vmem] * 4,
        out_specs=[vmem] * 3,
        out_shape=[
            jax.ShapeDtypeStruct((segs, 256), BF16),
            jax.ShapeDtypeStruct((1, pieces.shape[2]), F32),
            jax.ShapeDtypeStruct((1, 1), F32),
        ],
        scratch_shapes=[pltpu.VMEM(e.shape, BF16), pltpu.VMEM((segs, 256), F32)],
        compiler_params=LIMIT,
        name="gather",
    )(where, pieces, e, weighted, seg)


def volume_kernel(got, interp, count, out):
    total = got[0].astype(F32)
    for j in range(1, got.shape[0]):
        total = total + got[j].astype(F32)
    mixed = total.astype(BF16)
    acc = jnp.zeros((STENCILS, CELLS), F32)
    for s in range(STENCILS):
        row = lax.broadcasted_iota(jnp.int32, mixed.shape, 0) == s
        only = jnp.where(row, total, 0.0).astype(BF16)
        acc = acc + jnp.dot(only, interp[0, s], preferred_element_type=F32)
    del mixed
    out[...] = jnp.sum(acc, axis=0, keepdims=True) * lax.rsqrt(1.0 + count[...])


def volume_call(got, interp, count):
    return pl.pallas_call(
        volume_kernel,
        out_shape=jax.ShapeDtypeStruct((1, CELLS), F32),
        compiler_params=LIMIT,
        name="volume",
    )(got, interp, count)


def shifted(x, axis, by):
    size = lax.axis_size(axis)
    return lax.ppermute(x, axis, [(i, (i + by) % size) for i in range(size)])


def flipped(x, axis):
    return lax.ppermute(x, axis, [(0, 1), (1, 0)])


def body(images, shift_phase, noise_weight, refs, routing, stencil, interp):
    xh, y, c = (lax.axis_index(a) for a in IMG)

    tags = jnp.concatenate([routing[:, 0], stencil]).astype(BF16).reshape(3, SLICE)
    own_counts = jnp.sum(
        (routing == jnp.arange(BRICKS, dtype=jnp.int32)[None, :]).astype(F32), axis=0, keepdims=True
    ).astype(BF16)
    tags = jnp.concatenate(
        [
            tags,
            jnp.pad(own_counts, ((0, 0), (0, SLICE - BRICKS))),
            jnp.zeros((IDS - 4, SLICE), BF16),
        ]
    )
    mine = jnp.concatenate([refs, tags], axis=0)

    across = flipped(mine, "xh")
    left = shifted(mine, "y", 1)
    right = shifted(mine, "y", -1)
    far_low = shifted(left[:192], "y", 1)
    far_high = shifted(right[192:], "y", -1)
    aleft = shifted(across, "y", 1)
    aright = shifted(across, "y", -1)
    afar_low = shifted(aleft[:192], "y", 1)
    afar_high = shifted(aright[192:], "y", -1)
    rounds = [
        [(mine, 0, 384, (0, 0))],
        [(left, 0, 384, (0, -1)), (right, 0, 384, (0, 1)), (across, 0, 384, (1, 0))],
        [
            (far_low, 0, 192, (0, 2)),
            (far_high, 192, 192, (0, 2)),
            (aleft, 0, 384, (1, -1)),
            (aright, 0, 384, (1, 1)),
        ],
        [(afar_low, 0, 192, (1, 2)), (afar_high, 192, 192, (1, 2))],
    ]

    noise = noise_weight.reshape(16, 1, SLICE)
    by_block = noise_weight.reshape(1, NBLK, 2, BLOCK)
    angles = shift_phase.reshape(TRANS, NBLK, 1, BLOCK)
    cos = (jnp.cos(angles) * by_block).reshape(TRANS, 2 * PIX)
    sign = jnp.array([1.0, -1.0], F32).reshape(1, 1, 2, 1)
    sin = (jnp.sin(angles) * by_block * sign).reshape(TRANS, 2 * PIX)
    pose = lax.axis_index(POSE)
    where = jnp.stack([xh, y, c, pose, lax.axis_index(IMG_POSE)]).astype(jnp.int32)
    where, cos = lax.optimization_barrier((where, cos))
    weighted = weight_rows(images, cos, sin)

    paired = [[(p[0], flipped(p[0], "c"), *p[1:]) for p in turn] for turn in rounds]

    carried = None
    for j, pairs in enumerate(paired):
        carried = scores_call(pairs, where, weighted, noise, carried, j == len(paired) - 1)
    marks, e, pieces = carried

    for axis, bit in (("xl", 1), ("z", 1), ("z", 2)):
        size = lax.axis_size(axis)
        other = lax.ppermute(pieces, axis, [(i, i ^ bit) for i in range(size)])
        pieces = jnp.concatenate([pieces, other], axis=0)
    seg = route_call(marks)
    gathered, evidence, count = gather_call(where, pieces, e, weighted, seg)
    got = lax.all_to_all(
        gathered.reshape(BRICKS, STENCILS, 2 * BLOCK), IMG_POSE, 0, 0, tiled=True
    )
    volume = volume_call(got, interp, count)
    return (volume, evidence.reshape(-1))


def solution(mesh):
    finer = Mesh(mesh.devices.reshape(2, 4, 2, 4, 2), ("xh", "y", "c", "z", "xl"))
    return jax.shard_map(
        body,
        mesh=finer,
        in_specs=(
            P(IMG, None),
            P(),
            P(),
            P(POSE, IMG),
            P(POSE_IMG, None),
            P(POSE_IMG),
            P(IMG_POSE, None, None, None),
        ),
        out_specs=(P(IMG_POSE, None), P(IMG)),
        check_vma=False,
    )
```

time: 163 us -> 119 us (0.73); the launches traced: 161 us -> 119 us
  Pallas kernels: 74.9 us -> 40 us
  blocking collectives: 0 us -> 21.4 us
  starting transfers between devices: 35.3 us -> 24.2 us
  local copies, waits for them, and re-layouts: 10.5 us -> 3.66 us
  other arithmetic: 9.21 us -> 2.83 us
  waiting for transfers between devices: 30.2 us -> 25.8 us
    pallas_call x7, Pallas kernels: 71.5 us -> 38.2 us  [the longest x1 19.9 us: gather_call(): pl.pallas_call(gather_kernel, grid=(weighted.shape[0],), in_specs=[pl.Blo...]
    all_to_all x0 -> x1, blocking collectives: none -> 21.4 us  [body(): lax.all_to_all(gathered.reshape(BRICKS, STENCILS, 2 * BLOCK), IMG_POSE, 0...]
    ppermute x8, waiting for transfers between devices: 2.43 us -> 20.5 us  [shifted(): return lax.ppermute(x, axis, [(i, (i + by) % size) for i in range(size)])]
    all_to_all x2 -> x0, waiting for transfers between devices: 17.1 us -> none  [the longest x1 12.2 us: body(): lax.all_to_all(gathered.reshape(BRICKS, STENCILS, 2 * BLOCK), IMG_POSE, 0...]
    all_to_all x2 -> x0, starting transfers between devices: 13.5 us -> none  [the longest x1 7.28 us: body(): lax.all_to_all(gathered.reshape(BRICKS, STENCILS, 2 * BLOCK), IMG_POSE, 0...]
    ppermute x15 -> x14, waiting for transfers between devices: 10.6 us -> 5.34 us  [the longest x3 5.11 us: body(): other = lax.ppermute(pieces, axis, [(i, i ^ bit) for i in range(size)])]
    ppermute x15 -> x14, starting transfers between devices: 9.05 us -> 12.7 us  [the longest x3 7.37 us: body(): other = lax.ppermute(pieces, axis, [(i, i ^ bit) for i in range(size)])]
    unnamed x38 -> x26, local copies, waits for them, and re-layouts: 2.38 us -> 0.06 us
  transfers between devices with their start and end apart: 25 -> 22, of which waited for: 6 -> 8; matrix products, arithmetic and copies ran while one was open for 9% -> 3% of each run, Pallas kernels for 24% -> 13%
where the time goes in v2:
time: 119 us
  Pallas kernels  40 us (34%)
  waiting for transfers between devices  25.8 us (22%)
  starting transfers between devices  24.2 us (20%)
  blocking collectives  21.4 us (18%)
  local copies, waits for them, and re-layouts  3.66 us (3%)
  other arithmetic  2.83 us (2%)
    all_to_all x1, blocking collectives, body(): lax.all_to_all(gathered.reshape(BRICKS, STENCILS, 2 * BLOCK), IMG_POSE, 0...  21.4 us
    ppermute x8, waiting for transfers between devices, shifted(): return lax.ppermute(x, axis, [(i, (i + by) % size) for i in range(size)])  20.5 us
    pallas_call x1, Pallas kernels, gather_call(): pl.pallas_call(gather_kernel, grid=(weighted.shape[0],), in_specs=[pl.Blo...  19.9 us
    pallas_call x4, Pallas kernels, scores_call(): pl.pallas_call(kernel, in_specs=in_specs, out_specs=[vmem] * len(out_shap...  13.7 us
    ppermute x8, starting transfers between devices, shifted(): return lax.ppermute(x, axis, [(i, (i + by) % size) for i in range(size)])  11.5 us
    ppermute x3, starting transfers between devices, body(): other = lax.ppermute(pieces, axis, [(i, i ^ bit) for i in range(size)])  7.37 us
    ppermute x11, starting transfers between devices, flipped(): return lax.ppermute(x, axis, [(0, 1), (1, 0)])  5.31 us
    ppermute x3, waiting for transfers between devices, body(): other = lax.ppermute(pieces, axis, [(i, i ^ bit) for i in range(size)])  5.11 us
  transfers between devices with their start and end apart: 22, of which 8 were waited for; matrix products, arithmetic and copies ran while one was open for 3% of the time, Pallas kernels for 13%

profile of v2, /device:TPU:0, one launch (start us, length us, event | category | flops | bytes accessed | tf_op | source)
XLA Modules:
  0.0 118.8 jit_solution(9402383132184341119)
XLA Ops:
  0.6 0.0 copy-start.12
  0.7 0.7 reduce
  1.4 0.2 convert_reduce_fusion
  1.6 0.7 convert.7
  2.3 0.1 pad.17.clone
  2.4 1.1 fusion.3.refs_0_
  3.5 0.0 copy-start
  3.5 1.8 %collective-permute-start.7 = (bf16[400,512]{1,0:T(8,128)(2,1)S(1)}, bf16[400,512]{1,0:T(8,128)(2,1)}, u32[]{:S(2)}, u32[]{:S(2)}) collective-permute-start(bf16[400,512]{1,0:T(8,128)(2,1)S(1)} %fusion.3.refs_0_), channel_id=1, source_target_pairs={{0,16},{16,32},{32,48},{48,0},{1,17},{17,33},{33,49},{49,1},{2,18}... | collective-permute-start | bytes 1228808 | tf_op jit(solution)/shard_map/ppermute | solution.py:275
  5.3 3.0 %collective-permute-start = (bf16[400,512]{1,0:T(8,128)(2,1)S(1)}, bf16[400,512]{1,0:T(8,128)(2,1)}, u32[]{:S(2)}, u32[]{:S(2)}) collective-permute-start(bf16[400,512]{1,0:T(8,128)(2,1)S(1)} %fusion.3.refs_0_), channel_id=1, source_target_pairs={{0,64},{64,0},{1,65},{65,1},{2,66},{66,2},{3,67},{67,3},{4,68},{68... | collective-permute-start | bytes 1228808 | tf_op jit(solution)/shard_map/ppermute | solution.py:279
  8.3 1.7 %collective-permute-start.10 = (bf16[400,512]{1,0:T(8,128)(2,1)S(1)}, bf16[400,512]{1,0:T(8,128)(2,1)}, u32[]{:S(2)}, u32[]{:S(2)}) collective-permute-start(bf16[400,512]{1,0:T(8,128)(2,1)S(1)} %fusion.3.refs_0_), channel_id=1, source_target_pairs={{0,48},{16,0},{32,16},{48,32},{1,49},{17,1},{33,17},{49,33},{2,50}... | collective-permute-start | bytes 1228808 | tf_op jit(solution)/shard_map/ppermute | solution.py:275
  10.0 6.3 %collective-permute-done.7.refs_0_ = bf16[400,512]{1,0:T(8,128)(2,1)} collective-permute-done((bf16[400,512]{1,0:T(8,128)(2,1)S(1)}, bf16[400,512]{1,0:T(8,128)(2,1)}, u32[]{:S(2)}, u32[]{:S(2)}) %collective-permute-start.7) | collective-permute-done | bytes 409632 | tf_op jit(solution)/shard_map/ppermute | solution.py:275
  16.3 0.9 slice.18
  17.3 0.4 collective-permute-start.8
  17.6 0.2 collective-permute-done.refs_4_
  17.8 1.6 %collective-permute-start.1 = (bf16[400,512]{1,0:T(8,128)(2,1)}, bf16[400,512]{1,0:T(8,128)(2,1)}, u32[]{:S(2)}, u32[]{:S(2)}) collective-permute-start(bf16[400,512]{1,0:T(8,128)(2,1)} %collective-permute-done.refs_4_), channel_id=1, source_target_pairs={{0,16},{16,32},{32,48},{48,0},{1,17},{17,33},{33,49},{49,1},{2,18}... | collective-permute-start | bytes 1228808 | tf_op jit(solution)/shard_map/ppermute | solution.py:275
  19.4 1.7 %collective-permute-start.4 = (bf16[400,512]{1,0:T(8,128)(2,1)}, bf16[400,512]{1,0:T(8,128)(2,1)S(1)}, u32[]{:S(2)}, u32[]{:S(2)}) collective-permute-start(bf16[400,512]{1,0:T(8,128)(2,1)} %collective-permute-done.refs_4_), channel_id=1, source_target_pairs={{0,48},{16,0},{32,16},{48,32},{1,49},{17,1},{33,17},{49,33},{2,50}... | collective-permute-start | bytes 1228808 | tf_op jit(solution)/shard_map/ppermute | solution.py:275
  21.1 0.9 slice.19
  22.0 1.6 %collective-permute-start.11 = (bf16[208,512]{1,0:T(8,128)(2,1)S(1)}, bf16[208,512]{1,0:T(8,128)(2,1)S(1)}, u32[]{:S(2)}, u32[]{:S(2)}) collective-permute-start(bf16[208,512]{1,0:T(8,128)(2,1)S(1)} %slice.19), channel_id=1, source_target_pairs={{0,48},{16,0},{32,16},{48,32},{1,49},{17,1},{33,17},{49,33},{2,50}... | collective-permute-start | bytes 638984 | tf_op jit(solution)/shard_map/ppermute | solution.py:275
  23.6 2.7 %collective-permute-done.8.refs_0_ = bf16[192,512]{1,0:T(8,128)(2,1)S(1)} collective-permute-done((bf16[192,512]{1,0:T(8,128)(2,1)S(1)}, bf16[192,512]{1,0:T(8,128)(2,1)S(1)}, u32[]{:S(2)}, u32[]{:S(2)}) %collective-permute-start.8) | collective-permute-done | bytes 196640 | tf_op jit(solution)/shard_map/ppermute | solution.py:275
  26.3 0.5 sine_bitcast_fusion
  26.8 0.6 collective-permute-start.17
  27.4 8.2 %collective-permute-done.11.refs_2_ = bf16[208,512]{1,0:T(8,128)(2,1)S(1)} collective-permute-done((bf16[208,512]{1,0:T(8,128)(2,1)S(1)}, bf16[208,512]{1,0:T(8,128)(2,1)S(1)}, u32[]{:S(2)}, u32[]{:S(2)}) %collective-permute-start.11) | collective-permute-done | bytes 213024 | tf_op jit(solution)/shard_map/ppermute | solution.py:275
  35.6 0.5 collective-permute-start.16
  36.1 0.1 collective-permute-start.13
  36.2 0.4 collective-permute-start.14
  36.7 0.1 mul.67
  36.8 0.1 multiply_multiply_fusion
  36.9 0.1 stack.23.pos
  37.0 4.3 %weigh.1.refs_2_.refs_6_.refs_8_.refs_4_.w = bf16[16,1024,512]{2,1,0:T(8,128)(2,1)S(1)} custom-call(bf16[128,8192]{1,0:T(8,128)(2,1)S(1)} %copy-done, f32[8,8192]{1,0:T(8,128)S(1)} %get-tuple-element.23.cos, f32[8,8192]{1,0:T(8,128)S(1)} %get-tuple-element.44.sin), custom_call_target="tpu_custom_call" | custom-call | bytes 16777216 | tf_op jit(solution)/shard_map/weigh/pallas_call | solution.py:49
  41.3 1.6 %scores.4 = (f32[384,1024]{1,0:T(8,128)S(1)}, f32[384,128]{1,0:T(8,128)S(1)}, f32[1,128]{1,0:T(1,128)S(1)}, f32[12,16,128]{2,1,0:T(8,128)S(1)}) custom-call(s32[5]{0:T(128)S(1)} %stack.23.pos, bf16[400,512]{1,0:T(8,128)(2,1)S(1)} %fusion.3.refs_0_, bf16[400,512]{1,0:T(8,128)(2,1)S(1)} %copy-done.4, ...), custom_call_target="tpu_custom_call" | custom-call | flops 805306368 | bytes 1048576 | tf_op jit(solution)/shard_map/scores/pallas_call | solution.py:154
  42.9 0.9 slice.16
  43.9 0.2 collective-permute-start.12
  44.1 2.9 %collective-permute-start.5 = (bf16[208,512]{1,0:T(8,128)(2,1)S(1)}, bf16[208,512]{1,0:T(8,128)(2,1)S(1)}, u32[]{:S(2)}, u32[]{:S(2)}) collective-permute-start(bf16[208,512]{1,0:T(8,128)(2,1)S(1)} %slice.17), channel_id=1, source_target_pairs={{0,48},{16,0},{32,16},{48,32},{1,49},{17,1},{33,17},{49,33},{2,50}... | collective-permute-start | bytes 638984 | tf_op jit(solution)/shard_map/ppermute | solution.py:275
  47.0 4.9 %scores.5 = (f32[384,1024]{1,0:T(8,128)S(1)}, f32[384,128]{1,0:T(8,128)S(1)}, f32[1,128]{1,0:T(1,128)S(1)}, f32[12,16,128]{2,1,0:T(8,128)S(1)}) custom-call(s32[5]{0:T(128)S(1)} %stack.23.pos, bf16[400,512]{1,0:T(8,128)(2,1)} %collective-permute-done.7.refs_0_, ...), custom_call_target="tpu_custom_call", output_to_operand_aliasing={{0}: (9, {}), {1}: (10, {}), {2}: (11, {}), {3}: (12, {})} | custom-call | flops 2415919104 | bytes 1048576 | tf_op jit(solution)/shard_map/scores/pallas_call | solution.py:154
  51.9 3.2 %collective-permute-done.2.refs_0_ = bf16[192,512]{1,0:T(8,128)(2,1)S(1)} collective-permute-done((bf16[192,512]{1,0:T(8,128)(2,1)S(1)}, bf16[192,512]{1,0:T(8,128)(2,1)S(1)}, u32[]{:S(2)}, u32[]{:S(2)}) %collective-permute-start.2) | collective-permute-done | bytes 196640 | tf_op jit(solution)/shard_map/ppermute | solution.py:275
  55.1 0.5 collective-permute-start.6
  55.7 4.9 %scores.6 = (f32[384,1024]{1,0:T(8,128)S(1)}, f32[384,128]{1,0:T(8,128)S(1)}, f32[1,128]{1,0:T(1,128)S(1)}, f32[12,16,128]{2,1,0:T(8,128)S(1)}) custom-call(s32[5]{0:T(128)S(1)} %stack.23.pos, bf16[192,512]{1,0:T(8,128)(2,1)S(1)} %copy-done.8, ...), custom_call_target="tpu_custom_call", output_to_operand_aliasing={{0}: (11, {}), {1}: (12, {}), {2}: (13, {}), {3}: (14, {})} | custom-call | flops 2415919104 | bytes 1048576 | tf_op jit(solution)/shard_map/scores/pallas_call | solution.py:154
  60.5 2.4 %scores.7 = (f32[12,16,128]{2,1,0:T(8,128)S(1)}, f32[384,1024]{1,0:T(8,128)S(1)}, f32[1,3,128]{2,1,0:T(4,128)S(1)}) custom-call(s32[5]{0:T(128)S(1)} %stack.23.pos, bf16[192,512]{1,0:T(8,128)(2,1)S(1)} %collective-permute-done.2.refs_0_, bf16[192,512]{1,0:T(8,128)(2,1)S(1)} %collective-permute-done.3.refs_1_, ...), custom_call_target="tpu_custom_call", output_to_operand_aliasing={{0}: (10, {})} | custom-call | flops 805306368 | bytes 1048576 | tf_op jit(solution)/shard_map/scores/pallas_call | solution.py:154
  63.0 1.6 %collective-permute-start.19 = (f32[1,3,128]{2,1,0:T(4,128)S(1)}, f32[1,3,128]{2,1,0:T(4,128)S(1)}, u32[]{:S(2)}, u32[]{:S(2)}) collective-permute-start(f32[1,3,128]{2,1,0:T(4,128)S(1)} %get-tuple-element.36), channel_id=1, source_target_pairs={{0,1},{1,0},{2,3},{3,2},{4,5},{5,4},{6,7},{7,6},{8,9},{9,8},{10,11... | collective-permute-start | bytes 4616 | tf_op jit(solution)/shard_map/ppermute | solution.py:339
  64.5 2.1 %collective-permute-done.19 = f32[1,3,128]{2,1,0:T(4,128)S(1)} collective-permute-done((f32[1,3,128]{2,1,0:T(4,128)S(1)}, f32[1,3,128]{2,1,0:T(4,128)S(1)}, u32[]{:S(2)}, u32[]{:S(2)}) %collective-permute-start.19) | collective-permute-done | bytes 1568 | tf_op jit(solution)/shard_map/ppermute | solution.py:339
  66.6 1.9 %collective-permute-start.20 = (f32[2,3,128]{2,1,0:T(4,128)S(1)}, f32[2,3,128]{2,1,0:T(4,128)S(1)}, u32[]{:S(2)}, u32[]{:S(2)}) collective-permute-start(f32[2,3,128]{2,1,0:T(4,128)S(1)} %pad_maximum_fusion.3), channel_id=1, source_target_pairs={{0,2},{2,0},{4,6},{6,4},{1,3},{3,1},{5,7},{7,5},{8,10},{10,8},{12,... | collective-permute-start | bytes 9224 | tf_op jit(solution)/shard_map/ppermute | solution.py:339
  68.5 1.7 %collective-permute-done.20 = f32[2,3,128]{2,1,0:T(4,128)S(1)} collective-permute-done((f32[2,3,128]{2,1,0:T(4,128)S(1)}, f32[2,3,128]{2,1,0:T(4,128)S(1)}, u32[]{:S(2)}, u32[]{:S(2)}) %collective-permute-start.20) | collective-permute-done | bytes 3104 | tf_op jit(solution)/shard_map/ppermute | solution.py:339
  70.2 3.9 %collective-permute-start.21 = (f32[4,3,128]{2,1,0:T(4,128)S(1)}, f32[4,3,128]{2,1,0:T(4,128)S(1)}, u32[]{:S(2)}, u32[]{:S(2)}) collective-permute-start(f32[4,3,128]{2,1,0:T(4,128)S(1)} %pad_maximum_fusion.1), channel_id=1, source_target_pairs={{0,4},{2,6},{4,0},{6,2},{1,5},{3,7},{5,1},{7,3},{8,12},{10,14},{12... | collective-permute-start | bytes 18440 | tf_op jit(solution)/shard_map/ppermute | solution.py:339
  74.1 0.3 route.1.seg
  74.4 1.3 %collective-permute-done.21 = f32[4,3,128]{2,1,0:T(4,128)S(1)} collective-permute-done((f32[4,3,128]{2,1,0:T(4,128)S(1)}, f32[4,3,128]{2,1,0:T(4,128)S(1)}, u32[]{:S(2)}, u32[]{:S(2)}) %collective-permute-start.21) | collective-permute-done | bytes 6176 | tf_op jit(solution)/shard_map/ppermute | solution.py:339
  75.8 19.9 %gather.1 = (bf16[1024,256]{1,0:T(8,128)(2,1)S(1)}, f32[1,128]{1,0:T(1,128)}, f32[1,1]{1,0:T(1,128)}) custom-call(s32[5]{0:T(128)S(1)} %stack.23.pos, f32[8,3,128]{2,1,0:T(4,128)S(1)} %pad_maximum_fusion.pieces, f32[384,1024]{1,0:T(8,128)S(1)} %get-tuple-element.37.e, bf16[16,1024,512]{2,1,0:T(8,128)(2,1)S(1)} %weigh.1.refs_2_.refs_6_.refs_8_.refs_4_.w, ...), custom_call_target="tpu_custom_call" | custom-call | tf_op jit(solution)/shard_map/gather/pallas_call | solution.py:234
  95.6 21.4 %all_to_all.5.got = bf16[128,8,256]{2,1,0:T(8,128)(2,1)S(1)} all-to-all(bf16[128,8,256]{2,1,0:T(8,128)(2,1)S(1)} %bitcast.22), channel_id=1, replica_groups=mesh['xh'=2,'y'=4,'c'=2,'z'=4,'xl'=2] {'xh','y','c','z','xl'}, dimensions={0} | all-to-all | bytes 1048576 | tf_op jit(solution)/shard_map/all_to_all | solution.py:343
  117.0 1.8 %volume.1 = f32[1,512]{1,0:T(1,128)} custom-call(bf16[128,8,256]{2,1,0:T(8,128)(2,1)S(1)} %all_to_all.5.got, bf16[1,8,256,512]{3,2,1,0:T(8,128)(2,1)S(1)} %copy-done.1, f32[1,1]{1,0:T(1,128)} %get-tuple-element.40.count), custom_call_target="tpu_custom_call" | custom-call | tf_op jit(solution)/shard_map/volume/pallas_call | solution.py:265
  (53 shorter events, 0.2 us)
Async XLA Ops:
  0.6 36.0 %copy-start.12 = (f32[2]{0:T(128)S(1)}, f32[2]{0:T(128)}, u32[]{:S(2)}) copy-start(f32[2]{0:T(128)} %constant.35.clone) | copy-start | bytes 28
  0.6 36.2 %copy-start.2 = (f32[8192]{0:T(1024)S(1)}, f32[8192]{0:T(1024)}, u32[]{:S(2)}) copy-start(f32[8192]{0:T(1024)} %param.10) | copy-start | bytes 98308
  2.3 24.0 %copy-start.11 = (f32[8,4096]{1,0:T(8,128)S(1)}, f32[8,4096]{1,0:T(8,128)}, u32[]{:S(2)}) copy-start(f32[8,4096]{1,0:T(8,128)} %param.9) | copy-start | bytes 393220
  3.5 33.4 %copy-start = (bf16[128,8192]{1,0:T(8,128)(2,1)S(1)}, bf16[128,8192]{1,0:T(8,128)(2,1)}, u32[]{:S(2)}) copy-start(bf16[128,8192]{1,0:T(8,128)(2,1)} %img.1) | copy-start | bytes 6291460
  3.5 12.8 %collective-permute-start.7 = (bf16[400,512]{1,0:T(8,128)(2,1)S(1)}, bf16[400,512]{1,0:T(8,128)(2,1)}, u32[]{:S(2)}, u32[]{:S(2)}) collective-permute-start(bf16[400,512]{1,0:T(8,128)(2,1)S(1)} %fusion.3.refs_0_), channel_id=1, source_target_pairs={{0,16},{16,32},{32,48},{48,0},{1,17},{17,33},{33,49},{49,1},{2,18}... | collective-permute-start | bytes 1228808 | tf_op jit(solution)/shard_map/ppermute | solution.py:275
  5.3 12.5 %collective-permute-start = (bf16[400,512]{1,0:T(8,128)(2,1)S(1)}, bf16[400,512]{1,0:T(8,128)(2,1)}, u32[]{:S(2)}, u32[]{:S(2)}) collective-permute-start(bf16[400,512]{1,0:T(8,128)(2,1)S(1)} %fusion.3.refs_0_), channel_id=1, source_target_pairs={{0,64},{64,0},{1,65},{65,1},{2,66},{66,2},{3,67},{67,3},{4,68},{68... | collective-permute-start | bytes 1228808 | tf_op jit(solution)/shard_map/ppermute | solution.py:279
  8.3 12.8 %collective-permute-start.10 = (bf16[400,512]{1,0:T(8,128)(2,1)S(1)}, bf16[400,512]{1,0:T(8,128)(2,1)}, u32[]{:S(2)}, u32[]{:S(2)}) collective-permute-start(bf16[400,512]{1,0:T(8,128)(2,1)S(1)} %fusion.3.refs_0_), channel_id=1, source_target_pairs={{0,48},{16,0},{32,16},{48,32},{1,49},{17,1},{33,17},{49,33},{2,50}... | collective-permute-start | bytes 1228808 | tf_op jit(solution)/shard_map/ppermute | solution.py:275
  17.3 9.1 %collective-permute-start.8 = (bf16[192,512]{1,0:T(8,128)(2,1)S(1)}, bf16[192,512]{1,0:T(8,128)(2,1)S(1)}, u32[]{:S(2)}, u32[]{:S(2)}) collective-permute-start(bf16[192,512]{1,0:T(8,128)(2,1)S(1)} %slice.18), channel_id=1, source_target_pairs={{0,16},{16,32},{32,48},{48,0},{1,17},{17,33},{33,49},{49,1},{2,18}... | collective-permute-start | bytes 589832 | tf_op jit(solution)/shard_map/ppermute | solution.py:275
  17.6 9.2 %collective-permute-start.18 = (bf16[400,512]{1,0:T(8,128)(2,1)S(1)}, bf16[400,512]{1,0:T(8,128)(2,1)S(1)}, u32[]{:S(2)}, u32[]{:S(2)}) collective-permute-start(bf16[400,512]{1,0:T(8,128)(2,1)S(1)} %fusion.3.refs_0_), channel_id=1, source_target_pairs={{0,8},{8,0},{1,9},{9,1},{2,10},{10,2},{3,11},{11,3},{4,12},{12,4},... | collective-permute-start | bytes 1228808 | tf_op jit(solution)/shard_map/ppermute | solution.py:279
  17.8 18.3 %collective-permute-start.1 = (bf16[400,512]{1,0:T(8,128)(2,1)}, bf16[400,512]{1,0:T(8,128)(2,1)}, u32[]{:S(2)}, u32[]{:S(2)}) collective-permute-start(bf16[400,512]{1,0:T(8,128)(2,1)} %collective-permute-done.refs_4_), channel_id=1, source_target_pairs={{0,16},{16,32},{32,48},{48,0},{1,17},{17,33},{33,49},{49,1},{2,18}... | collective-permute-start | bytes 1228808 | tf_op jit(solution)/shard_map/ppermute | solution.py:275
  19.4 16.8 %collective-permute-start.4 = (bf16[400,512]{1,0:T(8,128)(2,1)}, bf16[400,512]{1,0:T(8,128)(2,1)S(1)}, u32[]{:S(2)}, u32[]{:S(2)}) collective-permute-start(bf16[400,512]{1,0:T(8,128)(2,1)} %collective-permute-done.refs_4_), channel_id=1, source_target_pairs={{0,48},{16,0},{32,16},{48,32},{1,49},{17,1},{33,17},{49,33},{2,50}... | collective-permute-start | bytes 1228808 | tf_op jit(solution)/shard_map/ppermute | solution.py:275
  22.0 13.6 %collective-permute-start.11 = (bf16[208,512]{1,0:T(8,128)(2,1)S(1)}, bf16[208,512]{1,0:T(8,128)(2,1)S(1)}, u32[]{:S(2)}, u32[]{:S(2)}) collective-permute-start(bf16[208,512]{1,0:T(8,128)(2,1)S(1)} %slice.19), channel_id=1, source_target_pairs={{0,48},{16,0},{32,16},{48,32},{1,49},{17,1},{33,17},{49,33},{2,50}... | collective-permute-start | bytes 638984 | tf_op jit(solution)/shard_map/ppermute | solution.py:275
  26.3 10.5 %copy-start.7 = (bf16[192,512]{1,0:T(8,128)(2,1)}, bf16[192,512]{1,0:T(8,128)(2,1)S(1)}, u32[]{:S(2)}) copy-start(bf16[192,512]{1,0:T(8,128)(2,1)S(1)} %collective-permute-done.8.refs_0_) | copy-start | bytes 589828
  26.3 9.3 %collective-permute-start.9 = (bf16[192,512]{1,0:T(8,128)(2,1)S(1)}, bf16[192,512]{1,0:T(8,128)(2,1)S(1)}, u32[]{:S(2)}, u32[]{:S(2)}) collective-permute-start(bf16[192,512]{1,0:T(8,128)(2,1)S(1)} %collective-permute-done.8.refs_0_), channel_id=1, source_target_pairs={{0,8},{8,0},{1,9},{9,1},{2,10},{10,2},{3,11},{11,3},{4,12},{12,4},... | collective-permute-start | bytes 589832 | tf_op jit(solution)/shard_map/ppermute | solution.py:279
  26.8 10.0 %copy-start.3 = (bf16[400,512]{1,0:T(8,128)(2,1)}, bf16[400,512]{1,0:T(8,128)(2,1)S(1)}, u32[]{:S(2)}) copy-start(bf16[400,512]{1,0:T(8,128)(2,1)S(1)} %collective-permute-done.18.refs_1_) | copy-start | bytes 1228804
  26.8 17.1 %collective-permute-start.17 = (bf16[400,512]{1,0:T(8,128)(2,1)}, bf16[400,512]{1,0:T(8,128)(2,1)}, u32[]{:S(2)}, u32[]{:S(2)}) collective-permute-start(bf16[400,512]{1,0:T(8,128)(2,1)} %collective-permute-done.refs_4_), channel_id=1, source_target_pairs={{0,8},{8,0},{1,9},{9,1},{2,10},{10,2},{3,11},{11,3},{4,12},{12,4},... | collective-permute-start | bytes 1228808 | tf_op jit(solution)/shard_map/ppermute | solution.py:279
  35.6 1.2 %copy-start.5 = (bf16[208,512]{1,0:T(8,128)(2,1)}, bf16[208,512]{1,0:T(8,128)(2,1)S(1)}, u32[]{:S(2)}) copy-start(bf16[208,512]{1,0:T(8,128)(2,1)S(1)} %collective-permute-done.11.refs_2_) | copy-start | bytes 638980
  35.6 8.5 %collective-permute-start.15 = (bf16[400,512]{1,0:T(8,128)(2,1)}, bf16[400,512]{1,0:T(8,128)(2,1)}, u32[]{:S(2)}, u32[]{:S(2)}) collective-permute-start(bf16[400,512]{1,0:T(8,128)(2,1)} %collective-permute-done.7.refs_0_), channel_id=1, source_target_pairs={{0,8},{8,0},{1,9},{9,1},{2,10},{10,2},{3,11},{11,3},{4,12},{12,4},... | collective-permute-start | bytes 1228808 | tf_op jit(solution)/shard_map/ppermute | solution.py:279
  35.6 1.2 %copy-start.9 = (bf16[192,512]{1,0:T(8,128)(2,1)}, bf16[192,512]{1,0:T(8,128)(2,1)S(1)}, u32[]{:S(2)}) copy-start(bf16[192,512]{1,0:T(8,128)(2,1)S(1)} %collective-permute-done.9.refs_1_) | copy-start | bytes 589828
  35.6 11.4 %collective-permute-start.16 = (bf16[400,512]{1,0:T(8,128)(2,1)}, bf16[400,512]{1,0:T(8,128)(2,1)}, u32[]{:S(2)}, u32[]{:S(2)}) collective-permute-start(bf16[400,512]{1,0:T(8,128)(2,1)} %collective-permute-done.10.refs_2_), channel_id=1, source_target_pairs={{0,8},{8,0},{1,9},{9,1},{2,10},{10,2},{3,11},{11,3},{4,12},{12,4},... | collective-permute-start | bytes 1228808 | tf_op jit(solution)/shard_map/ppermute | solution.py:279
  36.1 19.5 %collective-permute-start.13 = (bf16[400,512]{1,0:T(8,128)(2,1)}, bf16[400,512]{1,0:T(8,128)(2,1)}, u32[]{:S(2)}, u32[]{:S(2)}) collective-permute-start(bf16[400,512]{1,0:T(8,128)(2,1)} %collective-permute-done.1.refs_4_), channel_id=1, source_target_pairs={{0,8},{8,0},{1,9},{9,1},{2,10},{10,2},{3,11},{11,3},{4,12},{12,4},... | collective-permute-start | bytes 1228808 | tf_op jit(solution)/shard_map/ppermute | solution.py:279
  36.2 19.4 %collective-permute-start.14 = (bf16[400,512]{1,0:T(8,128)(2,1)S(1)}, bf16[400,512]{1,0:T(8,128)(2,1)}, u32[]{:S(2)}, u32[]{:S(2)}) collective-permute-start(bf16[400,512]{1,0:T(8,128)(2,1)S(1)} %collective-permute-done.4.refs_6_), channel_id=1, source_target_pairs={{0,8},{8,0},{1,9},{9,1},{2,10},{10,2},{3,11},{11,3},{4,12},{12,4},... | collective-permute-start | bytes 1228808 | tf_op jit(solution)/shard_map/ppermute | solution.py:279
  37.0 4.4 %copy-start.4 = (bf16[400,512]{1,0:T(8,128)(2,1)S(1)}, bf16[400,512]{1,0:T(8,128)(2,1)}, u32[]{:S(2)}) copy-start(bf16[400,512]{1,0:T(8,128)(2,1)} %copy-done.3) | copy-start | bytes 1228804
  41.3 2.6 %copy-start.6 = (bf16[208,512]{1,0:T(8,128)(2,1)S(1)}, bf16[208,512]{1,0:T(8,128)(2,1)}, u32[]{:S(2)}) copy-start(bf16[208,512]{1,0:T(8,128)(2,1)} %copy-done.5) | copy-start | bytes 638980
  43.9 11.7 %collective-permute-start.12 = (bf16[208,512]{1,0:T(8,128)(2,1)S(1)}, bf16[208,512]{1,0:T(8,128)(2,1)S(1)}, u32[]{:S(2)}, u32[]{:S(2)}) collective-permute-start(bf16[208,512]{1,0:T(8,128)(2,1)S(1)} %copy-done.6), channel_id=1, source_target_pairs={{0,8},{8,0},{1,9},{9,1},{2,10},{10,2},{3,11},{11,3},{4,12},{12,4},... | collective-permute-start | bytes 638984 | tf_op jit(solution)/shard_map/ppermute | solution.py:279
  44.1 11.0 %collective-permute-start.5 = (bf16[208,512]{1,0:T(8,128)(2,1)S(1)}, bf16[208,512]{1,0:T(8,128)(2,1)S(1)}, u32[]{:S(2)}, u32[]{:S(2)}) collective-permute-start(bf16[208,512]{1,0:T(8,128)(2,1)S(1)} %slice.17), channel_id=1, source_target_pairs={{0,48},{16,0},{32,16},{48,32},{1,49},{17,1},{33,17},{49,33},{2,50}... | collective-permute-start | bytes 638984 | tf_op jit(solution)/shard_map/ppermute | solution.py:275
  47.0 8.1 %collective-permute-start.2 = (bf16[192,512]{1,0:T(8,128)(2,1)S(1)}, bf16[192,512]{1,0:T(8,128)(2,1)S(1)}, u32[]{:S(2)}, u32[]{:S(2)}) collective-permute-start(bf16[192,512]{1,0:T(8,128)(2,1)S(1)} %slice.16), channel_id=1, source_target_pairs={{0,16},{16,32},{32,48},{48,0},{1,17},{17,33},{33,49},{49,1},{2,18}... | collective-permute-start | bytes 589832 | tf_op jit(solution)/shard_map/ppermute | solution.py:275
  47.0 8.7 %copy-start.8 = (bf16[192,512]{1,0:T(8,128)(2,1)S(1)}, bf16[192,512]{1,0:T(8,128)(2,1)}, u32[]{:S(2)}) copy-start(bf16[192,512]{1,0:T(8,128)(2,1)} %copy-done.7) | copy-start | bytes 589828
  47.0 8.7 %copy-start.10 = (bf16[192,512]{1,0:T(8,128)(2,1)S(1)}, bf16[192,512]{1,0:T(8,128)(2,1)}, u32[]{:S(2)}) copy-start(bf16[192,512]{1,0:T(8,128)(2,1)} %copy-done.9) | copy-start | bytes 589828
  55.1 5.4 %collective-permute-start.3 = (bf16[192,512]{1,0:T(8,128)(2,1)S(1)}, bf16[192,512]{1,0:T(8,128)(2,1)S(1)}, u32[]{:S(2)}, u32[]{:S(2)}) collective-permute-start(bf16[192,512]{1,0:T(8,128)(2,1)S(1)} %collective-permute-done.2.refs_0_), channel_id=1, source_target_pairs={{0,8},{8,0},{1,9},{9,1},{2,10},{10,2},{3,11},{11,3},{4,12},{12,4},... | collective-permute-start | bytes 589832 | tf_op jit(solution)/shard_map/ppermute | solution.py:279
  55.1 5.4 %collective-permute-start.6 = (bf16[208,512]{1,0:T(8,128)(2,1)S(1)}, bf16[208,512]{1,0:T(8,128)(2,1)S(1)}, u32[]{:S(2)}, u32[]{:S(2)}) collective-permute-start(bf16[208,512]{1,0:T(8,128)(2,1)S(1)} %collective-permute-done.5.refs_2_), channel_id=1, source_target_pairs={{0,8},{8,0},{1,9},{9,1},{2,10},{10,2},{3,11},{11,3},{4,12},{12,4},... | collective-permute-start | bytes 638984 | tf_op jit(solution)/shard_map/ppermute | solution.py:279
  63.0 3.7 %collective-permute-start.19 = (f32[1,3,128]{2,1,0:T(4,128)S(1)}, f32[1,3,128]{2,1,0:T(4,128)S(1)}, u32[]{:S(2)}, u32[]{:S(2)}) collective-permute-start(f32[1,3,128]{2,1,0:T(4,128)S(1)} %get-tuple-element.36), channel_id=1, source_target_pairs={{0,1},{1,0},{2,3},{3,2},{4,5},{5,4},{6,7},{7,6},{8,9},{9,8},{10,11... | collective-permute-start | bytes 4616 | tf_op jit(solution)/shard_map/ppermute | solution.py:339
  66.6 3.6 %collective-permute-start.20 = (f32[2,3,128]{2,1,0:T(4,128)S(1)}, f32[2,3,128]{2,1,0:T(4,128)S(1)}, u32[]{:S(2)}, u32[]{:S(2)}) collective-permute-start(f32[2,3,128]{2,1,0:T(4,128)S(1)} %pad_maximum_fusion.3), channel_id=1, source_target_pairs={{0,2},{2,0},{4,6},{6,4},{1,3},{3,1},{5,7},{7,5},{8,10},{10,8},{12,... | collective-permute-start | bytes 9224 | tf_op jit(solution)/shard_map/ppermute | solution.py:339
  70.2 5.5 %collective-permute-start.21 = (f32[4,3,128]{2,1,0:T(4,128)S(1)}, f32[4,3,128]{2,1,0:T(4,128)S(1)}, u32[]{:S(2)}, u32[]{:S(2)}) collective-permute-start(f32[4,3,128]{2,1,0:T(4,128)S(1)} %pad_maximum_fusion.1), channel_id=1, source_target_pairs={{0,4},{2,6},{4,0},{6,2},{1,5},{3,7},{5,1},{7,3},{8,12},{10,14},{12... | collective-permute-start | bytes 18440 | tf_op jit(solution)/shard_map/ppermute | solution.py:339
  75.8 41.2 %copy-start.1 = (bf16[1,8,256,512]{3,2,1,0:T(8,128)(2,1)S(1)}, bf16[1,8,256,512]{3,2,1,0:T(8,128)(2,1)}, u32[]{:S(2)}) copy-start(bf16[1,8,256,512]{3,2,1,0:T(8,128)(2,1)} %interp.1) | copy-start | bytes 6291460

commit v3 on v2

--- a/solution.py
+++ b/solution.py
@@ -216,12 +216,17 @@
             post[:, at] = (e[:, at] * scale).astype(BF16)
         acc[...] = jnp.zeros(acc.shape, F32)
 
-    rows = jnp.dot(post[...], w[step], preferred_element_type=F32).astype(BF16)
-    both = jnp.concatenate([rows[:, :256], rows[:, 256:]], axis=0)
-    ids = jnp.concatenate([seg[pl.ds(2 * step, 1), :], seg[pl.ds(2 * step + 1, 1), :]], axis=1)
-    hot = lax.broadcasted_iota(jnp.int32, (acc.shape[0], ids.shape[1]), 0) == ids
-    hot = jnp.where(hot, 1.0, 0.0).astype(BF16)
-    acc[...] += jnp.dot(hot, both, preferred_element_type=F32)
+    added = None
+    for u in range(2):
+        at = 2 * step + u
+        rows = jnp.dot(post[...], w[at], preferred_element_type=F32).astype(BF16)
+        both = jnp.concatenate([rows[:, :256], rows[:, 256:]], axis=0)
+        ids = jnp.concatenate([seg[pl.ds(2 * at, 1), :], seg[pl.ds(2 * at + 1, 1), :]], axis=1)
+        hot = lax.broadcasted_iota(jnp.int32, (acc.shape[0], ids.shape[1]), 0) == ids
+        hot = jnp.where(hot, 1.0, 0.0).astype(BF16)
+        part = jnp.dot(hot, both, preferred_element_type=F32)
+        added = part if added is None else added + part
+    acc[...] += added
 
     @pl.when(step == pl.num_programs(0) - 1)
     def _():
@@ -233,7 +238,7 @@
     vmem = pl.BlockSpec(memory_space=pltpu.VMEM)
     return pl.pallas_call(
         gather_kernel,
-        grid=(weighted.shape[0],),
+        grid=(weighted.shape[0] // 2,),
         in_specs=[pl.BlockSpec(memory_space=pltpu.SMEM)] + [vmem] * 4,
         out_specs=[vmem] * 3,
         out_shape=[
@@ -295,27 +300,6 @@
     )
     mine = jnp.concatenate([refs, tags], axis=0)
 
-    across = flipped(mine, "xh")
-    left = shifted(mine, "y", 1)
-    right = shifted(mine, "y", -1)
-    far_low = shifted(left[:192], "y", 1)
-    far_high = shifted(right[192:], "y", -1)
-    aleft = shifted(across, "y", 1)
-    aright = shifted(across, "y", -1)
-    afar_low = shifted(aleft[:192], "y", 1)
-    afar_high = shifted(aright[192:], "y", -1)
-    rounds = [
-        [(mine, 0, 384, (0, 0))],
-        [(left, 0, 384, (0, -1)), (right, 0, 384, (0, 1)), (across, 0, 384, (1, 0))],
-        [
-            (far_low, 0, 192, (0, 2)),
-            (far_high, 192, 192, (0, 2)),
-            (aleft, 0, 384, (1, -1)),
-            (aright, 0, 384, (1, 1)),
-        ],
-        [(afar_low, 0, 192, (1, 2)), (afar_high, 192, 192, (1, 2))],
-    ]
-
     noise = noise_weight.reshape(16, 1, SLICE)
     by_block = noise_weight.reshape(1, NBLK, 2, BLOCK)
     angles = shift_phase.reshape(TRANS, NBLK, 1, BLOCK)
@@ -325,14 +309,40 @@
     pose = lax.axis_index(POSE)
     where = jnp.stack([xh, y, c, pose, lax.axis_index(IMG_POSE)]).astype(jnp.int32)
     where, cos = lax.optimization_barrier((where, cos))
+
+    def swapped(piece):
+        return flipped(piece, "c")
+
+    near = swapped(mine)
+    left = shifted(mine, "y", 1)
+    right = shifted(mine, "y", -1)
+    across = flipped(mine, "xh")
     weighted = weight_rows(images, cos, sin)
-
-    paired = [[(p[0], flipped(p[0], "c"), *p[1:]) for p in turn] for turn in rounds]
-
-    carried = None
-    for j, pairs in enumerate(paired):
-        carried = scores_call(pairs, where, weighted, noise, carried, j == len(paired) - 1)
-    marks, e, pieces = carried
+    one = scores_call([(mine, near, 0, 384, (0, 0))], where, weighted, noise, None, False)
+    left, weighted = lax.optimization_barrier((left, weighted))
+    aleft = flipped(left, "xh")
+    far = shifted(left, "y", 1)
+    aright = shifted(across, "y", -1)
+
+    def pair(piece, flips):
+        return (piece, swapped(piece), 0, 384, flips)
+
+    two = scores_call(
+        [pair(left, (0, -1)), pair(right, (0, 1)), pair(across, (1, 0))],
+        where, weighted, noise, one, False,
+    )
+    aleft, two = lax.optimization_barrier((aleft, two))
+    alow = shifted(aleft[:256], "y", 1)
+    ahigh = shifted(aright[256:], "y", -1)
+    three = scores_call(
+        [pair(far, (0, 2)), pair(aleft, (1, -1))],
+        where, weighted, noise, two, False,
+    )
+    four = scores_call([pair(aright, (1, 1))], where, weighted, noise, three, False)
+    alow, ahigh, four = lax.optimization_barrier((alow, ahigh, four))
+    low = (alow, swapped(alow), 0, 256, (1, 2))
+    high = (ahigh, swapped(ahigh), 256, 128, (1, 2))
+    marks, e, pieces = scores_call([low, high], where, weighted, noise, four, True)
 
     for axis, bit in (("xl", 1), ("z", 1), ("z", 2)):
         size = lax.axis_size(axis)

time: 119 us -> 101 us (0.85)
  waiting for transfers between devices: 25.8 us -> 16 us
  Pallas kernels: 40 us -> 35.6 us
  local copies, waits for them, and re-layouts: 3.66 us -> 1.71 us
  starting transfers between devices: 24.2 us -> 22.8 us
    ppermute x8 -> x6, waiting for transfers between devices: 20.5 us -> 5.22 us  [shifted(): return lax.ppermute(x, axis, [(i, (i + by) % size) for i in range(size)])]
    ppermute x11, waiting for transfers between devices: 0.23 us -> 4.8 us  [flipped(): return lax.ppermute(x, axis, [(0, 1), (1, 0)])]
    pallas_call x1, Pallas kernels: 19.9 us -> 16.7 us  [gather_call(): pl.pallas_call(gather_kernel, grid=(weighted.shape[0] // 2,), in_specs=[p...]
    slice x4 -> x2, local copies, waits for them, and re-layouts: 2.84 us -> 0.03 us  [the longest x1 0.02 us: body(): alow = shifted(aleft[:256], 'y', 1)]
    ppermute x8 -> x6, starting transfers between devices: 11.5 us -> 10 us  [shifted(): return lax.ppermute(x, axis, [(i, (i + by) % size) for i in range(size)])]
    pallas_call x4 -> x5, Pallas kernels: 13.7 us -> 12.6 us  [scores_call(): pl.pallas_call(kernel, in_specs=in_specs, out_specs=[vmem] * len(out_shap...]
  transfers between devices with their start and end apart: 22 -> 20, of which waited for: 8 -> 11; matrix products, arithmetic and copies ran while one was open for 3% -> 2% of each run, Pallas kernels for 13% -> 15%
where the time goes in v3:
time: 101 us
  Pallas kernels  35.6 us (35%)
  starting transfers between devices  22.8 us (23%)
  blocking collectives  21.2 us (21%)
  waiting for transfers between devices  16 us (16%)
  other arithmetic  2.98 us (3%)
  local copies, waits for them, and re-layouts  1.71 us (2%)
    all_to_all x1, blocking collectives, body(): lax.all_to_all(gathered.reshape(BRICKS, STENCILS, 2 * BLOCK), IMG_POSE, 0...  21.2 us
    pallas_call x1, Pallas kernels, gather_call(): pl.pallas_call(gather_kernel, grid=(weighted.shape[0] // 2,), in_specs=[p...  16.7 us
    pallas_call x5, Pallas kernels, scores_call(): pl.pallas_call(kernel, in_specs=in_specs, out_specs=[vmem] * len(out_shap...  12.6 us
    ppermute x6, starting transfers between devices, shifted(): return lax.ppermute(x, axis, [(i, (i + by) % size) for i in range(size)])  10 us
    ppermute x3, starting transfers between devices, body(): other = lax.ppermute(pieces, axis, [(i, i ^ bit) for i in range(size)])  6.47 us
    ppermute x11, starting transfers between devices, flipped(): return lax.ppermute(x, axis, [(0, 1), (1, 0)])  6.35 us
    ppermute x3, waiting for transfers between devices, body(): other = lax.ppermute(pieces, axis, [(i, i ^ bit) for i in range(size)])  6.01 us
    ppermute x6, waiting for transfers between devices, shifted(): return lax.ppermute(x, axis, [(i, (i + by) % size) for i in range(size)])  5.22 us
  transfers between devices with their start and end apart: 20, of which 11 were waited for; matrix products, arithmetic and copies ran while one was open for 2% of the time, Pallas kernels for 15%

profile of v3, /device:TPU:0, one launch (start us, length us, event | category | flops | bytes accessed | tf_op | source)
XLA Modules:
  0.0 101.2 jit_solution(11426273956225956955)
XLA Ops:
  0.6 0.0 copy-start.3
  0.7 0.7 reduce
  1.4 0.2 convert_reduce_fusion
  1.6 0.7 convert.7
  2.3 0.1 pad.17.clone
  2.4 1.3 %fusion.3.refs_0_ = bf16[400,512]{1,0:T(8,128)(2,1)S(1)} fusion(bf16[1,128]{1,0:T(2,128)(2,1)S(1)} %bitcast.27, bf16[3,512]{1,0:T(4,128)(2,1)S(1)} %convert_element_type.24, bf16[384,512]{1,0:T(8,128)(2,1)} %param.11, bf16[400]{0:T(512)(128)(2,1)S(1)} %pad.17.clone), kind=kLoop, calls=%fused_computation.5 | loop fusion | flops 2457600 | bytes 806944 | tf_op jit(solution)/shard_map/concatenate | solution.py:301
  3.7 0.1 collective-permute-start.7
  3.8 1.8 %collective-permute-start = (bf16[400,512]{1,0:T(8,128)(2,1)S(1)}, bf16[400,512]{1,0:T(8,128)(2,1)}, u32[]{:S(2)}, u32[]{:S(2)}) collective-permute-start(bf16[400,512]{1,0:T(8,128)(2,1)S(1)} %fusion.3.refs_0_), channel_id=1, source_target_pairs={{0,16},{16,32},{32,48},{48,0},{1,17},{17,33},{33,49},{49,1},{2,18}... | collective-permute-start | bytes 1228808 | tf_op jit(solution)/shard_map/ppermute | solution.py:280
  5.5 3.0 %collective-permute-start.5 = (bf16[400,512]{1,0:T(8,128)(2,1)S(1)}, bf16[400,512]{1,0:T(8,128)(2,1)}, u32[]{:S(2)}, u32[]{:S(2)}) collective-permute-start(bf16[400,512]{1,0:T(8,128)(2,1)S(1)} %fusion.3.refs_0_), channel_id=1, source_target_pairs={{0,64},{64,0},{1,65},{65,1},{2,66},{66,2},{3,67},{67,3},{4,68},{68... | collective-permute-start | bytes 1228808 | tf_op jit(solution)/shard_map/ppermute | solution.py:284
  8.5 1.7 %collective-permute-start.3 = (bf16[400,512]{1,0:T(8,128)(2,1)S(1)}, bf16[400,512]{1,0:T(8,128)(2,1)}, u32[]{:S(2)}, u32[]{:S(2)}) collective-permute-start(bf16[400,512]{1,0:T(8,128)(2,1)S(1)} %fusion.3.refs_0_), channel_id=1, source_target_pairs={{0,48},{16,0},{32,16},{48,32},{1,49},{17,1},{33,17},{49,33},{2,50}... | collective-permute-start | bytes 1228808 | tf_op jit(solution)/shard_map/ppermute | solution.py:280
  10.2 1.4 %sine_bitcast_fusion = (f32[8,32,128]{2,0,1:T(8,128)S(1)}, f32[8,32,128]{2,0,1:T(8,128)S(1)}) fusion(f32[8,4096]{1,0:T(8,128)} %param.9), kind=kLoop, calls=%fused_computation.9 | loop fusion | bytes 393216 | tf_op jit(solution)/shard_map/sin | solution.py:308
  11.6 0.1 mul.67
  11.7 0.1 multiply_multiply_fusion
  11.8 0.1 stack.23.pos
  11.9 4.3 %weigh.1.refs_2_.refs_6_.refs_4_.w = bf16[16,1024,512]{2,1,0:T(8,128)(2,1)S(1)} custom-call(bf16[128,8192]{1,0:T(8,128)(2,1)S(1)} %copy-done, f32[8,8192]{1,0:T(8,128)S(1)} %get-tuple-element.40.cos, f32[8,8192]{1,0:T(8,128)S(1)} %get-tuple-element.78.sin), custom_call_target="tpu_custom_call" | custom-call | bytes 16777216 | tf_op jit(solution)/shard_map/weigh/pallas_call | solution.py:49
  16.2 0.9 collective-permute-done.refs_0_
  17.1 0.0 collective-permute-start.2
  17.1 1.5 %collective-permute-done.5.refs_4_ = bf16[400,512]{1,0:T(8,128)(2,1)} collective-permute-done((bf16[400,512]{1,0:T(8,128)(2,1)S(1)}, bf16[400,512]{1,0:T(8,128)(2,1)}, u32[]{:S(2)}, u32[]{:S(2)}) %collective-permute-start.5) | collective-permute-done | bytes 409632 | tf_op jit(solution)/shard_map/ppermute | solution.py:284
  18.7 0.0 collective-permute-start.6
  18.7 1.2 %collective-permute-done.3.refs_2_ = bf16[400,512]{1,0:T(8,128)(2,1)} collective-permute-done((bf16[400,512]{1,0:T(8,128)(2,1)S(1)}, bf16[400,512]{1,0:T(8,128)(2,1)}, u32[]{:S(2)}, u32[]{:S(2)}) %collective-permute-start.3) | collective-permute-done | bytes 409632 | tf_op jit(solution)/shard_map/ppermute | solution.py:280
  19.9 2.3 %collective-permute-start.1 = (bf16[400,512]{1,0:T(8,128)(2,1)}, bf16[400,512]{1,0:T(8,128)(2,1)S(1)}, u32[]{:S(2)}, u32[]{:S(2)}) collective-permute-start(bf16[400,512]{1,0:T(8,128)(2,1)} %collective-permute-done.refs_0_), channel_id=1, source_target_pairs={{0,64},{64,0},{1,65},{65,1},{2,66},{66,2},{3,67},{67,3},{4,68},{68... | collective-permute-start | bytes 1228808 | tf_op jit(solution)/shard_map/ppermute | solution.py:284
  22.2 1.6 %collective-permute-start.12 = (bf16[400,512]{1,0:T(8,128)(2,1)}, bf16[400,512]{1,0:T(8,128)(2,1)S(1)}, u32[]{:S(2)}, u32[]{:S(2)}) collective-permute-start(bf16[400,512]{1,0:T(8,128)(2,1)} %collective-permute-done.refs_0_), channel_id=1, source_target_pairs={{0,16},{16,32},{32,48},{48,0},{1,17},{17,33},{33,49},{49,1},{2,18}... | collective-permute-start | bytes 1228808 | tf_op jit(solution)/shard_map/ppermute | solution.py:280
  23.8 1.7 %collective-permute-start.9 = (bf16[400,512]{1,0:T(8,128)(2,1)}, bf16[400,512]{1,0:T(8,128)(2,1)S(1)}, u32[]{:S(2)}, u32[]{:S(2)}) collective-permute-start(bf16[400,512]{1,0:T(8,128)(2,1)} %collective-permute-done.5.refs_4_), channel_id=1, source_target_pairs={{0,48},{16,0},{32,16},{48,32},{1,49},{17,1},{33,17},{49,33},{2,50}... | collective-permute-start | bytes 1228808 | tf_op jit(solution)/shard_map/ppermute | solution.py:280
  25.4 1.6 %scores.5 = (f32[384,1024]{1,0:T(8,128)S(1)}, f32[384,128]{1,0:T(8,128)S(1)}, f32[1,128]{1,0:T(1,128)S(1)}, f32[12,16,128]{2,1,0:T(8,128)S(1)}) custom-call(s32[5]{0:T(128)S(1)} %stack.23.pos, bf16[400,512]{1,0:T(8,128)(2,1)S(1)} %fusion.3.refs_0_, bf16[400,512]{1,0:T(8,128)(2,1)S(1)} %collective-permute-done.7.refs_1_, ...), custom_call_target="tpu_custom_call" | custom-call | flops 805306368 | bytes 1048576 | tf_op jit(solution)/shard_map/scores/pallas_call | solution.py:154
  27.0 4.4 %scores.6 = (f32[384,1024]{1,0:T(8,128)S(1)}, f32[384,128]{1,0:T(8,128)S(1)}, f32[1,128]{1,0:T(1,128)S(1)}, f32[12,16,128]{2,1,0:T(8,128)S(1)}) custom-call(s32[5]{0:T(128)S(1)} %stack.23.pos, bf16[400,512]{1,0:T(8,128)(2,1)} %collective-permute-done.refs_0_, ...), custom_call_target="tpu_custom_call", output_to_operand_aliasing={{0}: (9, {}), {1}: (10, {}), {2}: (11, {}), {3}: (12, {})} | custom-call | flops 2415919104 | bytes 1048576 | tf_op jit(solution)/shard_map/scores/pallas_call | solution.py:154
  31.5 2.0 %collective-permute-done.1.refs_2_ = bf16[400,512]{1,0:T(8,128)(2,1)S(1)} collective-permute-done((bf16[400,512]{1,0:T(8,128)(2,1)}, bf16[400,512]{1,0:T(8,128)(2,1)S(1)}, u32[]{:S(2)}, u32[]{:S(2)}) %collective-permute-start.1) | collective-permute-done | bytes 409632 | tf_op jit(solution)/shard_map/ppermute | solution.py:284
  33.5 1.2 %collective-permute-done.12.refs_0_ = bf16[400,512]{1,0:T(8,128)(2,1)S(1)} collective-permute-done((bf16[400,512]{1,0:T(8,128)(2,1)}, bf16[400,512]{1,0:T(8,128)(2,1)S(1)}, u32[]{:S(2)}, u32[]{:S(2)}) %collective-permute-start.12) | collective-permute-done | bytes 409632 | tf_op jit(solution)/shard_map/ppermute | solution.py:280
  34.7 0.1 collective-permute-done.9.refs_0_
  34.8 0.4 collective-permute-start.11
  35.2 0.9 collective-permute-start.8
  36.2 2.4 %collective-permute-start.10 = (bf16[144,512]{1,0:T(8,128)(2,1)S(1)}, bf16[144,512]{1,0:T(8,128)(2,1)S(1)}, u32[]{:S(2)}, u32[]{:S(2)}) collective-permute-start(bf16[144,512]{1,0:T(8,128)(2,1)S(1)} %slice.8), channel_id=1, source_target_pairs={{0,48},{16,0},{32,16},{48,32},{1,49},{17,1},{33,17},{49,33},{2,50}... | collective-permute-start | bytes 442376 | tf_op jit(solution)/shard_map/ppermute | solution.py:280
  38.6 2.7 %scores.7 = (f32[384,1024]{1,0:T(8,128)S(1)}, f32[384,128]{1,0:T(8,128)S(1)}, f32[1,128]{1,0:T(1,128)S(1)}, f32[12,16,128]{2,1,0:T(8,128)S(1)}) custom-call(s32[5]{0:T(128)S(1)} %stack.23.pos, bf16[400,512]{1,0:T(8,128)(2,1)S(1)} %collective-permute-done.12.refs_0_, ...), custom_call_target="tpu_custom_call", output_to_operand_aliasing={{0}: (7, {}), {1}: (8, {}), {2}: (9, {}), {3}: (10, {})} | custom-call | flops 1610612736 | bytes 1048576 | tf_op jit(solution)/shard_map/scores/pallas_call | solution.py:154
  41.4 1.6 %scores.8 = (f32[384,1024]{1,0:T(8,128)S(1)}, f32[384,128]{1,0:T(8,128)S(1)}, f32[1,128]{1,0:T(1,128)S(1)}, f32[12,16,128]{2,1,0:T(8,128)S(1)}) custom-call(s32[5]{0:T(128)S(1)} %stack.23.pos, bf16[400,512]{1,0:T(8,128)(2,1)S(1)} %collective-permute-done.9.refs_0_, ...), custom_call_target="tpu_custom_call", output_to_operand_aliasing={{0}: (5, {}), {1}: (6, {}), {2}: (7, {}), {3}: (8, {})} | custom-call | flops 805306368 | bytes 1048576 | tf_op jit(solution)/shard_map/scores/pallas_call | solution.py:154
  43.0 1.8 %collective-permute-done.8.refs_0_ = bf16[256,512]{1,0:T(8,128)(2,1)S(1)} collective-permute-done((bf16[256,512]{1,0:T(8,128)(2,1)S(1)}, bf16[256,512]{1,0:T(8,128)(2,1)S(1)}, u32[]{:S(2)}, u32[]{:S(2)}) %collective-permute-start.8) | collective-permute-done | bytes 262176 | tf_op jit(solution)/shard_map/ppermute | solution.py:280
  44.8 0.0 collective-permute-start.15
  44.8 0.5 collective-permute-start.16
  45.3 1.2 %collective-permute-done.16.refs_3_ = bf16[144,512]{1,0:T(8,128)(2,1)S(1)} collective-permute-done((bf16[144,512]{1,0:T(8,128)(2,1)S(1)}, bf16[144,512]{1,0:T(8,128)(2,1)S(1)}, u32[]{:S(2)}, u32[]{:S(2)}) %collective-permute-start.16) | collective-permute-done | bytes 147488 | tf_op jit(solution)/shard_map/ppermute | solution.py:284
  46.6 2.3 %scores.9 = (f32[12,16,128]{2,1,0:T(8,128)S(1)}, f32[384,1024]{1,0:T(8,128)S(1)}, f32[1,3,128]{2,1,0:T(4,128)S(1)}) custom-call(s32[5]{0:T(128)S(1)} %stack.23.pos, bf16[256,512]{1,0:T(8,128)(2,1)S(1)} %collective-permute-done.8.refs_0_, bf16[256,512]{1,0:T(8,128)(2,1)S(1)} %collective-permute-done.15.refs_1_, ...), custom_call_target="tpu_custom_call", output_to_operand_aliasing={{0}: (10, {})} | custom-call | flops 805306368 | bytes 1048576 | tf_op jit(solution)/shard_map/scores/pallas_call | solution.py:154
  48.8 0.7 collective-permute-start.17
  49.5 3.0 %collective-permute-done.17 = f32[1,3,128]{2,1,0:T(4,128)S(1)} collective-permute-done((f32[1,3,128]{2,1,0:T(4,128)S(1)}, f32[1,3,128]{2,1,0:T(4,128)S(1)}, u32[]{:S(2)}, u32[]{:S(2)}) %collective-permute-start.17) | collective-permute-done | bytes 1568 | tf_op jit(solution)/shard_map/ppermute | solution.py:349
  52.5 1.9 %collective-permute-start.18 = (f32[2,3,128]{2,1,0:T(4,128)S(1)}, f32[2,3,128]{2,1,0:T(4,128)S(1)}, u32[]{:S(2)}, u32[]{:S(2)}) collective-permute-start(f32[2,3,128]{2,1,0:T(4,128)S(1)} %pad_maximum_fusion.3), channel_id=1, source_target_pairs={{0,2},{2,0},{4,6},{6,4},{1,3},{3,1},{5,7},{7,5},{8,10},{10,8},{12,... | collective-permute-start | bytes 9224 | tf_op jit(solution)/shard_map/ppermute | solution.py:349
  54.4 1.7 %collective-permute-done.18 = f32[2,3,128]{2,1,0:T(4,128)S(1)} collective-permute-done((f32[2,3,128]{2,1,0:T(4,128)S(1)}, f32[2,3,128]{2,1,0:T(4,128)S(1)}, u32[]{:S(2)}, u32[]{:S(2)}) %collective-permute-start.18) | collective-permute-done | bytes 3104 | tf_op jit(solution)/shard_map/ppermute | solution.py:349
  56.1 3.9 %collective-permute-start.19 = (f32[4,3,128]{2,1,0:T(4,128)S(1)}, f32[4,3,128]{2,1,0:T(4,128)S(1)}, u32[]{:S(2)}, u32[]{:S(2)}) collective-permute-start(f32[4,3,128]{2,1,0:T(4,128)S(1)} %pad_maximum_fusion.1), channel_id=1, source_target_pairs={{0,4},{2,6},{4,0},{6,2},{1,5},{3,7},{5,1},{7,3},{8,12},{10,14},{12... | collective-permute-start | bytes 18440 | tf_op jit(solution)/shard_map/ppermute | solution.py:349
  60.0 0.3 route.1.seg
  60.3 1.3 %collective-permute-done.19 = f32[4,3,128]{2,1,0:T(4,128)S(1)} collective-permute-done((f32[4,3,128]{2,1,0:T(4,128)S(1)}, f32[4,3,128]{2,1,0:T(4,128)S(1)}, u32[]{:S(2)}, u32[]{:S(2)}) %collective-permute-start.19) | collective-permute-done | bytes 6176 | tf_op jit(solution)/shard_map/ppermute | solution.py:349
  61.6 16.7 %gather.1 = (bf16[1024,256]{1,0:T(8,128)(2,1)S(1)}, f32[1,128]{1,0:T(1,128)}, f32[1,1]{1,0:T(1,128)}) custom-call(s32[5]{0:T(128)S(1)} %stack.23.pos, f32[8,3,128]{2,1,0:T(4,128)S(1)} %pad_maximum_fusion.pieces, f32[384,1024]{1,0:T(8,128)S(1)} %get-tuple-element.71.e, bf16[16,1024,512]{2,1,0:T(8,128)(2,1)S(1)} %weigh.1.refs_2_.refs_6_.refs_4_.w, ...), custom_call_target="tpu_custom_call" | custom-call | tf_op jit(solution)/shard_map/gather/pallas_call | solution.py:239
  78.3 21.2 %all_to_all.5.got = bf16[128,8,256]{2,1,0:T(8,128)(2,1)S(1)} all-to-all(bf16[128,8,256]{2,1,0:T(8,128)(2,1)S(1)} %bitcast.23), channel_id=1, replica_groups=mesh['xh'=2,'y'=4,'c'=2,'z'=4,'xl'=2] {'xh','y','c','z','xl'}, dimensions={0} | all-to-all | bytes 1048576 | tf_op jit(solution)/shard_map/all_to_all | solution.py:353
  99.5 1.7 %volume.1 = f32[1,512]{1,0:T(1,128)} custom-call(bf16[128,8,256]{2,1,0:T(8,128)(2,1)S(1)} %all_to_all.5.got, bf16[1,8,256,512]{3,2,1,0:T(8,128)(2,1)S(1)} %copy-done.1, f32[1,1]{1,0:T(1,128)} %get-tuple-element.74.count), custom_call_target="tpu_custom_call" | custom-call | tf_op jit(solution)/shard_map/volume/pallas_call | solution.py:270
  (30 shorter events, 0.2 us)
Async XLA Ops:
  0.6 11.0 %copy-start.3 = (f32[2]{0:T(128)S(1)}, f32[2]{0:T(128)}, u32[]{:S(2)}) copy-start(f32[2]{0:T(128)} %constant.35.clone) | copy-start | bytes 28
  0.6 11.1 %copy-start.2 = (f32[8192]{0:T(1024)S(1)}, f32[8192]{0:T(1024)}, u32[]{:S(2)}) copy-start(f32[8192]{0:T(1024)} %param.10) | copy-start | bytes 98308
  2.4 9.5 %copy-start = (bf16[128,8192]{1,0:T(8,128)(2,1)S(1)}, bf16[128,8192]{1,0:T(8,128)(2,1)}, u32[]{:S(2)}) copy-start(bf16[128,8192]{1,0:T(8,128)(2,1)} %img.1) | copy-start | bytes 6291460
  3.7 18.5 %collective-permute-start.7 = (bf16[400,512]{1,0:T(8,128)(2,1)S(1)}, bf16[400,512]{1,0:T(8,128)(2,1)S(1)}, u32[]{:S(2)}, u32[]{:S(2)}) collective-permute-start(bf16[400,512]{1,0:T(8,128)(2,1)S(1)} %fusion.3.refs_0_), channel_id=1, source_target_pairs={{0,8},{8,0},{1,9},{9,1},{2,10},{10,2},{3,11},{11,3},{4,12},{12,4},... | collective-permute-start | bytes 1228808 | tf_op jit(solution)/shard_map/ppermute | solution.py:284
  3.8 13.4 %collective-permute-start = (bf16[400,512]{1,0:T(8,128)(2,1)S(1)}, bf16[400,512]{1,0:T(8,128)(2,1)}, u32[]{:S(2)}, u32[]{:S(2)}) collective-permute-start(bf16[400,512]{1,0:T(8,128)(2,1)S(1)} %fusion.3.refs_0_), channel_id=1, source_target_pairs={{0,16},{16,32},{32,48},{48,0},{1,17},{17,33},{33,49},{49,1},{2,18}... | collective-permute-start | bytes 1228808 | tf_op jit(solution)/shard_map/ppermute | solution.py:280
  5.5 13.1 %collective-permute-start.5 = (bf16[400,512]{1,0:T(8,128)(2,1)S(1)}, bf16[400,512]{1,0:T(8,128)(2,1)}, u32[]{:S(2)}, u32[]{:S(2)}) collective-permute-start(bf16[400,512]{1,0:T(8,128)(2,1)S(1)} %fusion.3.refs_0_), channel_id=1, source_target_pairs={{0,64},{64,0},{1,65},{65,1},{2,66},{66,2},{3,67},{67,3},{4,68},{68... | collective-permute-start | bytes 1228808 | tf_op jit(solution)/shard_map/ppermute | solution.py:284
  8.5 11.3 %collective-permute-start.3 = (bf16[400,512]{1,0:T(8,128)(2,1)S(1)}, bf16[400,512]{1,0:T(8,128)(2,1)}, u32[]{:S(2)}, u32[]{:S(2)}) collective-permute-start(bf16[400,512]{1,0:T(8,128)(2,1)S(1)} %fusion.3.refs_0_), channel_id=1, source_target_pairs={{0,48},{16,0},{32,16},{48,32},{1,49},{17,1},{33,17},{49,33},{2,50}... | collective-permute-start | bytes 1228808 | tf_op jit(solution)/shard_map/ppermute | solution.py:280
  17.1 6.7 %collective-permute-start.2 = (bf16[400,512]{1,0:T(8,128)(2,1)}, bf16[400,512]{1,0:T(8,128)(2,1)S(1)}, u32[]{:S(2)}, u32[]{:S(2)}) collective-permute-start(bf16[400,512]{1,0:T(8,128)(2,1)} %collective-permute-done.refs_0_), channel_id=1, source_target_pairs={{0,8},{8,0},{1,9},{9,1},{2,10},{10,2},{3,11},{11,3},{4,12},{12,4},... | collective-permute-start | bytes 1228808 | tf_op jit(solution)/shard_map/ppermute | solution.py:284
  18.7 8.3 %collective-permute-start.6 = (bf16[400,512]{1,0:T(8,128)(2,1)}, bf16[400,512]{1,0:T(8,128)(2,1)S(1)}, u32[]{:S(2)}, u32[]{:S(2)}) collective-permute-start(bf16[400,512]{1,0:T(8,128)(2,1)} %collective-permute-done.5.refs_4_), channel_id=1, source_target_pairs={{0,8},{8,0},{1,9},{9,1},{2,10},{10,2},{3,11},{11,3},{4,12},{12,4},... | collective-permute-start | bytes 1228808 | tf_op jit(solution)/shard_map/ppermute | solution.py:284
  19.9 7.1 %collective-permute-start.4 = (bf16[400,512]{1,0:T(8,128)(2,1)}, bf16[400,512]{1,0:T(8,128)(2,1)S(1)}, u32[]{:S(2)}, u32[]{:S(2)}) collective-permute-start(bf16[400,512]{1,0:T(8,128)(2,1)} %collective-permute-done.3.refs_2_), channel_id=1, source_target_pairs={{0,8},{8,0},{1,9},{9,1},{2,10},{10,2},{3,11},{11,3},{4,12},{12,4},... | collective-permute-start | bytes 1228808 | tf_op jit(solution)/shard_map/ppermute | solution.py:284
  19.9 13.6 %collective-permute-start.1 = (bf16[400,512]{1,0:T(8,128)(2,1)}, bf16[400,512]{1,0:T(8,128)(2,1)S(1)}, u32[]{:S(2)}, u32[]{:S(2)}) collective-permute-start(bf16[400,512]{1,0:T(8,128)(2,1)} %collective-permute-done.refs_0_), channel_id=1, source_target_pairs={{0,64},{64,0},{1,65},{65,1},{2,66},{66,2},{3,67},{67,3},{4,68},{68... | collective-permute-start | bytes 1228808 | tf_op jit(solution)/shard_map/ppermute | solution.py:284
  22.2 12.5 %collective-permute-start.12 = (bf16[400,512]{1,0:T(8,128)(2,1)}, bf16[400,512]{1,0:T(8,128)(2,1)S(1)}, u32[]{:S(2)}, u32[]{:S(2)}) collective-permute-start(bf16[400,512]{1,0:T(8,128)(2,1)} %collective-permute-done.refs_0_), channel_id=1, source_target_pairs={{0,16},{16,32},{32,48},{48,0},{1,17},{17,33},{33,49},{49,1},{2,18}... | collective-permute-start | bytes 1228808 | tf_op jit(solution)/shard_map/ppermute | solution.py:280
  23.8 11.0 %collective-permute-start.9 = (bf16[400,512]{1,0:T(8,128)(2,1)}, bf16[400,512]{1,0:T(8,128)(2,1)S(1)}, u32[]{:S(2)}, u32[]{:S(2)}) collective-permute-start(bf16[400,512]{1,0:T(8,128)(2,1)} %collective-permute-done.5.refs_4_), channel_id=1, source_target_pairs={{0,48},{16,0},{32,16},{48,32},{1,49},{17,1},{33,17},{49,33},{2,50}... | collective-permute-start | bytes 1228808 | tf_op jit(solution)/shard_map/ppermute | solution.py:280
  33.5 5.1 %collective-permute-start.14 = (bf16[400,512]{1,0:T(8,128)(2,1)S(1)}, bf16[400,512]{1,0:T(8,128)(2,1)S(1)}, u32[]{:S(2)}, u32[]{:S(2)}) collective-permute-start(bf16[400,512]{1,0:T(8,128)(2,1)S(1)} %collective-permute-done.1.refs_2_), channel_id=1, source_target_pairs={{0,8},{8,0},{1,9},{9,1},{2,10},{10,2},{3,11},{11,3},{4,12},{12,4},... | collective-permute-start | bytes 1228808 | tf_op jit(solution)/shard_map/ppermute | solution.py:284
  34.7 3.9 %collective-permute-start.13 = (bf16[400,512]{1,0:T(8,128)(2,1)S(1)}, bf16[400,512]{1,0:T(8,128)(2,1)S(1)}, u32[]{:S(2)}, u32[]{:S(2)}) collective-permute-start(bf16[400,512]{1,0:T(8,128)(2,1)S(1)} %collective-permute-done.12.refs_0_), channel_id=1, source_target_pairs={{0,8},{8,0},{1,9},{9,1},{2,10},{10,2},{3,11},{11,3},{4,12},{12,4},... | collective-permute-start | bytes 1228808 | tf_op jit(solution)/shard_map/ppermute | solution.py:284
  34.8 6.6 %collective-permute-start.11 = (bf16[400,512]{1,0:T(8,128)(2,1)S(1)}, bf16[400,512]{1,0:T(8,128)(2,1)S(1)}, u32[]{:S(2)}, u32[]{:S(2)}) collective-permute-start(bf16[400,512]{1,0:T(8,128)(2,1)S(1)} %collective-permute-done.9.refs_0_), channel_id=1, source_target_pairs={{0,8},{8,0},{1,9},{9,1},{2,10},{10,2},{3,11},{11,3},{4,12},{12,4},... | collective-permute-start | bytes 1228808 | tf_op jit(solution)/shard_map/ppermute | solution.py:284
  35.2 9.6 %collective-permute-start.8 = (bf16[256,512]{1,0:T(8,128)(2,1)S(1)}, bf16[256,512]{1,0:T(8,128)(2,1)S(1)}, u32[]{:S(2)}, u32[]{:S(2)}) collective-permute-start(bf16[256,512]{1,0:T(8,128)(2,1)S(1)} %slice.6), channel_id=1, source_target_pairs={{0,16},{16,32},{32,48},{48,0},{1,17},{17,33},{33,49},{49,1},{2,18}... | collective-permute-start | bytes 786440 | tf_op jit(solution)/shard_map/ppermute | solution.py:280
  36.2 6.8 %collective-permute-start.10 = (bf16[144,512]{1,0:T(8,128)(2,1)S(1)}, bf16[144,512]{1,0:T(8,128)(2,1)S(1)}, u32[]{:S(2)}, u32[]{:S(2)}) collective-permute-start(bf16[144,512]{1,0:T(8,128)(2,1)S(1)} %slice.8), channel_id=1, source_target_pairs={{0,48},{16,0},{32,16},{48,32},{1,49},{17,1},{33,17},{49,33},{2,50}... | collective-permute-start | bytes 442376 | tf_op jit(solution)/shard_map/ppermute | solution.py:280
  44.8 1.8 %collective-permute-start.15 = (bf16[256,512]{1,0:T(8,128)(2,1)S(1)}, bf16[256,512]{1,0:T(8,128)(2,1)S(1)}, u32[]{:S(2)}, u32[]{:S(2)}) collective-permute-start(bf16[256,512]{1,0:T(8,128)(2,1)S(1)} %collective-permute-done.8.refs_0_), channel_id=1, source_target_pairs={{0,8},{8,0},{1,9},{9,1},{2,10},{10,2},{3,11},{11,3},{4,12},{12,4},... | collective-permute-start | bytes 786440 | tf_op jit(solution)/shard_map/ppermute | solution.py:284
  44.8 1.7 %collective-permute-start.16 = (bf16[144,512]{1,0:T(8,128)(2,1)S(1)}, bf16[144,512]{1,0:T(8,128)(2,1)S(1)}, u32[]{:S(2)}, u32[]{:S(2)}) collective-permute-start(bf16[144,512]{1,0:T(8,128)(2,1)S(1)} %collective-permute-done.10.refs_2_), channel_id=1, source_target_pairs={{0,8},{8,0},{1,9},{9,1},{2,10},{10,2},{3,11},{11,3},{4,12},{12,4},... | collective-permute-start | bytes 442376 | tf_op jit(solution)/shard_map/ppermute | solution.py:284
  48.8 3.7 %collective-permute-start.17 = (f32[1,3,128]{2,1,0:T(4,128)S(1)}, f32[1,3,128]{2,1,0:T(4,128)S(1)}, u32[]{:S(2)}, u32[]{:S(2)}) collective-permute-start(f32[1,3,128]{2,1,0:T(4,128)S(1)} %get-tuple-element.70), channel_id=1, source_target_pairs={{0,1},{1,0},{2,3},{3,2},{4,5},{5,4},{6,7},{7,6},{8,9},{9,8},{10,11... | collective-permute-start | bytes 4616 | tf_op jit(solution)/shard_map/ppermute | solution.py:349
  52.5 3.6 %collective-permute-start.18 = (f32[2,3,128]{2,1,0:T(4,128)S(1)}, f32[2,3,128]{2,1,0:T(4,128)S(1)}, u32[]{:S(2)}, u32[]{:S(2)}) collective-permute-start(f32[2,3,128]{2,1,0:T(4,128)S(1)} %pad_maximum_fusion.3), channel_id=1, source_target_pairs={{0,2},{2,0},{4,6},{6,4},{1,3},{3,1},{5,7},{7,5},{8,10},{10,8},{12,... | collective-permute-start | bytes 9224 | tf_op jit(solution)/shard_map/ppermute | solution.py:349
  56.1 5.5 %collective-permute-start.19 = (f32[4,3,128]{2,1,0:T(4,128)S(1)}, f32[4,3,128]{2,1,0:T(4,128)S(1)}, u32[]{:S(2)}, u32[]{:S(2)}) collective-permute-start(f32[4,3,128]{2,1,0:T(4,128)S(1)} %pad_maximum_fusion.1), channel_id=1, source_target_pairs={{0,4},{2,6},{4,0},{6,2},{1,5},{3,7},{5,1},{7,3},{8,12},{10,14},{12... | collective-permute-start | bytes 18440 | tf_op jit(solution)/shard_map/ppermute | solution.py:349
  61.6 37.9 %copy-start.1 = (bf16[1,8,256,512]{3,2,1,0:T(8,128)(2,1)S(1)}, bf16[1,8,256,512]{3,2,1,0:T(8,128)(2,1)}, u32[]{:S(2)}) copy-start(bf16[1,8,256,512]{3,2,1,0:T(8,128)(2,1)} %interp.1) | copy-start | bytes 6291460

commit v4 on v3

--- a/solution.py
+++ b/solution.py
@@ -22,12 +22,68 @@
 BF16 = jnp.bfloat16
 
 
-LIMIT = pltpu.CompilerParams(vmem_limit_bytes=24 << 20)
-IDS = 16
-
-
-def weight_kernel(img, cos, sin, out):
-    step = pl.program_id(0)
+LIMIT = pltpu.CompilerParams(vmem_limit_bytes=12 << 20)
+IDS = 8
+LOW = 288
+
+
+def slice_kernel(pos, *arrays):
+    sources, out, copied, done = arrays[:4], arrays[4], arrays[5:9], arrays[9]
+    copies = [
+        pltpu.make_async_copy(sources[j], copied[j], done.at[j]) for j in range(4)
+    ]
+    for copy in copies:
+        copy.start()
+    for copy in copies:
+        copy.wait()
+    refs, noise, routing, stencil = copied
+    n = refs.shape[0]
+    out[:n, :] = refs[...]
+    bricks = routing[...].astype(F32)
+    kinds = stencil[...].reshape(1, -1).astype(F32)
+    one = bricks[:, :512]
+    two = jnp.concatenate([bricks[:, 512:], kinds[:, :256]], axis=1)
+    three = kinds[:, 256:]
+    lane = lax.broadcasted_iota(jnp.int32, (BRICKS, 128), 0)
+    hits = jnp.zeros((BRICKS, 128), F32)
+    for u in range(6):
+        hits = hits + jnp.where(lane == routing[:, u * 128 : u * 128 + 128], 1.0, 0.0)
+    counts = jnp.sum(hits.T, axis=0, keepdims=True)
+    chip = pos[0] * 4 + pos[1]
+    wide = refs[...].astype(F32)
+    q = wide * wide * noise[chip * 2 + pos[2]]
+    q = q[:, :128] + q[:, 128:256] + (q[:, 256:384] + q[:, 384:])
+    norm = jnp.concatenate(
+        [jnp.sum(q[j : j + 128, :].T, axis=0, keepdims=True) for j in range(0, n, 128)], axis=1
+    )
+    high = norm.astype(BF16).astype(F32)
+    four = jnp.concatenate([counts, high], axis=1)
+    five = jnp.concatenate([jnp.zeros_like(counts), norm - high], axis=1)
+    rest = jnp.zeros((IDS - 5, SLICE), F32)
+    tags = jnp.concatenate([one, two, three, four, five, rest], axis=0)
+    out[n : n + IDS, :] = tags.astype(BF16)
+
+
+def slice_call(where, refs, noise, routing, stencil):
+    arrays = [
+        pltpu.with_memory_space_constraint(a, pltpu.HBM)
+        for a in (refs, noise, routing, stencil)
+    ]
+    return pl.pallas_call(
+        slice_kernel,
+        in_specs=[pl.BlockSpec(memory_space=pltpu.SMEM)]
+        + [pl.BlockSpec(memory_space=pltpu.HBM)] * 4,
+        out_specs=pl.BlockSpec(memory_space=pltpu.VMEM),
+        scratch_shapes=[pltpu.VMEM(a.shape, a.dtype) for a in arrays]
+        + [pltpu.SemaphoreType.DMA((4,))],
+        out_shape=jax.ShapeDtypeStruct((refs.shape[0] + IDS, SLICE), BF16),
+        compiler_params=LIMIT,
+        name="slice",
+    )(where, *arrays)
+
+
+def weight_kernel(img, cos, sin, out, first=0):
+    step = first + pl.program_id(0)
     n = img.shape[0]
     for p in range(SLICE // 256):
         re_at = slice(p * 256, p * 256 + 128)
@@ -62,57 +118,90 @@
     )(images, cos, sin)
 
 
-def scores_call(pairs, where, weighted, noise, carried, last):
-    count = len(pairs)
-    arrays = [a for pair in pairs for a in pair[:2]]
+def weight_half(where, images, cos, sin, turn, filled=None):
+    n, width = images.shape
+    slices = width // SLICE // 2
+    first = turn * slices // 2
+
+    def kernel(pos, img, cos, sin, *rest):
+        weight_kernel(img, cos, sin, rest[-1], first)
+
+    def at(i, pos):
+        return (0, pos[2] * slices + first + i)
+
+    specs = [
+        pl.BlockSpec((n, SLICE), at),
+        pl.BlockSpec((TRANS, SLICE), at),
+        pl.BlockSpec((TRANS, SLICE), at),
+    ]
+    args = [where, images, cos, sin]
+    vmem = pl.BlockSpec(memory_space=pltpu.VMEM)
+    if filled is not None:
+        specs.append(vmem)
+        args.append(filled)
+    return pl.pallas_call(
+        kernel,
+        grid_spec=pltpu.PrefetchScalarGridSpec(
+            num_scalar_prefetch=1, grid=(slices // 2,), in_specs=specs, out_specs=vmem
+        ),
+        out_shape=pltpu.VMEM((slices, n * TRANS, SLICE), BF16),
+        input_output_aliases={} if filled is None else {4: 0},
+        compiler_params=LIMIT,
+        cost_estimate=pl.CostEstimate(flops=0, bytes_accessed=4 << 20, transcendentals=0),
+        name="weigh_half",
+    )(*args)
+
+
+def scores_call(pairs, where, weighted, carried, last):
+    arrays = [a for pair in pairs for a in pair[:2] if a is not None]
+    count = len(arrays)
     rows = weighted.shape[1]
     imgs = rows // TRANS
     poses = 384
 
     def kernel(pos, *refs):
-        parts = refs[: 2 * count]
-        w, nz = refs[2 * count : 2 * count + 2]
-        rest = refs[2 * count + 2 :]
+        parts = list(refs[:count])
+        w = refs[count]
+        rest = refs[count + 1 :]
         if carried is not None:
             s_in, p_in, n_in = rest[:3]
             rest = rest[4:]
         if last:
-            h_acc, e_out, st_out, s_acc, p_acc = rest
+            h_acc, e_out, st_out, s_acc = rest
         else:
             s_acc, p_acc, n_acc, h_acc = rest
         number = jnp.zeros((1, BRICKS), F32) if carried is None else n_in[...]
-        for j, (_, _, lo, n, (fx, dy)) in enumerate(pairs):
+        norm = jnp.zeros((1, poses), F32) if carried is None else p_in[...]
+        for *both, lo, n, (fx, dy) in pairs:
             chip = jnp.bitwise_xor(pos[0], fx) * 4 + jnp.bitwise_and(pos[1] + dy + 4, 3)
             total = None
-            norm = None
             for side in range(2):
+                if both[side] is None:
+                    continue
+                part = parts.pop(0)
                 at = chip * 2 + jnp.bitwise_xor(pos[2], side)
-                a = parts[2 * j + side][:n, :]
+                a = part[:n, :]
                 if lo + n == poses:
-                    tag = parts[2 * j + side][n : n + IDS, :].astype(F32)
+                    tag = part[n : n + IDS, :].astype(F32)
                     number = number + tag[3:4, :BRICKS]
+                    norm = norm + (tag[3:4, BRICKS:] + tag[4:5, BRICKS:])
                     for u in range(12):
                         lanes = slice(u % 4 * 128, u % 4 * 128 + 128)
                         h_acc[u, pl.ds(at, 1), :] = tag[u // 4 : u // 4 + 1, lanes]
                 d = lax.dot_general(
                     a, w[at], (((1,), (1,)), ((), ())), preferred_element_type=F32
                 )
-                wide = a.astype(F32)
-                q = wide * wide * nz[at]
-                q = q[:, :128] + q[:, 128:256] + (q[:, 256:384] + q[:, 384:])
                 total = d if total is None else total + d
-                norm = q if norm is None else norm + q
             at = slice(lo, lo + n)
             if carried is None:
                 s_acc[at, :] = total
-                p_acc[at, :] = norm
             else:
                 s_acc[at, :] = s_in[at, :] + total
-                p_acc[at, :] = p_in[at, :] + norm
         if not last:
             n_acc[...] = number
+            p_acc[...] = norm
         if last:
-            half = 0.5 * jnp.sum(p_acc[...], axis=1, keepdims=True)
+            half = jnp.broadcast_to(0.5 * norm, (8, poses)).T[:, :1]
             m = None
             for t in range(TRANS):
                 at = slice(t * imgs, (t + 1) * imgs)
@@ -132,9 +221,9 @@
 
     vmem = pl.BlockSpec(memory_space=pltpu.VMEM)
     smem = pl.BlockSpec(memory_space=pltpu.SMEM)
-    in_specs = [smem] + [vmem] * (2 * count + 2)
-    args = [where, *arrays, weighted, noise]
-    acc_shapes = ((poses, rows), (poses, 128), (1, BRICKS), (12, 16, 128))
+    in_specs = [smem] + [vmem] * (count + 1)
+    args = [where, *arrays, weighted]
+    acc_shapes = ((poses, rows), (1, poses), (1, BRICKS), (12, 16, 128))
     alias = {}
     if carried is not None:
         in_specs += [vmem] * 4
@@ -146,7 +235,7 @@
             pltpu.VMEM((poses, rows), F32),
             jax.ShapeDtypeStruct((1, 3, imgs), F32),
         ]
-        scratch = [pltpu.VMEM(s, F32) for s in acc_shapes[:2]]
+        scratch = [pltpu.VMEM(acc_shapes[0], F32)]
     else:
         out_shape = [pltpu.VMEM(s, F32) for s in acc_shapes]
         scratch = []
@@ -192,34 +281,44 @@
     )(h)
 
 
-def gather_kernel(pos, pieces, e, w, seg, g_out, ev_out, num_out, post, acc):
+def gather_kernel(pos, pieces, e, e2, w, w2, seg, g_out, ev_out, num_out, post, post2, acc):
     step = pl.program_id(0)
 
     @pl.when(step == 0)
     def _():
         imgs = pieces.shape[2]
-        group = [pieces[jnp.bitwise_xor(pos[3], j)] for j in range(8)]
-        peak = group[0][0:1, :]
-        for g in group[1:]:
-            peak = jnp.maximum(peak, g[0:1, :])
-        total = jnp.zeros_like(peak)
-        number = jnp.zeros_like(peak)
-        for g in group:
-            total = total + g[1:2, :] * jnp.exp(g[0:1, :] - peak)
-            number = number + g[2:3, :]
-        ev_out[...] = peak + jnp.log(total)
-        here = lax.broadcasted_iota(jnp.int32, number.shape, 1) == pos[4]
-        num_out[...] = jnp.sum(jnp.where(here, number, 0.0), axis=1, keepdims=True)
-        scale = jnp.exp(pieces[0, 0:1, :] - peak) / total
-        for t in range(TRANS):
-            at = slice(t * imgs, (t + 1) * imgs)
-            post[:, at] = (e[:, at] * scale).astype(BF16)
+        for side, (mass, out) in enumerate(((e, post), (e2, post2))):
+            group = []
+            for j in range(8):
+                far = jnp.bitwise_xor(pos[3], j)
+                hops = jnp.right_shift(far, 1)
+                hops = jnp.bitwise_xor(hops, jnp.right_shift(hops, 1))
+                group.append(pieces[hops * 4 + jnp.bitwise_and(far, 1) * 2 + side])
+            peak = group[0][0:1, :]
+            for g in group[1:]:
+                peak = jnp.maximum(peak, g[0:1, :])
+            total = jnp.zeros_like(peak)
+            number = jnp.zeros_like(peak)
+            for g in group:
+                total = total + g[1:2, :] * jnp.exp(g[0:1, :] - peak)
+                number = number + g[2:3, :]
+            if side == 0:
+                ev_out[...] = peak + jnp.log(total)
+                here = lax.broadcasted_iota(jnp.int32, number.shape, 1) == pos[4]
+                num_out[...] = jnp.sum(jnp.where(here, number, 0.0), axis=1, keepdims=True)
+            scale = jnp.exp(pieces[side, 0:1, :] - peak) / total
+            for t in range(TRANS):
+                at = slice(t * imgs, (t + 1) * imgs)
+                out[:, at] = (mass[:, at] * scale).astype(BF16)
         acc[...] = jnp.zeros(acc.shape, F32)
 
     added = None
     for u in range(2):
-        at = 2 * step + u
-        rows = jnp.dot(post[...], w[at], preferred_element_type=F32).astype(BF16)
+        near = 2 * step + u
+        at = pos[2] * w2.shape[0] + near
+        rows = jnp.dot(post[...], w[at], preferred_element_type=F32)
+        rows = rows + jnp.dot(post2[...], w2[near], preferred_element_type=F32)
+        rows = rows.astype(BF16)
         both = jnp.concatenate([rows[:, :256], rows[:, 256:]], axis=0)
         ids = jnp.concatenate([seg[pl.ds(2 * at, 1), :], seg[pl.ds(2 * at + 1, 1), :]], axis=1)
         hot = lax.broadcasted_iota(jnp.int32, (acc.shape[0], ids.shape[1]), 0) == ids
@@ -233,23 +332,27 @@
         g_out[...] = acc[...].astype(BF16)
 
 
-def gather_call(where, pieces, e, weighted, seg):
+def gather_call(where, pieces, e, e2, weighted, half, seg):
     segs = BRICKS * STENCILS
     vmem = pl.BlockSpec(memory_space=pltpu.VMEM)
     return pl.pallas_call(
         gather_kernel,
-        grid=(weighted.shape[0] // 2,),
-        in_specs=[pl.BlockSpec(memory_space=pltpu.SMEM)] + [vmem] * 4,
+        grid=(half.shape[0] // 2,),
+        in_specs=[pl.BlockSpec(memory_space=pltpu.SMEM)] + [vmem] * 6,
         out_specs=[vmem] * 3,
         out_shape=[
             jax.ShapeDtypeStruct((segs, 256), BF16),
             jax.ShapeDtypeStruct((1, pieces.shape[2]), F32),
             jax.ShapeDtypeStruct((1, 1), F32),
         ],
-        scratch_shapes=[pltpu.VMEM(e.shape, BF16), pltpu.VMEM((segs, 256), F32)],
+        scratch_shapes=[
+            pltpu.VMEM(e.shape, BF16),
+            pltpu.VMEM(e.shape, BF16),
+            pltpu.VMEM((segs, 256), F32),
+        ],
         compiler_params=LIMIT,
         name="gather",
-    )(where, pieces, e, weighted, seg)
+    )(where, pieces, e, e2, weighted, half, seg)
 
 
 def volume_kernel(got, interp, count, out):
@@ -287,28 +390,16 @@
 def body(images, shift_phase, noise_weight, refs, routing, stencil, interp):
     xh, y, c = (lax.axis_index(a) for a in IMG)
 
-    tags = jnp.concatenate([routing[:, 0], stencil]).astype(BF16).reshape(3, SLICE)
-    own_counts = jnp.sum(
-        (routing == jnp.arange(BRICKS, dtype=jnp.int32)[None, :]).astype(F32), axis=0, keepdims=True
-    ).astype(BF16)
-    tags = jnp.concatenate(
-        [
-            tags,
-            jnp.pad(own_counts, ((0, 0), (0, SLICE - BRICKS))),
-            jnp.zeros((IDS - 4, SLICE), BF16),
-        ]
-    )
-    mine = jnp.concatenate([refs, tags], axis=0)
-
+    pose = lax.axis_index(POSE)
+    where = jnp.stack([xh, y, c, pose, lax.axis_index(IMG_POSE)]).astype(jnp.int32)
     noise = noise_weight.reshape(16, 1, SLICE)
+    mine = slice_call(where, refs, noise, routing.reshape(1, -1), stencil)
+
     by_block = noise_weight.reshape(1, NBLK, 2, BLOCK)
     angles = shift_phase.reshape(TRANS, NBLK, 1, BLOCK)
     cos = (jnp.cos(angles) * by_block).reshape(TRANS, 2 * PIX)
     sign = jnp.array([1.0, -1.0], F32).reshape(1, 1, 2, 1)
     sin = (jnp.sin(angles) * by_block * sign).reshape(TRANS, 2 * PIX)
-    pose = lax.axis_index(POSE)
-    where = jnp.stack([xh, y, c, pose, lax.axis_index(IMG_POSE)]).astype(jnp.int32)
-    where, cos = lax.optimization_barrier((where, cos))
 
     def swapped(piece):
         return flipped(piece, "c")
@@ -317,8 +408,9 @@
     left = shifted(mine, "y", 1)
     right = shifted(mine, "y", -1)
     across = flipped(mine, "xh")
+    other_images = swapped(images)
     weighted = weight_rows(images, cos, sin)
-    one = scores_call([(mine, near, 0, 384, (0, 0))], where, weighted, noise, None, False)
+    one = scores_call([(mine, near, 0, 384, (0, 0))], where, weighted, None, False)
     left, weighted = lax.optimization_barrier((left, weighted))
     aleft = flipped(left, "xh")
     far = shifted(left, "y", 1)
@@ -329,27 +421,42 @@
 
     two = scores_call(
         [pair(left, (0, -1)), pair(right, (0, 1)), pair(across, (1, 0))],
-        where, weighted, noise, one, False,
+        where, weighted, one, False,
     )
     aleft, two = lax.optimization_barrier((aleft, two))
-    alow = shifted(aleft[:256], "y", 1)
-    ahigh = shifted(aright[256:], "y", -1)
-    three = scores_call(
-        [pair(far, (0, 2)), pair(aleft, (1, -1))],
-        where, weighted, noise, two, False,
-    )
-    four = scores_call([pair(aright, (1, 1))], where, weighted, noise, three, False)
-    alow, ahigh, four = lax.optimization_barrier((alow, ahigh, four))
-    low = (alow, swapped(alow), 0, 256, (1, 2))
-    high = (ahigh, swapped(ahigh), 256, 128, (1, 2))
-    marks, e, pieces = scores_call([low, high], where, weighted, noise, four, True)
-
-    for axis, bit in (("xl", 1), ("z", 1), ("z", 2)):
+    alow = shifted(aleft[:LOW], "y", 1)
+    three = scores_call([pair(aleft, (1, -1))], where, weighted, two, False)
+    aright, three = lax.optimization_barrier((aright, three))
+    ahigh = shifted(aright[LOW:], "y", -1)
+    four = scores_call([pair(far, (0, 2))], where, weighted, three, False)
+    five = scores_call([pair(aright, (1, 1))], where, weighted, four, False)
+    alow, ahigh, five = lax.optimization_barrier((alow, ahigh, five))
+    low, high = swapped(alow), swapped(ahigh)
+    six = scores_call(
+        [(alow, None, 0, LOW, (1, 2)), (ahigh, None, LOW, 384 - LOW, (1, 2))],
+        where, weighted, five, False,
+    )
+    marks, e, pieces = scores_call(
+        [(None, low, 0, LOW, (1, 2)), (None, high, LOW, 384 - LOW, (1, 2))],
+        where, weighted, six, True,
+    )
+
+    other = swapped(pieces)
+    e2 = swapped(e)
+    pieces = jnp.concatenate([pieces, other], axis=0)
+    pieces, other_images = lax.optimization_barrier((pieces, other_images))
+    half = weight_half(where, other_images, cos, sin, 0)
+    for axis, bit in (("xl", 1), ("z", 1), ("z", 3)):
         size = lax.axis_size(axis)
         other = lax.ppermute(pieces, axis, [(i, i ^ bit) for i in range(size)])
         pieces = jnp.concatenate([pieces, other], axis=0)
+        if axis == "xl":
+            pieces, half = lax.optimization_barrier((pieces, half))
+            half = weight_half(where, other_images, cos, sin, 1, half)
+        elif bit == 1:
+            pieces, half = lax.optimization_barrier((pieces, half))
     seg = route_call(marks)
-    gathered, evidence, count = gather_call(where, pieces, e, weighted, seg)
+    gathered, evidence, count = gather_call(where, pieces, e, e2, weighted, half, seg)
     got = lax.all_to_all(
         gathered.reshape(BRICKS, STENCILS, 2 * BLOCK), IMG_POSE, 0, 0, tiled=True
     )

time: 101 us -> 111 us (1.099)
  waiting for transfers between devices: 16 us -> 24.8 us
  other arithmetic: 2.98 us -> 0.08 us
  starting transfers between devices: 22.8 us -> 25.4 us
  Pallas kernels: 35.6 us -> 37.4 us
    ppermute x6, waiting for transfers between devices: 5.22 us -> 13.5 us  [shifted(): return lax.ppermute(x, axis, [(i, (i + by) % size) for i in range(size)])]
    ppermute x11 -> x14, waiting for transfers between devices: 4.8 us -> 8.56 us  [flipped(): return lax.ppermute(x, axis, [(0, 1), (1, 0)])]
    ppermute x3, waiting for transfers between devices: 6.01 us -> 2.77 us  [body(): other = lax.ppermute(pieces, axis, [(i, i ^ bit) for i in range(size)])]
    ppermute x6, starting transfers between devices: 10 us -> 11.8 us  [shifted(): return lax.ppermute(x, axis, [(i, (i + by) % size) for i in range(size)])]
    pallas_call x1 -> x4, Pallas kernels: 16.7 us -> 18 us  [the longest x1 12.7 us: gather_call(): pl.pallas_call(gather_kernel, grid=(half.shape[0] // 2,), in_specs=[pl.Bl...]
    concatenate x2 -> x0, other arithmetic: 1.31 us -> none  [the longest x1 1.3 us: body(): mine = jnp.concatenate([refs, tags], axis=0)]
    ppermute x11 -> x14, starting transfers between devices: 6.35 us -> 7.02 us  [flipped(): return lax.ppermute(x, axis, [(0, 1), (1, 0)])]
    pallas_call x5 -> x7, Pallas kernels: 12.6 us -> 13 us  [scores_call(): pl.pallas_call(kernel, in_specs=in_specs, out_specs=[vmem] * len(out_shap...]
  transfers between devices with their start and end apart: 20 -> 23, of which waited for: 11 -> 9; matrix products, arithmetic and copies ran while one was open for 2% -> 1% of each run, Pallas kernels for 15% -> 19%
where the time goes in v4:
time: 111 us; the launch traced here: 110 us
  Pallas kernels  37.4 us (34%)
  starting transfers between devices  25.4 us (23%)
  waiting for transfers between devices  24.8 us (22%)
  blocking collectives  20.2 us (18%)
  local copies, waits for them, and re-layouts  1.62 us (1%)
    all_to_all x1, blocking collectives, body(): lax.all_to_all(gathered.reshape(BRICKS, STENCILS, 2 * BLOCK), IMG_POSE, 0...  20.2 us
    ppermute x6, waiting for transfers between devices, shifted(): return lax.ppermute(x, axis, [(i, (i + by) % size) for i in range(size)])  13.5 us
    pallas_call x7, Pallas kernels, scores_call(): pl.pallas_call(kernel, in_specs=in_specs, out_specs=[vmem] * len(out_shap...  13 us
    pallas_call x1, Pallas kernels, gather_call(): pl.pallas_call(gather_kernel, grid=(half.shape[0] // 2,), in_specs=[pl.Bl...  12.7 us
    ppermute x6, starting transfers between devices, shifted(): return lax.ppermute(x, axis, [(i, (i + by) % size) for i in range(size)])  11.8 us
    ppermute x14, waiting for transfers between devices, flipped(): return lax.ppermute(x, axis, [(0, 1), (1, 0)])  8.56 us
    ppermute x14, starting transfers between devices, flipped(): return lax.ppermute(x, axis, [(0, 1), (1, 0)])  7.02 us
    ppermute x3, starting transfers between devices, body(): other = lax.ppermute(pieces, axis, [(i, i ^ bit) for i in range(size)])  6.61 us
  transfers between devices with their start and end apart: 23, of which 9 were waited for; matrix products, arithmetic and copies ran while one was open for 1% of the time, Pallas kernels for 19%

profile of v4, /device:TPU:0, one launch (start us, length us, event | category | flops | bytes accessed | tf_op | source)
XLA Modules:
  0.0 110.4 jit_solution(4119672022024895235)
XLA Ops:
  0.6 0.0 copy-start.3
  0.6 0.0 copy-start.2
  0.7 0.1 stack.23.pos
  0.8 1.9 %slice.9.refs_0_ = bf16[392,512]{1,0:T(8,128)(2,1)S(1)} custom-call(s32[5]{0:T(128)S(1)} %stack.23.pos, bf16[384,512]{1,0:T(8,128)(2,1)} %arrays_0_.1, f32[16,1,512]{2,1,0:T(1,128)} %bitcast.19, s32[1,768]{1,0:T(1,128)} %bitcast.21, s32[768]{0:T(1024)} %arrays_3_.1), custom_call_target="tpu_custom_call" | custom-call | tf_op jit(solution)/shard_map/slice/pallas_call | solution.py:72
  2.7 0.1 collective-permute-start.7
  2.8 1.8 %collective-permute-start = (bf16[392,512]{1,0:T(8,128)(2,1)S(1)}, bf16[392,512]{1,0:T(8,128)(2,1)S(1)}, u32[]{:S(2)}, u32[]{:S(2)}) collective-permute-start(bf16[392,512]{1,0:T(8,128)(2,1)S(1)} %slice.9.refs_0_), channel_id=1, source_target_pairs={{0,16},{16,32},{32,48},{48,0},{1,17},{17,33},{33,49},{49,1},{2,18}... | collective-permute-start | bytes 1204232 | tf_op jit(solution)/shard_map/ppermute | solution.py:383
  4.5 3.0 %collective-permute-start.5 = (bf16[392,512]{1,0:T(8,128)(2,1)S(1)}, bf16[392,512]{1,0:T(8,128)(2,1)S(1)}, u32[]{:S(2)}, u32[]{:S(2)}) collective-permute-start(bf16[392,512]{1,0:T(8,128)(2,1)S(1)} %slice.9.refs_0_), channel_id=1, source_target_pairs={{0,64},{64,0},{1,65},{65,1},{2,66},{66,2},{3,67},{67,3},{4,68},{68... | collective-permute-start | bytes 1204232 | tf_op jit(solution)/shard_map/ppermute | solution.py:387
  7.5 1.7 %collective-permute-start.3 = (bf16[392,512]{1,0:T(8,128)(2,1)S(1)}, bf16[392,512]{1,0:T(8,128)(2,1)S(1)}, u32[]{:S(2)}, u32[]{:S(2)}) collective-permute-start(bf16[392,512]{1,0:T(8,128)(2,1)S(1)} %slice.9.refs_0_), channel_id=1, source_target_pairs={{0,48},{16,0},{32,16},{48,32},{1,49},{17,1},{33,17},{49,33},{2,50}... | collective-permute-start | bytes 1204232 | tf_op jit(solution)/shard_map/ppermute | solution.py:383
  9.2 1.4 %sine_bitcast_fusion = (f32[8,32,128]{2,0,1:T(8,128)S(1)}, f32[8,32,128]{2,0,1:T(8,128)S(1)}) fusion(f32[8,4096]{1,0:T(8,128)} %param.9), kind=kLoop, calls=%fused_computation.1 | loop fusion | bytes 393216 | tf_op jit(solution)/shard_map/sin | solution.py:402
  10.6 0.1 mul.67
  10.7 0.1 multiply_multiply_fusion
  10.8 4.4 %weigh.1.refs_2_.refs_6_.w = bf16[16,1024,512]{2,1,0:T(8,128)(2,1)S(1)} custom-call(bf16[128,8192]{1,0:T(8,128)(2,1)S(1)} %copy-done, f32[8,8192]{1,0:T(8,128)S(1)} %get-tuple-element.113.cos, f32[8,8192]{1,0:T(8,128)S(1)} %get-tuple-element.112.sin), custom_call_target="tpu_custom_call" | custom-call | bytes 16777216 | tf_op jit(solution)/shard_map/weigh/pallas_call | solution.py:105
  15.1 0.7 collective-permute-done.refs_0_
  15.8 1.5 %collective-permute-done.5.refs_4_ = bf16[392,512]{1,0:T(8,128)(2,1)S(1)} collective-permute-done((bf16[392,512]{1,0:T(8,128)(2,1)S(1)}, bf16[392,512]{1,0:T(8,128)(2,1)S(1)}, u32[]{:S(2)}, u32[]{:S(2)}) %collective-permute-start.5) | collective-permute-done | bytes 401440 | tf_op jit(solution)/shard_map/ppermute | solution.py:387
  17.4 1.2 %collective-permute-done.3.refs_2_ = bf16[392,512]{1,0:T(8,128)(2,1)S(1)} collective-permute-done((bf16[392,512]{1,0:T(8,128)(2,1)S(1)}, bf16[392,512]{1,0:T(8,128)(2,1)S(1)}, u32[]{:S(2)}, u32[]{:S(2)}) %collective-permute-start.3) | collective-permute-done | bytes 401440 | tf_op jit(solution)/shard_map/ppermute | solution.py:383
  18.6 2.3 %collective-permute-start.1 = (bf16[392,512]{1,0:T(8,128)(2,1)S(1)}, bf16[392,512]{1,0:T(8,128)(2,1)S(1)}, u32[]{:S(2)}, u32[]{:S(2)}) collective-permute-start(bf16[392,512]{1,0:T(8,128)(2,1)S(1)} %collective-permute-done.refs_0_), channel_id=1, source_target_pairs={{0,64},{64,0},{1,65},{65,1},{2,66},{66,2},{3,67},{67,3},{4,68},{68... | collective-permute-start | bytes 1204232 | tf_op jit(solution)/shard_map/ppermute | solution.py:387
  20.9 1.6 %collective-permute-start.13 = (bf16[392,512]{1,0:T(8,128)(2,1)S(1)}, bf16[392,512]{1,0:T(8,128)(2,1)S(1)}, u32[]{:S(2)}, u32[]{:S(2)}) collective-permute-start(bf16[392,512]{1,0:T(8,128)(2,1)S(1)} %collective-permute-done.refs_0_), channel_id=1, source_target_pairs={{0,16},{16,32},{32,48},{48,0},{1,17},{17,33},{33,49},{49,1},{2,18}... | collective-permute-start | bytes 1204232 | tf_op jit(solution)/shard_map/ppermute | solution.py:383
  22.5 1.6 %scores.7 = (f32[384,1024]{1,0:T(8,128)S(1)}, f32[1,384]{1,0:T(1,128)S(1)}, f32[1,128]{1,0:T(1,128)S(1)}, f32[12,16,128]{2,1,0:T(8,128)S(1)}) custom-call(s32[5]{0:T(128)S(1)} %stack.23.pos, bf16[392,512]{1,0:T(8,128)(2,1)S(1)} %slice.9.refs_0_, bf16[392,512]{1,0:T(8,128)(2,1)S(1)} %collective-permute-done.7.refs_1_, ...), custom_call_target="tpu_custom_call" | custom-call | flops 805306368 | bytes 1048576 | tf_op jit(solution)/shard_map/scores/pallas_call | solution.py:243
  24.1 3.6 %scores.8 = (f32[384,1024]{1,0:T(8,128)S(1)}, f32[1,384]{1,0:T(1,128)S(1)}, f32[1,128]{1,0:T(1,128)S(1)}, f32[12,16,128]{2,1,0:T(8,128)S(1)}) custom-call(s32[5]{0:T(128)S(1)} %stack.23.pos, bf16[392,512]{1,0:T(8,128)(2,1)S(1)} %collective-permute-done.refs_0_, ...), custom_call_target="tpu_custom_call", output_to_operand_aliasing={{0}: (8, {}), {1}: (9, {}), {2}: (10, {}), {3}: (11, {})} | custom-call | flops 2415919104 | bytes 1048576 | tf_op jit(solution)/shard_map/scores/pallas_call | solution.py:243
  27.7 4.1 %collective-permute-done.1.refs_0_ = bf16[392,512]{1,0:T(8,128)(2,1)S(1)} collective-permute-done((bf16[392,512]{1,0:T(8,128)(2,1)S(1)}, bf16[392,512]{1,0:T(8,128)(2,1)S(1)}, u32[]{:S(2)}, u32[]{:S(2)}) %collective-permute-start.1) | collective-permute-done | bytes 401440 | tf_op jit(solution)/shard_map/ppermute | solution.py:387
  31.8 2.9 %collective-permute-start.9 = (bf16[392,512]{1,0:T(8,128)(2,1)S(1)}, bf16[392,512]{1,0:T(8,128)(2,1)S(1)}, u32[]{:S(2)}, u32[]{:S(2)}) collective-permute-start(bf16[392,512]{1,0:T(8,128)(2,1)S(1)} %collective-permute-done.5.refs_4_), channel_id=1, source_target_pairs={{0,48},{16,0},{32,16},{48,32},{1,49},{17,1},{33,17},{49,33},{2,50}... | collective-permute-start | bytes 1204232 | tf_op jit(solution)/shard_map/ppermute | solution.py:383
  34.7 0.2 collective-permute-start.18
  35.0 0.3 collective-permute-start.14
  35.3 1.6 %scores.9 = (f32[384,1024]{1,0:T(8,128)S(1)}, f32[1,384]{1,0:T(1,128)S(1)}, f32[1,128]{1,0:T(1,128)S(1)}, f32[12,16,128]{2,1,0:T(8,128)S(1)}) custom-call(s32[5]{0:T(128)S(1)} %stack.23.pos, bf16[392,512]{1,0:T(8,128)(2,1)S(1)} %collective-permute-done.1.refs_0_, ...), custom_call_target="tpu_custom_call", output_to_operand_aliasing={{0}: (4, {}), {1}: (5, {}), {2}: (6, {}), {3}: (7, {})} | custom-call | flops 805306368 | bytes 1048576 | tf_op jit(solution)/shard_map/scores/pallas_call | solution.py:243
  36.8 7.1 %collective-permute-done.9.refs_0_ = bf16[392,512]{1,0:T(8,128)(2,1)S(1)} collective-permute-done((bf16[392,512]{1,0:T(8,128)(2,1)S(1)}, bf16[392,512]{1,0:T(8,128)(2,1)S(1)}, u32[]{:S(2)}, u32[]{:S(2)}) %collective-permute-start.9) | collective-permute-done | bytes 401440 | tf_op jit(solution)/shard_map/ppermute | solution.py:383
  44.0 1.2 %collective-permute-start.8 = (bf16[288,512]{1,0:T(8,128)(2,1)S(1)}, bf16[288,512]{1,0:T(8,128)(2,1)S(1)}, u32[]{:S(2)}, u32[]{:S(2)}) collective-permute-start(bf16[288,512]{1,0:T(8,128)(2,1)S(1)} %slice.7), channel_id=1, source_target_pairs={{0,16},{16,32},{32,48},{48,0},{1,17},{17,33},{33,49},{49,1},{2,18}... | collective-permute-start | bytes 884744 | tf_op jit(solution)/shard_map/ppermute | solution.py:383
  45.2 2.7 %collective-permute-start.11 = (bf16[104,512]{1,0:T(8,128)(2,1)S(1)}, bf16[104,512]{1,0:T(8,128)(2,1)S(1)}, u32[]{:S(2)}, u32[]{:S(2)}) collective-permute-start(bf16[104,512]{1,0:T(8,128)(2,1)S(1)} %slice.8), channel_id=1, source_target_pairs={{0,48},{16,0},{32,16},{48,32},{1,49},{17,1},{33,17},{49,33},{2,50}... | collective-permute-start | bytes 319496 | tf_op jit(solution)/shard_map/ppermute | solution.py:383
  47.9 1.6 %scores.10 = (f32[384,1024]{1,0:T(8,128)S(1)}, f32[1,384]{1,0:T(1,128)S(1)}, f32[1,128]{1,0:T(1,128)S(1)}, f32[12,16,128]{2,1,0:T(8,128)S(1)}) custom-call(s32[5]{0:T(128)S(1)} %stack.23.pos, bf16[392,512]{1,0:T(8,128)(2,1)S(1)} %collective-permute-done.13.refs_0_, ...), custom_call_target="tpu_custom_call", output_to_operand_aliasing={{0}: (4, {}), {1}: (5, {}), {2}: (6, {}), {3}: (7, {})} | custom-call | flops 805306368 | bytes 1048576 | tf_op jit(solution)/shard_map/scores/pallas_call | solution.py:243
  49.5 1.6 %scores.11 = (f32[384,1024]{1,0:T(8,128)S(1)}, f32[1,384]{1,0:T(1,128)S(1)}, f32[1,128]{1,0:T(1,128)S(1)}, f32[12,16,128]{2,1,0:T(8,128)S(1)}) custom-call(s32[5]{0:T(128)S(1)} %stack.23.pos, bf16[392,512]{1,0:T(8,128)(2,1)S(1)} %collective-permute-done.9.refs_0_, ...), custom_call_target="tpu_custom_call", output_to_operand_aliasing={{0}: (4, {}), {1}: (5, {}), {2}: (6, {}), {3}: (7, {})} | custom-call | flops 805306368 | bytes 1048576 | tf_op jit(solution)/shard_map/scores/pallas_call | solution.py:243
  51.0 4.4 %collective-permute-done.8.refs_0_ = bf16[288,512]{1,0:T(8,128)(2,1)S(1)} collective-permute-done((bf16[288,512]{1,0:T(8,128)(2,1)S(1)}, bf16[288,512]{1,0:T(8,128)(2,1)S(1)}, u32[]{:S(2)}, u32[]{:S(2)}) %collective-permute-start.8) | collective-permute-done | bytes 294944 | tf_op jit(solution)/shard_map/ppermute | solution.py:383
  55.4 0.5 collective-permute-start.16
  56.0 1.4 %scores.12 = (f32[384,1024]{1,0:T(8,128)S(1)}, f32[1,384]{1,0:T(1,128)S(1)}, f32[1,128]{1,0:T(1,128)S(1)}, f32[12,16,128]{2,1,0:T(8,128)S(1)}) custom-call(s32[5]{0:T(128)S(1)} %stack.23.pos, bf16[288,512]{1,0:T(8,128)(2,1)S(1)} %collective-permute-done.8.refs_0_, ...), custom_call_target="tpu_custom_call", output_to_operand_aliasing={{0}: (4, {}), {1}: (5, {}), {2}: (6, {}), {3}: (7, {})} | custom-call | flops 805306368 | bytes 1048576 | tf_op jit(solution)/shard_map/scores/pallas_call | solution.py:243
  57.4 1.7 %scores.13 = (f32[12,16,128]{2,1,0:T(8,128)S(1)}, f32[384,1024]{1,0:T(8,128)S(1)}, f32[1,3,128]{2,1,0:T(4,128)S(1)}) custom-call(s32[5]{0:T(128)S(1)} %stack.23.pos, bf16[288,512]{1,0:T(8,128)(2,1)S(1)} %collective-permute-done.15.refs_0_, bf16[104,512]{1,0:T(8,128)(2,1)S(1)} %collective-permute-done.16.refs_1_, ...), custom_call_target="tpu_custom_call", output_to_operand_aliasing={{0}: (7, {})} | custom-call | flops 805306368 | bytes 1048576 | tf_op jit(solution)/shard_map/scores/pallas_call | solution.py:243
  59.1 0.1 collective-permute-start.22
  59.1 0.5 collective-permute-start.17
  59.6 2.9 %collective-permute-done.17 = f32[1,3,128]{2,1,0:T(4,128)S(1)} collective-permute-done((f32[1,3,128]{2,1,0:T(4,128)S(1)}, f32[1,3,128]{2,1,0:T(4,128)S(1)}, u32[]{:S(2)}, u32[]{:S(2)}) %collective-permute-start.17) | collective-permute-done | bytes 1568 | tf_op jit(solution)/shard_map/ppermute | solution.py:387
  62.6 0.7 collective-permute-start.19
  63.2 1.7 %weigh_half.2.rest_0_ = bf16[8,1024,512]{2,1,0:T(8,128)(2,1)S(1)} custom-call(s32[5]{0:T(128)S(1)} %stack.23.pos, bf16[128,8192]{1,0:T(8,128)(2,1)S(1)} %collective-permute-done.18.img, f32[8,8192]{1,0:T(8,128)S(1)} %get-tuple-element.113.cos, f32[8,8192]{1,0:T(8,128)S(1)} %get-tuple-element.112.sin), custom_call_target="tpu_custom_call" | custom-call | bytes 4194304 | tf_op jit(solution)/shard_map/weigh_half/pallas_call | solution.py:142
  64.9 1.3 %collective-permute-done.19 = f32[2,3,128]{2,1,0:T(4,128)S(1)} collective-permute-done((f32[2,3,128]{2,1,0:T(4,128)S(1)}, f32[2,3,128]{2,1,0:T(4,128)S(1)}, u32[]{:S(2)}, u32[]{:S(2)}) %collective-permute-start.19) | collective-permute-done | bytes 3104 | tf_op jit(solution)/shard_map/ppermute | solution.py:451
  66.2 1.9 %collective-permute-start.20 = (f32[4,3,128]{2,1,0:T(4,128)S(1)}, f32[4,3,128]{2,1,0:T(4,128)S(1)}, u32[]{:S(2)}, u32[]{:S(2)}) collective-permute-start(f32[4,3,128]{2,1,0:T(4,128)S(1)} %pad_maximum_fusion.2), channel_id=1, source_target_pairs={{0,2},{2,0},{4,6},{6,4},{1,3},{3,1},{5,7},{7,5},{8,10},{10,8},{12,... | collective-permute-start | bytes 18440 | tf_op jit(solution)/shard_map/ppermute | solution.py:451
  68.2 1.7 %weigh_half.3.w2 = bf16[8,1024,512]{2,1,0:T(8,128)(2,1)S(1)} custom-call(s32[5]{0:T(128)S(1)} %stack.23.pos, bf16[128,8192]{1,0:T(8,128)(2,1)S(1)} %collective-permute-done.18.img, f32[8,8192]{1,0:T(8,128)S(1)} %get-tuple-element.113.cos, f32[8,8192]{1,0:T(8,128)S(1)} %get-tuple-element.112.sin, ...), custom_call_target="tpu_custom_call", output_to_operand_aliasing={{}: (4, {})} | custom-call | bytes 4194304 | tf_op jit(solution)/shard_map/weigh_half/pallas_call | solution.py:142
  69.9 0.0 collective-permute-done.20
  69.9 4.0 %collective-permute-start.21 = (f32[8,3,128]{2,1,0:T(4,128)S(1)}, f32[8,3,128]{2,1,0:T(4,128)S(1)}, u32[]{:S(2)}, u32[]{:S(2)}) collective-permute-start(f32[8,3,128]{2,1,0:T(4,128)S(1)} %pad_maximum_fusion.1), channel_id=1, source_target_pairs={{0,6},{2,4},{4,2},{6,0},{1,7},{3,5},{5,3},{7,1},{8,14},{10,12},{12... | collective-permute-start | bytes 36872 | tf_op jit(solution)/shard_map/ppermute | solution.py:451
  73.9 0.3 route.1.seg
  74.2 1.4 %collective-permute-done.21 = f32[8,3,128]{2,1,0:T(4,128)S(1)} collective-permute-done((f32[8,3,128]{2,1,0:T(4,128)S(1)}, f32[8,3,128]{2,1,0:T(4,128)S(1)}, u32[]{:S(2)}, u32[]{:S(2)}) %collective-permute-start.21) | collective-permute-done | bytes 12320 | tf_op jit(solution)/shard_map/ppermute | solution.py:451
  75.7 12.7 %gather.1 = (bf16[1024,256]{1,0:T(8,128)(2,1)S(1)}, f32[1,128]{1,0:T(1,128)}, f32[1,1]{1,0:T(1,128)}) custom-call(s32[5]{0:T(128)S(1)} %stack.23.pos, f32[16,3,128]{2,1,0:T(4,128)S(1)} %pad_maximum_fusion.pieces, f32[384,1024]{1,0:T(8,128)S(1)} %get-tuple-element.104.e, f32[384,1024]{1,0:T(8,128)S(1)} %collective-permute-done.22.e2, ...), custom_call_target="tpu_custom_call" | custom-call | tf_op jit(solution)/shard_map/gather/pallas_call | solution.py:338
  88.4 20.2 %all_to_all.5.got = bf16[128,8,256]{2,1,0:T(8,128)(2,1)S(1)} all-to-all(bf16[128,8,256]{2,1,0:T(8,128)(2,1)S(1)} %bitcast.16), channel_id=1, replica_groups=mesh['xh'=2,'y'=4,'c'=2,'z'=4,'xl'=2] {'xh','y','c','z','xl'}, dimensions={0} | all-to-all | bytes 1048576 | tf_op jit(solution)/shard_map/all_to_all | solution.py:460
  108.6 1.8 %volume.1 = f32[1,512]{1,0:T(1,128)} custom-call(bf16[128,8,256]{2,1,0:T(8,128)(2,1)S(1)} %all_to_all.5.got, bf16[1,8,256,512]{3,2,1,0:T(8,128)(2,1)S(1)} %copy-done.1, f32[1,1]{1,0:T(1,128)} %get-tuple-element.108.count), custom_call_target="tpu_custom_call" | custom-call | tf_op jit(solution)/shard_map/volume/pallas_call | solution.py:373
  (33 shorter events, 0.2 us)
Async XLA Ops:
  0.6 10.0 %copy-start.3 = (f32[2]{0:T(128)S(1)}, f32[2]{0:T(128)}, u32[]{:S(2)}) copy-start(f32[2]{0:T(128)} %constant.29.clone) | copy-start | bytes 28
  0.6 10.1 %copy-start.2 = (f32[8192]{0:T(1024)S(1)}, f32[8192]{0:T(1024)}, u32[]{:S(2)}) copy-start(f32[8192]{0:T(1024)} %param.10) | copy-start | bytes 98308
  0.8 10.0 %copy-start = (bf16[128,8192]{1,0:T(8,128)(2,1)S(1)}, bf16[128,8192]{1,0:T(8,128)(2,1)}, u32[]{:S(2)}) copy-start(bf16[128,8192]{1,0:T(8,128)(2,1)} %img.1) | copy-start | bytes 6291460
  2.7 18.2 %collective-permute-start.7 = (bf16[392,512]{1,0:T(8,128)(2,1)S(1)}, bf16[392,512]{1,0:T(8,128)(2,1)S(1)}, u32[]{:S(2)}, u32[]{:S(2)}) collective-permute-start(bf16[392,512]{1,0:T(8,128)(2,1)S(1)} %slice.9.refs_0_), channel_id=1, source_target_pairs={{0,8},{8,0},{1,9},{9,1},{2,10},{10,2},{3,11},{11,3},{4,12},{12,4},... | collective-permute-start | bytes 1204232 | tf_op jit(solution)/shard_map/ppermute | solution.py:387
  2.8 13.1 %collective-permute-start = (bf16[392,512]{1,0:T(8,128)(2,1)S(1)}, bf16[392,512]{1,0:T(8,128)(2,1)S(1)}, u32[]{:S(2)}, u32[]{:S(2)}) collective-permute-start(bf16[392,512]{1,0:T(8,128)(2,1)S(1)} %slice.9.refs_0_), channel_id=1, source_target_pairs={{0,16},{16,32},{32,48},{48,0},{1,17},{17,33},{33,49},{49,1},{2,18}... | collective-permute-start | bytes 1204232 | tf_op jit(solution)/shard_map/ppermute | solution.py:383
  4.5 12.8 %collective-permute-start.5 = (bf16[392,512]{1,0:T(8,128)(2,1)S(1)}, bf16[392,512]{1,0:T(8,128)(2,1)S(1)}, u32[]{:S(2)}, u32[]{:S(2)}) collective-permute-start(bf16[392,512]{1,0:T(8,128)(2,1)S(1)} %slice.9.refs_0_), channel_id=1, source_target_pairs={{0,64},{64,0},{1,65},{65,1},{2,66},{66,2},{3,67},{67,3},{4,68},{68... | collective-permute-start | bytes 1204232 | tf_op jit(solution)/shard_map/ppermute | solution.py:387
  7.5 11.1 %collective-permute-start.3 = (bf16[392,512]{1,0:T(8,128)(2,1)S(1)}, bf16[392,512]{1,0:T(8,128)(2,1)S(1)}, u32[]{:S(2)}, u32[]{:S(2)}) collective-permute-start(bf16[392,512]{1,0:T(8,128)(2,1)S(1)} %slice.9.refs_0_), channel_id=1, source_target_pairs={{0,48},{16,0},{32,16},{48,32},{1,49},{17,1},{33,17},{49,33},{2,50}... | collective-permute-start | bytes 1204232 | tf_op jit(solution)/shard_map/ppermute | solution.py:383
  15.8 8.2 %collective-permute-start.2 = (bf16[392,512]{1,0:T(8,128)(2,1)S(1)}, bf16[392,512]{1,0:T(8,128)(2,1)S(1)}, u32[]{:S(2)}, u32[]{:S(2)}) collective-permute-start(bf16[392,512]{1,0:T(8,128)(2,1)S(1)} %collective-permute-done.refs_0_), channel_id=1, source_target_pairs={{0,8},{8,0},{1,9},{9,1},{2,10},{10,2},{3,11},{11,3},{4,12},{12,4},... | collective-permute-start | bytes 1204232 | tf_op jit(solution)/shard_map/ppermute | solution.py:387
  17.4 6.7 %collective-permute-start.6 = (bf16[392,512]{1,0:T(8,128)(2,1)S(1)}, bf16[392,512]{1,0:T(8,128)(2,1)S(1)}, u32[]{:S(2)}, u32[]{:S(2)}) collective-permute-start(bf16[392,512]{1,0:T(8,128)(2,1)S(1)} %collective-permute-done.5.refs_4_), channel_id=1, source_target_pairs={{0,8},{8,0},{1,9},{9,1},{2,10},{10,2},{3,11},{11,3},{4,12},{12,4},... | collective-permute-start | bytes 1204232 | tf_op jit(solution)/shard_map/ppermute | solution.py:387
  18.6 5.5 %collective-permute-start.4 = (bf16[392,512]{1,0:T(8,128)(2,1)S(1)}, bf16[392,512]{1,0:T(8,128)(2,1)S(1)}, u32[]{:S(2)}, u32[]{:S(2)}) collective-permute-start(bf16[392,512]{1,0:T(8,128)(2,1)S(1)} %collective-permute-done.3.refs_2_), channel_id=1, source_target_pairs={{0,8},{8,0},{1,9},{9,1},{2,10},{10,2},{3,11},{11,3},{4,12},{12,4},... | collective-permute-start | bytes 1204232 | tf_op jit(solution)/shard_map/ppermute | solution.py:387
  18.6 13.2 %collective-permute-start.1 = (bf16[392,512]{1,0:T(8,128)(2,1)S(1)}, bf16[392,512]{1,0:T(8,128)(2,1)S(1)}, u32[]{:S(2)}, u32[]{:S(2)}) collective-permute-start(bf16[392,512]{1,0:T(8,128)(2,1)S(1)} %collective-permute-done.refs_0_), channel_id=1, source_target_pairs={{0,64},{64,0},{1,65},{65,1},{2,66},{66,2},{3,67},{67,3},{4,68},{68... | collective-permute-start | bytes 1204232 | tf_op jit(solution)/shard_map/ppermute | solution.py:387
  20.9 14.1 %collective-permute-start.13 = (bf16[392,512]{1,0:T(8,128)(2,1)S(1)}, bf16[392,512]{1,0:T(8,128)(2,1)S(1)}, u32[]{:S(2)}, u32[]{:S(2)}) collective-permute-start(bf16[392,512]{1,0:T(8,128)(2,1)S(1)} %collective-permute-done.refs_0_), channel_id=1, source_target_pairs={{0,16},{16,32},{32,48},{48,0},{1,17},{17,33},{33,49},{49,1},{2,18}... | collective-permute-start | bytes 1204232 | tf_op jit(solution)/shard_map/ppermute | solution.py:383
  31.8 3.5 %collective-permute-start.10 = (bf16[392,512]{1,0:T(8,128)(2,1)S(1)}, bf16[392,512]{1,0:T(8,128)(2,1)S(1)}, u32[]{:S(2)}, u32[]{:S(2)}) collective-permute-start(bf16[392,512]{1,0:T(8,128)(2,1)S(1)} %collective-permute-done.1.refs_0_), channel_id=1, source_target_pairs={{0,8},{8,0},{1,9},{9,1},{2,10},{10,2},{3,11},{11,3},{4,12},{12,4},... | collective-permute-start | bytes 1204232 | tf_op jit(solution)/shard_map/ppermute | solution.py:387
  31.8 12.2 %collective-permute-start.9 = (bf16[392,512]{1,0:T(8,128)(2,1)S(1)}, bf16[392,512]{1,0:T(8,128)(2,1)S(1)}, u32[]{:S(2)}, u32[]{:S(2)}) collective-permute-start(bf16[392,512]{1,0:T(8,128)(2,1)S(1)} %collective-permute-done.5.refs_4_), channel_id=1, source_target_pairs={{0,48},{16,0},{32,16},{48,32},{1,49},{17,1},{33,17},{49,33},{2,50}... | collective-permute-start | bytes 1204232 | tf_op jit(solution)/shard_map/ppermute | solution.py:383
  34.7 27.8 %collective-permute-start.18 = (bf16[128,8192]{1,0:T(8,128)(2,1)S(1)}, bf16[128,8192]{1,0:T(8,128)(2,1)S(1)}, u32[]{:S(2)}, u32[]{:S(2)}) collective-permute-start(bf16[128,8192]{1,0:T(8,128)(2,1)S(1)} %copy-done), channel_id=1, source_target_pairs={{0,8},{8,0},{1,9},{9,1},{2,10},{10,2},{3,11},{11,3},{4,12},{12,4},... | collective-permute-start | bytes 6291464 | tf_op jit(solution)/shard_map/ppermute | solution.py:387
  35.0 12.9 %collective-permute-start.14 = (bf16[392,512]{1,0:T(8,128)(2,1)S(1)}, bf16[392,512]{1,0:T(8,128)(2,1)S(1)}, u32[]{:S(2)}, u32[]{:S(2)}) collective-permute-start(bf16[392,512]{1,0:T(8,128)(2,1)S(1)} %collective-permute-done.13.refs_0_), channel_id=1, source_target_pairs={{0,8},{8,0},{1,9},{9,1},{2,10},{10,2},{3,11},{11,3},{4,12},{12,4},... | collective-permute-start | bytes 1204232 | tf_op jit(solution)/shard_map/ppermute | solution.py:387
  44.0 5.5 %collective-permute-start.12 = (bf16[392,512]{1,0:T(8,128)(2,1)S(1)}, bf16[392,512]{1,0:T(8,128)(2,1)S(1)}, u32[]{:S(2)}, u32[]{:S(2)}) collective-permute-start(bf16[392,512]{1,0:T(8,128)(2,1)S(1)} %collective-permute-done.9.refs_0_), channel_id=1, source_target_pairs={{0,8},{8,0},{1,9},{9,1},{2,10},{10,2},{3,11},{11,3},{4,12},{12,4},... | collective-permute-start | bytes 1204232 | tf_op jit(solution)/shard_map/ppermute | solution.py:387
  44.0 11.4 %collective-permute-start.8 = (bf16[288,512]{1,0:T(8,128)(2,1)S(1)}, bf16[288,512]{1,0:T(8,128)(2,1)S(1)}, u32[]{:S(2)}, u32[]{:S(2)}) collective-permute-start(bf16[288,512]{1,0:T(8,128)(2,1)S(1)} %slice.7), channel_id=1, source_target_pairs={{0,16},{16,32},{32,48},{48,0},{1,17},{17,33},{33,49},{49,1},{2,18}... | collective-permute-start | bytes 884744 | tf_op jit(solution)/shard_map/ppermute | solution.py:383
  45.2 10.2 %collective-permute-start.11 = (bf16[104,512]{1,0:T(8,128)(2,1)S(1)}, bf16[104,512]{1,0:T(8,128)(2,1)S(1)}, u32[]{:S(2)}, u32[]{:S(2)}) collective-permute-start(bf16[104,512]{1,0:T(8,128)(2,1)S(1)} %slice.8), channel_id=1, source_target_pairs={{0,48},{16,0},{32,16},{48,32},{1,49},{17,1},{33,17},{49,33},{2,50}... | collective-permute-start | bytes 319496 | tf_op jit(solution)/shard_map/ppermute | solution.py:383
  55.4 1.9 %collective-permute-start.15 = (bf16[288,512]{1,0:T(8,128)(2,1)S(1)}, bf16[288,512]{1,0:T(8,128)(2,1)S(1)}, u32[]{:S(2)}, u32[]{:S(2)}) collective-permute-start(bf16[288,512]{1,0:T(8,128)(2,1)S(1)} %collective-permute-done.8.refs_0_), channel_id=1, source_target_pairs={{0,8},{8,0},{1,9},{9,1},{2,10},{10,2},{3,11},{11,3},{4,12},{12,4},... | collective-permute-start | bytes 884744 | tf_op jit(solution)/shard_map/ppermute | solution.py:387
  55.4 1.9 %collective-permute-start.16 = (bf16[104,512]{1,0:T(8,128)(2,1)S(1)}, bf16[104,512]{1,0:T(8,128)(2,1)S(1)}, u32[]{:S(2)}, u32[]{:S(2)}) collective-permute-start(bf16[104,512]{1,0:T(8,128)(2,1)S(1)} %collective-permute-done.11.refs_1_), channel_id=1, source_target_pairs={{0,8},{8,0},{1,9},{9,1},{2,10},{10,2},{3,11},{11,3},{4,12},{12,4},... | collective-permute-start | bytes 319496 | tf_op jit(solution)/shard_map/ppermute | solution.py:387
  59.1 16.6 %collective-permute-start.22 = (f32[384,1024]{1,0:T(8,128)S(1)}, f32[384,1024]{1,0:T(8,128)S(1)}, u32[]{:S(2)}, u32[]{:S(2)}) collective-permute-start(f32[384,1024]{1,0:T(8,128)S(1)} %get-tuple-element.104.e), channel_id=1, source_target_pairs={{0,8},{8,0},{1,9},{9,1},{2,10},{10,2},{3,11},{11,3},{4,12},{12,4},... | collective-permute-start | bytes 4718600 | tf_op jit(solution)/shard_map/ppermute | solution.py:387
  59.1 3.4 %collective-permute-start.17 = (f32[1,3,128]{2,1,0:T(4,128)S(1)}, f32[1,3,128]{2,1,0:T(4,128)S(1)}, u32[]{:S(2)}, u32[]{:S(2)}) collective-permute-start(f32[1,3,128]{2,1,0:T(4,128)S(1)} %get-tuple-element.98), channel_id=1, source_target_pairs={{0,8},{8,0},{1,9},{9,1},{2,10},{10,2},{3,11},{11,3},{4,12},{12,4},... | collective-permute-start | bytes 4616 | tf_op jit(solution)/shard_map/ppermute | solution.py:387
  62.6 3.7 %collective-permute-start.19 = (f32[2,3,128]{2,1,0:T(4,128)S(1)}, f32[2,3,128]{2,1,0:T(4,128)S(1)}, u32[]{:S(2)}, u32[]{:S(2)}) collective-permute-start(f32[2,3,128]{2,1,0:T(4,128)S(1)} %pad_maximum_fusion.3), channel_id=1, source_target_pairs={{0,1},{1,0},{2,3},{3,2},{4,5},{5,4},{6,7},{7,6},{8,9},{9,8},{10,11... | collective-permute-start | bytes 9224 | tf_op jit(solution)/shard_map/ppermute | solution.py:451
  66.2 3.7 %collective-permute-start.20 = (f32[4,3,128]{2,1,0:T(4,128)S(1)}, f32[4,3,128]{2,1,0:T(4,128)S(1)}, u32[]{:S(2)}, u32[]{:S(2)}) collective-permute-start(f32[4,3,128]{2,1,0:T(4,128)S(1)} %pad_maximum_fusion.2), channel_id=1, source_target_pairs={{0,2},{2,0},{4,6},{6,4},{1,3},{3,1},{5,7},{7,5},{8,10},{10,8},{12,... | collective-permute-start | bytes 18440 | tf_op jit(solution)/shard_map/ppermute | solution.py:451
  69.9 5.8 %collective-permute-start.21 = (f32[8,3,128]{2,1,0:T(4,128)S(1)}, f32[8,3,128]{2,1,0:T(4,128)S(1)}, u32[]{:S(2)}, u32[]{:S(2)}) collective-permute-start(f32[8,3,128]{2,1,0:T(4,128)S(1)} %pad_maximum_fusion.1), channel_id=1, source_target_pairs={{0,6},{2,4},{4,2},{6,0},{1,7},{3,5},{5,3},{7,1},{8,14},{10,12},{12... | collective-permute-start | bytes 36872 | tf_op jit(solution)/shard_map/ppermute | solution.py:451
  75.7 33.0 %copy-start.1 = (bf16[1,8,256,512]{3,2,1,0:T(8,128)(2,1)S(1)}, bf16[1,8,256,512]{3,2,1,0:T(8,128)(2,1)}, u32[]{:S(2)}) copy-start(bf16[1,8,256,512]{3,2,1,0:T(8,128)(2,1)} %interp.1) | copy-start | bytes 6291460

commit v5 on v4

--- a/solution.py
+++ b/solution.py
@@ -24,21 +24,21 @@
 
 LIMIT = pltpu.CompilerParams(vmem_limit_bytes=12 << 20)
 IDS = 8
-LOW = 288
+LOW = 224
 
 
 def slice_kernel(pos, *arrays):
-    sources, out, copied, done = arrays[:4], arrays[4], arrays[5:9], arrays[9]
+    sources, out, copied, done = arrays[:4], arrays[4], arrays[5:8], arrays[8]
+    n = sources[0].shape[0]
+    places = (out.at[pl.ds(0, n), :], *copied)
     copies = [
-        pltpu.make_async_copy(sources[j], copied[j], done.at[j]) for j in range(4)
+        pltpu.make_async_copy(sources[j], places[j], done.at[j]) for j in range(4)
     ]
     for copy in copies:
         copy.start()
-    for copy in copies:
-        copy.wait()
-    refs, noise, routing, stencil = copied
-    n = refs.shape[0]
-    out[:n, :] = refs[...]
+    noise, routing, stencil = copied
+    copies[2].wait()
+    copies[3].wait()
     bricks = routing[...].astype(F32)
     kinds = stencil[...].reshape(1, -1).astype(F32)
     one = bricks[:, :512]
@@ -50,7 +50,9 @@
         hits = hits + jnp.where(lane == routing[:, u * 128 : u * 128 + 128], 1.0, 0.0)
     counts = jnp.sum(hits.T, axis=0, keepdims=True)
     chip = pos[0] * 4 + pos[1]
-    wide = refs[...].astype(F32)
+    copies[0].wait()
+    copies[1].wait()
+    wide = out[:n, :].astype(F32)
     q = wide * wide * noise[chip * 2 + pos[2]]
     q = q[:, :128] + q[:, 128:256] + (q[:, 256:384] + q[:, 384:])
     norm = jnp.concatenate(
@@ -74,7 +76,7 @@
         in_specs=[pl.BlockSpec(memory_space=pltpu.SMEM)]
         + [pl.BlockSpec(memory_space=pltpu.HBM)] * 4,
         out_specs=pl.BlockSpec(memory_space=pltpu.VMEM),
-        scratch_shapes=[pltpu.VMEM(a.shape, a.dtype) for a in arrays]
+        scratch_shapes=[pltpu.VMEM(a.shape, a.dtype) for a in arrays[1:]]
         + [pltpu.SemaphoreType.DMA((4,))],
         out_shape=jax.ShapeDtypeStruct((refs.shape[0] + IDS, SLICE), BF16),
         compiler_params=LIMIT,
@@ -205,14 +207,12 @@
             m = None
             for t in range(TRANS):
                 at = slice(t * imgs, (t + 1) * imgs)
-                s = s_acc[:, at] - half
-                s_acc[:, at] = s
-                s = jnp.max(s, axis=0, keepdims=True)
+                s = jnp.max(s_acc[:, at] - half, axis=0, keepdims=True)
                 m = s if m is None else jnp.maximum(m, s)
             total = jnp.zeros((1, imgs), F32)
             for t in range(TRANS):
                 at = slice(t * imgs, (t + 1) * imgs)
-                e = jnp.exp(s_acc[:, at] - m)
+                e = jnp.exp((s_acc[:, at] - half) - m)
                 e_out[:, at] = e
                 total = total + jnp.sum(e, axis=0, keepdims=True)
             st_out[0, 0:1, :] = m
@@ -253,7 +253,7 @@
     )(*args)
 
 
-def route_kernel(h, seg):
+def route_kernel(pos, h, seg):
     ids = None
     for kind, scale in ((0, STENCILS), (1, 1)):
         flat = h[6 * kind : 6 * kind + 6].reshape(96, 128)
@@ -266,22 +266,38 @@
             part = jnp.dot(turned[j * 32 : j * 32 + 32, :], put, preferred_element_type=F32)
             part = part * float(scale)
             ids = part if ids is None else ids + part
-    seg[...] = ids.astype(jnp.int32)
-
-
-def route_call(h):
+    ids = ids.astype(jnp.int32)
+    core = jnp.bitwise_and(jnp.right_shift(ids, 6), 1)
+    short = jnp.right_shift(ids, 7) * 64 + jnp.bitwise_and(ids, 63)
+    seg[0] = jnp.where(core == pos[2], -1, short)
+    seg[1] = jnp.where(core == pos[2], short, -1)
+
+
+def route_call(where, h):
     return pl.pallas_call(
         route_kernel,
-        in_specs=[pl.BlockSpec(memory_space=pltpu.VMEM)],
+        in_specs=[
+            pl.BlockSpec(memory_space=pltpu.SMEM),
+            pl.BlockSpec(memory_space=pltpu.VMEM),
+        ],
         out_specs=pl.BlockSpec(memory_space=pltpu.VMEM),
-        out_shape=pltpu.VMEM((NBLK, 384), jnp.int32),
+        out_shape=pltpu.VMEM((2, NBLK, 384), jnp.int32),
         compiler_params=LIMIT,
         cost_estimate=pl.CostEstimate(flops=1 << 26, bytes_accessed=1 << 20, transcendentals=0),
         name="route",
-    )(h)
-
-
-def gather_kernel(pos, pieces, e, e2, w, w2, seg, g_out, ev_out, num_out, post, post2, acc):
+    )(where, h)
+
+
+def picked(seg, side, at, rows, count):
+    ids = [seg[side, pl.ds(2 * at + j, 1), :] for j in range(2)]
+    hot = lax.broadcasted_iota(jnp.int32, (count, 768), 0) == jnp.concatenate(ids, axis=1)
+    hot = jnp.where(hot, 1.0, 0.0).astype(BF16)
+    return jnp.dot(hot, rows, preferred_element_type=F32)
+
+
+def gather_kernel(
+    pos, pieces, e, e2, w, w2, seg, g_out, store, ev_out, num_out, post, post2, acc
+):
     step = pl.program_id(0)
 
     @pl.when(step == 0)
@@ -320,10 +336,8 @@
         rows = rows + jnp.dot(post2[...], w2[near], preferred_element_type=F32)
         rows = rows.astype(BF16)
         both = jnp.concatenate([rows[:, :256], rows[:, 256:]], axis=0)
-        ids = jnp.concatenate([seg[pl.ds(2 * at, 1), :], seg[pl.ds(2 * at + 1, 1), :]], axis=1)
-        hot = lax.broadcasted_iota(jnp.int32, (acc.shape[0], ids.shape[1]), 0) == ids
-        hot = jnp.where(hot, 1.0, 0.0).astype(BF16)
-        part = jnp.dot(hot, both, preferred_element_type=F32)
+        store[near] = both
+        part = picked(seg, 0, at, both, acc.shape[0])
         added = part if added is None else added + part
     acc[...] += added
 
@@ -333,15 +347,16 @@
 
 
 def gather_call(where, pieces, e, e2, weighted, half, seg):
-    segs = BRICKS * STENCILS
+    segs = BRICKS * STENCILS // 2
     vmem = pl.BlockSpec(memory_space=pltpu.VMEM)
     return pl.pallas_call(
         gather_kernel,
         grid=(half.shape[0] // 2,),
         in_specs=[pl.BlockSpec(memory_space=pltpu.SMEM)] + [vmem] * 6,
-        out_specs=[vmem] * 3,
+        out_specs=[vmem] * 4,
         out_shape=[
             jax.ShapeDtypeStruct((segs, 256), BF16),
+            pltpu.VMEM((half.shape[0], 768, 256), BF16),
             jax.ShapeDtypeStruct((1, pieces.shape[2]), F32),
             jax.ShapeDtypeStruct((1, 1), F32),
         ],
@@ -351,8 +366,31 @@
             pltpu.VMEM((segs, 256), F32),
         ],
         compiler_params=LIMIT,
+        cost_estimate=pl.CostEstimate(flops=1 << 33, bytes_accessed=1 << 20, transcendentals=0),
         name="gather",
     )(where, pieces, e, e2, weighted, half, seg)
+
+
+def keep_kernel(pos, store, seg, out):
+    total = None
+    for near in range(store.shape[0]):
+        at = pos[2] * store.shape[0] + near
+        part = picked(seg, 1, at, store[near], out.shape[0])
+        total = part if total is None else total + part
+    out[...] = total
+
+
+def keep_call(where, store, seg):
+    vmem = pl.BlockSpec(memory_space=pltpu.VMEM)
+    return pl.pallas_call(
+        keep_kernel,
+        in_specs=[pl.BlockSpec(memory_space=pltpu.SMEM)] + [vmem] * 2,
+        out_specs=vmem,
+        out_shape=pltpu.VMEM((BRICKS * STENCILS // 2, 256), F32),
+        compiler_params=LIMIT,
+        cost_estimate=pl.CostEstimate(flops=1 << 31, bytes_accessed=1 << 20, transcendentals=0),
+        name="keep",
+    )(where, store, seg)
 
 
 def volume_kernel(got, interp, count, out):
@@ -425,9 +463,8 @@
     )
     aleft, two = lax.optimization_barrier((aleft, two))
     alow = shifted(aleft[:LOW], "y", 1)
+    ahigh = shifted(aright[LOW:], "y", -1)
     three = scores_call([pair(aleft, (1, -1))], where, weighted, two, False)
-    aright, three = lax.optimization_barrier((aright, three))
-    ahigh = shifted(aright[LOW:], "y", -1)
     four = scores_call([pair(far, (0, 2))], where, weighted, three, False)
     five = scores_call([pair(aright, (1, 1))], where, weighted, four, False)
     alow, ahigh, five = lax.optimization_barrier((alow, ahigh, five))
@@ -455,10 +492,14 @@
             half = weight_half(where, other_images, cos, sin, 1, half)
         elif bit == 1:
             pieces, half = lax.optimization_barrier((pieces, half))
-    seg = route_call(marks)
-    gathered, evidence, count = gather_call(where, pieces, e, e2, weighted, half, seg)
+    seg = route_call(where, marks)
+    given, store, evidence, count = gather_call(where, pieces, e, e2, weighted, half, seg)
+    taken = swapped(given)
+    kept = keep_call(where, store, seg)
+    gathered = (kept + taken.astype(F32)).astype(BF16)
     got = lax.all_to_all(
-        gathered.reshape(BRICKS, STENCILS, 2 * BLOCK), IMG_POSE, 0, 0, tiled=True
+        gathered.reshape(BRICKS // 2, STENCILS, 2 * BLOCK),
+        ("xh", "y", "z", "xl"), 0, 0, tiled=True,
     )
     volume = volume_call(got, interp, count)
     return (volume, evidence.reshape(-1))

time: 111 us -> 96.8 us (0.87)
  waiting for transfers between devices: 24.8 us -> 12.5 us
  blocking collectives: 20.2 us -> 18.8 us
  starting transfers between devices: 25.4 us -> 24.1 us
    ppermute x6, waiting for transfers between devices: 13.5 us -> 3.41 us  [shifted(): return lax.ppermute(x, axis, [(i, (i + by) % size) for i in range(size)])]
    pallas_call x1 -> x2, Pallas kernels: 0.29 us -> 3.18 us  [the longest x1 2.33 us: keep_call(): pl.pallas_call(keep_kernel, in_specs=[pl.BlockSpec(memory_space=pltpu.SME...]
    ppermute x6, starting transfers between devices: 11.8 us -> 10 us  [shifted(): return lax.ppermute(x, axis, [(i, (i + by) % size) for i in range(size)])]
    pallas_call x1, Pallas kernels: 12.7 us -> 11.1 us  [gather_call(): pl.pallas_call(gather_kernel, grid=(half.shape[0] // 2,), in_specs=[pl.Bl...]
    ppermute x14 -> x15, waiting for transfers between devices: 8.56 us -> 6.91 us  [flipped(): return lax.ppermute(x, axis, [(0, 1), (1, 0)])]
    all_to_all x1, blocking collectives: 20.2 us -> 18.8 us  [body(): lax.all_to_all(gathered.reshape(BRICKS // 2, STENCILS, 2 * BLOCK), ('xh',...]
    ppermute x14 -> x15, starting transfers between devices: 7.02 us -> 7.44 us  [flipped(): return lax.ppermute(x, axis, [(0, 1), (1, 0)])]
  transfers between devices with their start and end apart: 23 -> 24, of which waited for: 9 -> 10; matrix products, arithmetic and copies ran while one was open for 1% -> 2% of each run, Pallas kernels for 19% -> 25%
where the time goes in v5:
time: 96.8 us; the launch traced here: 96.6 us
  Pallas kernels  38.5 us (40%)
  starting transfers between devices  24.1 us (25%)
  blocking collectives  18.8 us (19%)
  waiting for transfers between devices  12.5 us (13%)
  local copies, waits for them, and re-layouts  1.61 us (2%)
    all_to_all x1, blocking collectives, body(): lax.all_to_all(gathered.reshape(BRICKS // 2, STENCILS, 2 * BLOCK), ('xh',...  18.8 us
    pallas_call x7, Pallas kernels, scores_call(): pl.pallas_call(kernel, in_specs=in_specs, out_specs=[vmem] * len(out_shap...  13 us
    pallas_call x1, Pallas kernels, gather_call(): pl.pallas_call(gather_kernel, grid=(half.shape[0] // 2,), in_specs=[pl.Bl...  11.1 us
    ppermute x6, starting transfers between devices, shifted(): return lax.ppermute(x, axis, [(i, (i + by) % size) for i in range(size)])  10 us
    ppermute x15, starting transfers between devices, flipped(): return lax.ppermute(x, axis, [(0, 1), (1, 0)])  7.44 us
    ppermute x15, waiting for transfers between devices, flipped(): return lax.ppermute(x, axis, [(0, 1), (1, 0)])  6.91 us
    ppermute x3, starting transfers between devices, body(): other = lax.ppermute(pieces, axis, [(i, i ^ bit) for i in range(size)])  6.63 us
    pallas_call x1, Pallas kernels, weight_rows(): pl.pallas_call(weight_kernel, grid=(slices,), in_specs=[pl.BlockSpec((n,...  4.36 us
  transfers between devices with their start and end apart: 24, of which 10 were waited for; matrix products, arithmetic and copies ran while one was open for 2% of the time, Pallas kernels for 25%

profile of v5, /device:TPU:0, one launch (start us, length us, event | category | flops | bytes accessed | tf_op | source)
XLA Modules:
  0.0 96.6 jit_solution(781268485516172029)
XLA Ops:
  0.7 0.1 stack.23.pos
  0.8 1.8 %slice.10.refs_0_ = bf16[392,512]{1,0:T(8,128)(2,1)S(1)} custom-call(s32[5]{0:T(128)S(1)} %stack.23.pos, bf16[384,512]{1,0:T(8,128)(2,1)} %arrays_0_.1, f32[16,1,512]{2,1,0:T(1,128)} %bitcast.19, s32[1,768]{1,0:T(1,128)} %bitcast.21, s32[768]{0:T(1024)} %arrays_3_.1), custom_call_target="tpu_custom_call" | custom-call | tf_op jit(solution)/shard_map/slice/pallas_call | solution.py:74
  2.6 0.1 collective-permute-start.7
  2.7 1.8 %collective-permute-start = (bf16[392,512]{1,0:T(8,128)(2,1)S(1)}, bf16[392,512]{1,0:T(8,128)(2,1)S(1)}, u32[]{:S(2)}, u32[]{:S(2)}) collective-permute-start(bf16[392,512]{1,0:T(8,128)(2,1)S(1)} %slice.10.refs_0_), channel_id=1, source_target_pairs={{0,16},{16,32},{32,48},{48,0},{1,17},{17,33},{33,49},{49,1},{2,18}... | collective-permute-start | bytes 1204232 | tf_op jit(solution)/shard_map/ppermute | solution.py:421
  4.5 3.0 %collective-permute-start.5 = (bf16[392,512]{1,0:T(8,128)(2,1)S(1)}, bf16[392,512]{1,0:T(8,128)(2,1)S(1)}, u32[]{:S(2)}, u32[]{:S(2)}) collective-permute-start(bf16[392,512]{1,0:T(8,128)(2,1)S(1)} %slice.10.refs_0_), channel_id=1, source_target_pairs={{0,64},{64,0},{1,65},{65,1},{2,66},{66,2},{3,67},{67,3},{4,68},{68... | collective-permute-start | bytes 1204232 | tf_op jit(solution)/shard_map/ppermute | solution.py:425
  7.5 1.7 %collective-permute-start.3 = (bf16[392,512]{1,0:T(8,128)(2,1)S(1)}, bf16[392,512]{1,0:T(8,128)(2,1)S(1)}, u32[]{:S(2)}, u32[]{:S(2)}) collective-permute-start(bf16[392,512]{1,0:T(8,128)(2,1)S(1)} %slice.10.refs_0_), channel_id=1, source_target_pairs={{0,48},{16,0},{32,16},{48,32},{1,49},{17,1},{33,17},{49,33},{2,50}... | collective-permute-start | bytes 1204232 | tf_op jit(solution)/shard_map/ppermute | solution.py:421
  9.1 1.4 %sine_bitcast_fusion = (f32[8,32,128]{2,0,1:T(8,128)S(1)}, f32[8,32,128]{2,0,1:T(8,128)S(1)}) fusion(f32[8,4096]{1,0:T(8,128)} %param.9), kind=kLoop, calls=%fused_computation.3 | loop fusion | bytes 393216 | tf_op jit(solution)/shard_map/sin | solution.py:440
  10.6 0.1 mul.67
  10.7 0.1 multiply_multiply_fusion
  10.7 4.4 %weigh.1.refs_2_.refs_6_.w = bf16[16,1024,512]{2,1,0:T(8,128)(2,1)S(1)} custom-call(bf16[128,8192]{1,0:T(8,128)(2,1)S(1)} %copy-done, f32[8,8192]{1,0:T(8,128)S(1)} %get-tuple-element.105.cos, f32[8,8192]{1,0:T(8,128)S(1)} %get-tuple-element.104.sin), custom_call_target="tpu_custom_call" | custom-call | bytes 16777216 | tf_op jit(solution)/shard_map/weigh/pallas_call | solution.py:107
  15.1 0.7 collective-permute-done.refs_0_
  15.8 1.5 %collective-permute-done.5.refs_4_ = bf16[392,512]{1,0:T(8,128)(2,1)S(1)} collective-permute-done((bf16[392,512]{1,0:T(8,128)(2,1)S(1)}, bf16[392,512]{1,0:T(8,128)(2,1)S(1)}, u32[]{:S(2)}, u32[]{:S(2)}) %collective-permute-start.5) | collective-permute-done | bytes 401440 | tf_op jit(solution)/shard_map/ppermute | solution.py:425
  17.3 1.2 %collective-permute-done.3.refs_2_ = bf16[392,512]{1,0:T(8,128)(2,1)S(1)} collective-permute-done((bf16[392,512]{1,0:T(8,128)(2,1)S(1)}, bf16[392,512]{1,0:T(8,128)(2,1)S(1)}, u32[]{:S(2)}, u32[]{:S(2)}) %collective-permute-start.3) | collective-permute-done | bytes 401440 | tf_op jit(solution)/shard_map/ppermute | solution.py:421
  18.5 2.3 %collective-permute-start.1 = (bf16[392,512]{1,0:T(8,128)(2,1)S(1)}, bf16[392,512]{1,0:T(8,128)(2,1)S(1)}, u32[]{:S(2)}, u32[]{:S(2)}) collective-permute-start(bf16[392,512]{1,0:T(8,128)(2,1)S(1)} %collective-permute-done.refs_0_), channel_id=1, source_target_pairs={{0,64},{64,0},{1,65},{65,1},{2,66},{66,2},{3,67},{67,3},{4,68},{68... | collective-permute-start | bytes 1204232 | tf_op jit(solution)/shard_map/ppermute | solution.py:425
  20.8 1.6 %collective-permute-start.12 = (bf16[392,512]{1,0:T(8,128)(2,1)S(1)}, bf16[392,512]{1,0:T(8,128)(2,1)S(1)}, u32[]{:S(2)}, u32[]{:S(2)}) collective-permute-start(bf16[392,512]{1,0:T(8,128)(2,1)S(1)} %collective-permute-done.refs_0_), channel_id=1, source_target_pairs={{0,16},{16,32},{32,48},{48,0},{1,17},{17,33},{33,49},{49,1},{2,18}... | collective-permute-start | bytes 1204232 | tf_op jit(solution)/shard_map/ppermute | solution.py:421
  22.4 1.7 %collective-permute-start.9 = (bf16[392,512]{1,0:T(8,128)(2,1)S(1)}, bf16[392,512]{1,0:T(8,128)(2,1)S(1)}, u32[]{:S(2)}, u32[]{:S(2)}) collective-permute-start(bf16[392,512]{1,0:T(8,128)(2,1)S(1)} %collective-permute-done.5.refs_4_), channel_id=1, source_target_pairs={{0,48},{16,0},{32,16},{48,32},{1,49},{17,1},{33,17},{49,33},{2,50}... | collective-permute-start | bytes 1204232 | tf_op jit(solution)/shard_map/ppermute | solution.py:421
  24.1 1.6 %scores.7 = (f32[384,1024]{1,0:T(8,128)S(1)}, f32[1,384]{1,0:T(1,128)S(1)}, f32[1,128]{1,0:T(1,128)S(1)}, f32[12,16,128]{2,1,0:T(8,128)S(1)}) custom-call(s32[5]{0:T(128)S(1)} %stack.23.pos, bf16[392,512]{1,0:T(8,128)(2,1)S(1)} %slice.10.refs_0_, bf16[392,512]{1,0:T(8,128)(2,1)S(1)} %collective-permute-done.7.refs_1_, ...), custom_call_target="tpu_custom_call" | custom-call | flops 805306368 | bytes 1048576 | tf_op jit(solution)/shard_map/scores/pallas_call | solution.py:243
  25.7 3.6 %scores.8 = (f32[384,1024]{1,0:T(8,128)S(1)}, f32[1,384]{1,0:T(1,128)S(1)}, f32[1,128]{1,0:T(1,128)S(1)}, f32[12,16,128]{2,1,0:T(8,128)S(1)}) custom-call(s32[5]{0:T(128)S(1)} %stack.23.pos, bf16[392,512]{1,0:T(8,128)(2,1)S(1)} %collective-permute-done.refs_0_, ...), custom_call_target="tpu_custom_call", output_to_operand_aliasing={{0}: (8, {}), {1}: (9, {}), {2}: (10, {}), {3}: (11, {})} | custom-call | flops 2415919104 | bytes 1048576 | tf_op jit(solution)/shard_map/scores/pallas_call | solution.py:243
  29.3 2.5 %collective-permute-done.1.refs_0_ = bf16[392,512]{1,0:T(8,128)(2,1)S(1)} collective-permute-done((bf16[392,512]{1,0:T(8,128)(2,1)S(1)}, bf16[392,512]{1,0:T(8,128)(2,1)S(1)}, u32[]{:S(2)}, u32[]{:S(2)}) %collective-permute-start.1) | collective-permute-done | bytes 401440 | tf_op jit(solution)/shard_map/ppermute | solution.py:425
  31.8 0.5 collective-permute-start.18
  32.3 0.7 collective-permute-done.12.refs_0_
  33.0 0.1 collective-permute-done.9.refs_0_
  33.1 0.4 collective-permute-start.11
  33.5 0.9 collective-permute-start.8
  34.5 2.4 %collective-permute-start.10 = (bf16[168,512]{1,0:T(8,128)(2,1)S(1)}, bf16[168,512]{1,0:T(8,128)(2,1)S(1)}, u32[]{:S(2)}, u32[]{:S(2)}) collective-permute-start(bf16[168,512]{1,0:T(8,128)(2,1)S(1)} %slice.9), channel_id=1, source_target_pairs={{0,48},{16,0},{32,16},{48,32},{1,49},{17,1},{33,17},{49,33},{2,50}... | collective-permute-start | bytes 516104 | tf_op jit(solution)/shard_map/ppermute | solution.py:421
  36.9 1.6 %scores.9 = (f32[384,1024]{1,0:T(8,128)S(1)}, f32[1,384]{1,0:T(1,128)S(1)}, f32[1,128]{1,0:T(1,128)S(1)}, f32[12,16,128]{2,1,0:T(8,128)S(1)}) custom-call(s32[5]{0:T(128)S(1)} %stack.23.pos, bf16[392,512]{1,0:T(8,128)(2,1)S(1)} %collective-permute-done.1.refs_0_, ...), custom_call_target="tpu_custom_call", output_to_operand_aliasing={{0}: (4, {}), {1}: (5, {}), {2}: (6, {}), {3}: (7, {})} | custom-call | flops 805306368 | bytes 1048576 | tf_op jit(solution)/shard_map/scores/pallas_call | solution.py:243
  38.5 1.6 %scores.10 = (f32[384,1024]{1,0:T(8,128)S(1)}, f32[1,384]{1,0:T(1,128)S(1)}, f32[1,128]{1,0:T(1,128)S(1)}, f32[12,16,128]{2,1,0:T(8,128)S(1)}) custom-call(s32[5]{0:T(128)S(1)} %stack.23.pos, bf16[392,512]{1,0:T(8,128)(2,1)S(1)} %collective-permute-done.12.refs_0_, ...), custom_call_target="tpu_custom_call", output_to_operand_aliasing={{0}: (4, {}), {1}: (5, {}), {2}: (6, {}), {3}: (7, {})} | custom-call | flops 805306368 | bytes 1048576 | tf_op jit(solution)/shard_map/scores/pallas_call | solution.py:243
  40.1 1.6 %scores.11 = (f32[384,1024]{1,0:T(8,128)S(1)}, f32[1,384]{1,0:T(1,128)S(1)}, f32[1,128]{1,0:T(1,128)S(1)}, f32[12,16,128]{2,1,0:T(8,128)S(1)}) custom-call(s32[5]{0:T(128)S(1)} %stack.23.pos, bf16[392,512]{1,0:T(8,128)(2,1)S(1)} %collective-permute-done.9.refs_0_, ...), custom_call_target="tpu_custom_call", output_to_operand_aliasing={{0}: (4, {}), {1}: (5, {}), {2}: (6, {}), {3}: (7, {})} | custom-call | flops 805306368 | bytes 1048576 | tf_op jit(solution)/shard_map/scores/pallas_call | solution.py:243
  41.7 0.7 collective-permute-done.8.refs_0_
  42.4 0.5 collective-permute-start.16
  42.9 1.4 %scores.12 = (f32[384,1024]{1,0:T(8,128)S(1)}, f32[1,384]{1,0:T(1,128)S(1)}, f32[1,128]{1,0:T(1,128)S(1)}, f32[12,16,128]{2,1,0:T(8,128)S(1)}) custom-call(s32[5]{0:T(128)S(1)} %stack.23.pos, bf16[224,512]{1,0:T(8,128)(2,1)S(1)} %collective-permute-done.8.refs_0_, ...), custom_call_target="tpu_custom_call", output_to_operand_aliasing={{0}: (4, {}), {1}: (5, {}), {2}: (6, {}), {3}: (7, {})} | custom-call | flops 805306368 | bytes 1048576 | tf_op jit(solution)/shard_map/scores/pallas_call | solution.py:243
  44.3 1.7 %scores.13 = (f32[12,16,128]{2,1,0:T(8,128)S(1)}, f32[384,1024]{1,0:T(8,128)S(1)}, f32[1,3,128]{2,1,0:T(4,128)S(1)}) custom-call(s32[5]{0:T(128)S(1)} %stack.23.pos, bf16[224,512]{1,0:T(8,128)(2,1)S(1)} %collective-permute-done.15.refs_0_, bf16[168,512]{1,0:T(8,128)(2,1)S(1)} %collective-permute-done.16.refs_1_, ...), custom_call_target="tpu_custom_call", output_to_operand_aliasing={{0}: (7, {})} | custom-call | flops 805306368 | bytes 1048576 | tf_op jit(solution)/shard_map/scores/pallas_call | solution.py:243
  46.0 0.1 collective-permute-start.22
  46.1 0.5 collective-permute-start.17
  46.6 2.9 %collective-permute-done.17 = f32[1,3,128]{2,1,0:T(4,128)S(1)} collective-permute-done((f32[1,3,128]{2,1,0:T(4,128)S(1)}, f32[1,3,128]{2,1,0:T(4,128)S(1)}, u32[]{:S(2)}, u32[]{:S(2)}) %collective-permute-start.17) | collective-permute-done | bytes 1568 | tf_op jit(solution)/shard_map/ppermute | solution.py:425
  49.5 0.7 collective-permute-start.19
  50.2 1.7 %weigh_half.2.rest_0_ = bf16[8,1024,512]{2,1,0:T(8,128)(2,1)S(1)} custom-call(s32[5]{0:T(128)S(1)} %stack.23.pos, bf16[128,8192]{1,0:T(8,128)(2,1)S(1)} %collective-permute-done.18.img, f32[8,8192]{1,0:T(8,128)S(1)} %get-tuple-element.105.cos, f32[8,8192]{1,0:T(8,128)S(1)} %get-tuple-element.104.sin), custom_call_target="tpu_custom_call" | custom-call | bytes 4194304 | tf_op jit(solution)/shard_map/weigh_half/pallas_call | solution.py:144
  51.9 1.3 %collective-permute-done.19 = f32[2,3,128]{2,1,0:T(4,128)S(1)} collective-permute-done((f32[2,3,128]{2,1,0:T(4,128)S(1)}, f32[2,3,128]{2,1,0:T(4,128)S(1)}, u32[]{:S(2)}, u32[]{:S(2)}) %collective-permute-start.19) | collective-permute-done | bytes 3104 | tf_op jit(solution)/shard_map/ppermute | solution.py:488
  53.2 1.9 %collective-permute-start.20 = (f32[4,3,128]{2,1,0:T(4,128)S(1)}, f32[4,3,128]{2,1,0:T(4,128)S(1)}, u32[]{:S(2)}, u32[]{:S(2)}) collective-permute-start(f32[4,3,128]{2,1,0:T(4,128)S(1)} %pad_maximum_fusion.2), channel_id=1, source_target_pairs={{0,2},{2,0},{4,6},{6,4},{1,3},{3,1},{5,7},{7,5},{8,10},{10,8},{12,... | collective-permute-start | bytes 18440 | tf_op jit(solution)/shard_map/ppermute | solution.py:488
  55.1 1.7 %weigh_half.3.w2 = bf16[8,1024,512]{2,1,0:T(8,128)(2,1)S(1)} custom-call(s32[5]{0:T(128)S(1)} %stack.23.pos, bf16[128,8192]{1,0:T(8,128)(2,1)S(1)} %collective-permute-done.18.img, f32[8,8192]{1,0:T(8,128)S(1)} %get-tuple-element.105.cos, f32[8,8192]{1,0:T(8,128)S(1)} %get-tuple-element.104.sin, ...), custom_call_target="tpu_custom_call", output_to_operand_aliasing={{}: (4, {})} | custom-call | bytes 4194304 | tf_op jit(solution)/shard_map/weigh_half/pallas_call | solution.py:144
  56.9 4.0 %collective-permute-start.21 = (f32[8,3,128]{2,1,0:T(4,128)S(1)}, f32[8,3,128]{2,1,0:T(4,128)S(1)}, u32[]{:S(2)}, u32[]{:S(2)}) collective-permute-start(f32[8,3,128]{2,1,0:T(4,128)S(1)} %pad_maximum_fusion.1), channel_id=1, source_target_pairs={{0,6},{2,4},{4,2},{6,0},{1,7},{3,5},{5,3},{7,1},{8,14},{10,12},{12... | collective-permute-start | bytes 36872 | tf_op jit(solution)/shard_map/ppermute | solution.py:488
  60.9 0.9 route.1.seg
  61.8 0.9 collective-permute-done.21
  62.6 11.1 %gather.1 = (bf16[512,256]{1,0:T(8,128)(2,1)S(1)}, bf16[8,768,256]{2,1,0:T(8,128)(2,1)S(1)}, f32[1,128]{1,0:T(1,128)}, f32[1,1]{1,0:T(1,128)}) custom-call(s32[5]{0:T(128)S(1)} %stack.23.pos, f32[16,3,128]{2,1,0:T(4,128)S(1)} %pad_maximum_fusion.pieces, f32[384,1024]{1,0:T(8,128)S(1)} %get-tuple-element.95.e, f32[384,1024]{1,0:T(8,128)S(1)} %collective-permute-done.22.e2, ...), custom_call_target="tpu_custom_call" | custom-call | flops 8589934592 | bytes 1048576 | tf_op jit(solution)/shard_map/gather/pallas_call | solution.py:352
  73.7 2.3 %keep.1 = f32[512,256]{1,0:T(8,128)S(1)} custom-call(s32[5]{0:T(128)S(1)} %stack.23.pos, bf16[8,768,256]{2,1,0:T(8,128)(2,1)S(1)} %get-tuple-element.98.store, s32[2,32,384]{2,1,0:T(8,128)S(1)} %route.1.seg), custom_call_target="tpu_custom_call" | custom-call | flops 2147483648 | bytes 1048576 | tf_op jit(solution)/shard_map/keep/pallas_call | solution.py:385
  76.0 0.1 fusion
  76.1 18.8 %all_to_all.5.got = bf16[64,8,256]{2,1,0:T(8,128)(2,1)S(1)} all-to-all(bf16[64,8,256]{2,1,0:T(8,128)(2,1)S(1)} %fusion), channel_id=1, replica_groups=mesh['xh'=2,'y'=4,'c'=2,'z'=4,'xl'=2] {'xh','y','z','xl'}, dimensions={0} | all-to-all | bytes 524288 | tf_op jit(solution)/shard_map/all_to_all | solution.py:500
  94.9 1.7 %volume.1 = f32[1,512]{1,0:T(1,128)} custom-call(bf16[64,8,256]{2,1,0:T(8,128)(2,1)S(1)} %all_to_all.5.got, bf16[1,8,256,512]{3,2,1,0:T(8,128)(2,1)S(1)} %copy-done.1, f32[1,1]{1,0:T(1,128)} %get-tuple-element.100.count), custom_call_target="tpu_custom_call" | custom-call | tf_op jit(solution)/shard_map/volume/pallas_call | solution.py:411
  (37 shorter events, 0.2 us)
Async XLA Ops:
  0.6 9.9 %copy-start.3 = (f32[2]{0:T(128)S(1)}, f32[2]{0:T(128)}, u32[]{:S(2)}) copy-start(f32[2]{0:T(128)} %constant.29.clone) | copy-start | bytes 28
  0.6 10.0 %copy-start.2 = (f32[8192]{0:T(1024)S(1)}, f32[8192]{0:T(1024)}, u32[]{:S(2)}) copy-start(f32[8192]{0:T(1024)} %param.10) | copy-start | bytes 98308
  0.8 10.0 %copy-start = (bf16[128,8192]{1,0:T(8,128)(2,1)S(1)}, bf16[128,8192]{1,0:T(8,128)(2,1)}, u32[]{:S(2)}) copy-start(bf16[128,8192]{1,0:T(8,128)(2,1)} %img.1) | copy-start | bytes 6291460
  2.6 18.2 %collective-permute-start.7 = (bf16[392,512]{1,0:T(8,128)(2,1)S(1)}, bf16[392,512]{1,0:T(8,128)(2,1)S(1)}, u32[]{:S(2)}, u32[]{:S(2)}) collective-permute-start(bf16[392,512]{1,0:T(8,128)(2,1)S(1)} %slice.10.refs_0_), channel_id=1, source_target_pairs={{0,8},{8,0},{1,9},{9,1},{2,10},{10,2},{3,11},{11,3},{4,12},{12,4},... | collective-permute-start | bytes 1204232 | tf_op jit(solution)/shard_map/ppermute | solution.py:425
  2.7 13.1 %collective-permute-start = (bf16[392,512]{1,0:T(8,128)(2,1)S(1)}, bf16[392,512]{1,0:T(8,128)(2,1)S(1)}, u32[]{:S(2)}, u32[]{:S(2)}) collective-permute-start(bf16[392,512]{1,0:T(8,128)(2,1)S(1)} %slice.10.refs_0_), channel_id=1, source_target_pairs={{0,16},{16,32},{32,48},{48,0},{1,17},{17,33},{33,49},{49,1},{2,18}... | collective-permute-start | bytes 1204232 | tf_op jit(solution)/shard_map/ppermute | solution.py:421
  4.5 12.8 %collective-permute-start.5 = (bf16[392,512]{1,0:T(8,128)(2,1)S(1)}, bf16[392,512]{1,0:T(8,128)(2,1)S(1)}, u32[]{:S(2)}, u32[]{:S(2)}) collective-permute-start(bf16[392,512]{1,0:T(8,128)(2,1)S(1)} %slice.10.refs_0_), channel_id=1, source_target_pairs={{0,64},{64,0},{1,65},{65,1},{2,66},{66,2},{3,67},{67,3},{4,68},{68... | collective-permute-start | bytes 1204232 | tf_op jit(solution)/shard_map/ppermute | solution.py:425
  7.5 11.1 %collective-permute-start.3 = (bf16[392,512]{1,0:T(8,128)(2,1)S(1)}, bf16[392,512]{1,0:T(8,128)(2,1)S(1)}, u32[]{:S(2)}, u32[]{:S(2)}) collective-permute-start(bf16[392,512]{1,0:T(8,128)(2,1)S(1)} %slice.10.refs_0_), channel_id=1, source_target_pairs={{0,48},{16,0},{32,16},{48,32},{1,49},{17,1},{33,17},{49,33},{2,50}... | collective-permute-start | bytes 1204232 | tf_op jit(solution)/shard_map/ppermute | solution.py:421
  15.8 6.7 %collective-permute-start.2 = (bf16[392,512]{1,0:T(8,128)(2,1)S(1)}, bf16[392,512]{1,0:T(8,128)(2,1)S(1)}, u32[]{:S(2)}, u32[]{:S(2)}) collective-permute-start(bf16[392,512]{1,0:T(8,128)(2,1)S(1)} %collective-permute-done.refs_0_), channel_id=1, source_target_pairs={{0,8},{8,0},{1,9},{9,1},{2,10},{10,2},{3,11},{11,3},{4,12},{12,4},... | collective-permute-start | bytes 1204232 | tf_op jit(solution)/shard_map/ppermute | solution.py:425
  17.3 8.3 %collective-permute-start.6 = (bf16[392,512]{1,0:T(8,128)(2,1)S(1)}, bf16[392,512]{1,0:T(8,128)(2,1)S(1)}, u32[]{:S(2)}, u32[]{:S(2)}) collective-permute-start(bf16[392,512]{1,0:T(8,128)(2,1)S(1)} %collective-permute-done.5.refs_4_), channel_id=1, source_target_pairs={{0,8},{8,0},{1,9},{9,1},{2,10},{10,2},{3,11},{11,3},{4,12},{12,4},... | collective-permute-start | bytes 1204232 | tf_op jit(solution)/shard_map/ppermute | solution.py:425
  18.5 7.1 %collective-permute-start.4 = (bf16[392,512]{1,0:T(8,128)(2,1)S(1)}, bf16[392,512]{1,0:T(8,128)(2,1)S(1)}, u32[]{:S(2)}, u32[]{:S(2)}) collective-permute-start(bf16[392,512]{1,0:T(8,128)(2,1)S(1)} %collective-permute-done.3.refs_2_), channel_id=1, source_target_pairs={{0,8},{8,0},{1,9},{9,1},{2,10},{10,2},{3,11},{11,3},{4,12},{12,4},... | collective-permute-start | bytes 1204232 | tf_op jit(solution)/shard_map/ppermute | solution.py:425
  18.5 13.2 %collective-permute-start.1 = (bf16[392,512]{1,0:T(8,128)(2,1)S(1)}, bf16[392,512]{1,0:T(8,128)(2,1)S(1)}, u32[]{:S(2)}, u32[]{:S(2)}) collective-permute-start(bf16[392,512]{1,0:T(8,128)(2,1)S(1)} %collective-permute-done.refs_0_), channel_id=1, source_target_pairs={{0,64},{64,0},{1,65},{65,1},{2,66},{66,2},{3,67},{67,3},{4,68},{68... | collective-permute-start | bytes 1204232 | tf_op jit(solution)/shard_map/ppermute | solution.py:425
  20.8 12.1 %collective-permute-start.12 = (bf16[392,512]{1,0:T(8,128)(2,1)S(1)}, bf16[392,512]{1,0:T(8,128)(2,1)S(1)}, u32[]{:S(2)}, u32[]{:S(2)}) collective-permute-start(bf16[392,512]{1,0:T(8,128)(2,1)S(1)} %collective-permute-done.refs_0_), channel_id=1, source_target_pairs={{0,16},{16,32},{32,48},{48,0},{1,17},{17,33},{33,49},{49,1},{2,18}... | collective-permute-start | bytes 1204232 | tf_op jit(solution)/shard_map/ppermute | solution.py:421
  22.4 10.6 %collective-permute-start.9 = (bf16[392,512]{1,0:T(8,128)(2,1)S(1)}, bf16[392,512]{1,0:T(8,128)(2,1)S(1)}, u32[]{:S(2)}, u32[]{:S(2)}) collective-permute-start(bf16[392,512]{1,0:T(8,128)(2,1)S(1)} %collective-permute-done.5.refs_4_), channel_id=1, source_target_pairs={{0,48},{16,0},{32,16},{48,32},{1,49},{17,1},{33,17},{49,33},{2,50}... | collective-permute-start | bytes 1204232 | tf_op jit(solution)/shard_map/ppermute | solution.py:421
  31.8 2.7 %collective-permute-start.14 = (bf16[392,512]{1,0:T(8,128)(2,1)S(1)}, bf16[392,512]{1,0:T(8,128)(2,1)S(1)}, u32[]{:S(2)}, u32[]{:S(2)}) collective-permute-start(bf16[392,512]{1,0:T(8,128)(2,1)S(1)} %collective-permute-done.1.refs_0_), channel_id=1, source_target_pairs={{0,8},{8,0},{1,9},{9,1},{2,10},{10,2},{3,11},{11,3},{4,12},{12,4},... | collective-permute-start | bytes 1204232 | tf_op jit(solution)/shard_map/ppermute | solution.py:425
  31.8 17.8 %collective-permute-start.18 = (bf16[128,8192]{1,0:T(8,128)(2,1)S(1)}, bf16[128,8192]{1,0:T(8,128)(2,1)S(1)}, u32[]{:S(2)}, u32[]{:S(2)}) collective-permute-start(bf16[128,8192]{1,0:T(8,128)(2,1)S(1)} %copy-done), channel_id=1, source_target_pairs={{0,8},{8,0},{1,9},{9,1},{2,10},{10,2},{3,11},{11,3},{4,12},{12,4},... | collective-permute-start | bytes 6291464 | tf_op jit(solution)/shard_map/ppermute | solution.py:425
  33.0 5.5 %collective-permute-start.13 = (bf16[392,512]{1,0:T(8,128)(2,1)S(1)}, bf16[392,512]{1,0:T(8,128)(2,1)S(1)}, u32[]{:S(2)}, u32[]{:S(2)}) collective-permute-start(bf16[392,512]{1,0:T(8,128)(2,1)S(1)} %collective-permute-done.12.refs_0_), channel_id=1, source_target_pairs={{0,8},{8,0},{1,9},{9,1},{2,10},{10,2},{3,11},{11,3},{4,12},{12,4},... | collective-permute-start | bytes 1204232 | tf_op jit(solution)/shard_map/ppermute | solution.py:425
  33.1 7.0 %collective-permute-start.11 = (bf16[392,512]{1,0:T(8,128)(2,1)S(1)}, bf16[392,512]{1,0:T(8,128)(2,1)S(1)}, u32[]{:S(2)}, u32[]{:S(2)}) collective-permute-start(bf16[392,512]{1,0:T(8,128)(2,1)S(1)} %collective-permute-done.9.refs_0_), channel_id=1, source_target_pairs={{0,8},{8,0},{1,9},{9,1},{2,10},{10,2},{3,11},{11,3},{4,12},{12,4},... | collective-permute-start | bytes 1204232 | tf_op jit(solution)/shard_map/ppermute | solution.py:425
  33.5 8.9 %collective-permute-start.8 = (bf16[224,512]{1,0:T(8,128)(2,1)S(1)}, bf16[224,512]{1,0:T(8,128)(2,1)S(1)}, u32[]{:S(2)}, u32[]{:S(2)}) collective-permute-start(bf16[224,512]{1,0:T(8,128)(2,1)S(1)} %slice.7), channel_id=1, source_target_pairs={{0,16},{16,32},{32,48},{48,0},{1,17},{17,33},{33,49},{49,1},{2,18}... | collective-permute-start | bytes 688136 | tf_op jit(solution)/shard_map/ppermute | solution.py:421
  34.5 7.2 %collective-permute-start.10 = (bf16[168,512]{1,0:T(8,128)(2,1)S(1)}, bf16[168,512]{1,0:T(8,128)(2,1)S(1)}, u32[]{:S(2)}, u32[]{:S(2)}) collective-permute-start(bf16[168,512]{1,0:T(8,128)(2,1)S(1)} %slice.9), channel_id=1, source_target_pairs={{0,48},{16,0},{32,16},{48,32},{1,49},{17,1},{33,17},{49,33},{2,50}... | collective-permute-start | bytes 516104 | tf_op jit(solution)/shard_map/ppermute | solution.py:421
  42.4 1.9 %collective-permute-start.15 = (bf16[224,512]{1,0:T(8,128)(2,1)S(1)}, bf16[224,512]{1,0:T(8,128)(2,1)S(1)}, u32[]{:S(2)}, u32[]{:S(2)}) collective-permute-start(bf16[224,512]{1,0:T(8,128)(2,1)S(1)} %collective-permute-done.8.refs_0_), channel_id=1, source_target_pairs={{0,8},{8,0},{1,9},{9,1},{2,10},{10,2},{3,11},{11,3},{4,12},{12,4},... | collective-permute-start | bytes 688136 | tf_op jit(solution)/shard_map/ppermute | solution.py:425
  42.4 1.9 %collective-permute-start.16 = (bf16[168,512]{1,0:T(8,128)(2,1)S(1)}, bf16[168,512]{1,0:T(8,128)(2,1)S(1)}, u32[]{:S(2)}, u32[]{:S(2)}) collective-permute-start(bf16[168,512]{1,0:T(8,128)(2,1)S(1)} %collective-permute-done.10.refs_1_), channel_id=1, source_target_pairs={{0,8},{8,0},{1,9},{9,1},{2,10},{10,2},{3,11},{11,3},{4,12},{12,4},... | collective-permute-start | bytes 516104 | tf_op jit(solution)/shard_map/ppermute | solution.py:425
  46.0 16.6 %collective-permute-start.22 = (f32[384,1024]{1,0:T(8,128)S(1)}, f32[384,1024]{1,0:T(8,128)S(1)}, u32[]{:S(2)}, u32[]{:S(2)}) collective-permute-start(f32[384,1024]{1,0:T(8,128)S(1)} %get-tuple-element.95.e), channel_id=1, source_target_pairs={{0,8},{8,0},{1,9},{9,1},{2,10},{10,2},{3,11},{11,3},{4,12},{12,4},... | collective-permute-start | bytes 4718600 | tf_op jit(solution)/shard_map/ppermute | solution.py:425
  46.1 3.4 %collective-permute-start.17 = (f32[1,3,128]{2,1,0:T(4,128)S(1)}, f32[1,3,128]{2,1,0:T(4,128)S(1)}, u32[]{:S(2)}, u32[]{:S(2)}) collective-permute-start(f32[1,3,128]{2,1,0:T(4,128)S(1)} %get-tuple-element.89), channel_id=1, source_target_pairs={{0,8},{8,0},{1,9},{9,1},{2,10},{10,2},{3,11},{11,3},{4,12},{12,4},... | collective-permute-start | bytes 4616 | tf_op jit(solution)/shard_map/ppermute | solution.py:425
  49.5 3.7 %collective-permute-start.19 = (f32[2,3,128]{2,1,0:T(4,128)S(1)}, f32[2,3,128]{2,1,0:T(4,128)S(1)}, u32[]{:S(2)}, u32[]{:S(2)}) collective-permute-start(f32[2,3,128]{2,1,0:T(4,128)S(1)} %pad_maximum_fusion.3), channel_id=1, source_target_pairs={{0,1},{1,0},{2,3},{3,2},{4,5},{5,4},{6,7},{7,6},{8,9},{9,8},{10,11... | collective-permute-start | bytes 9224 | tf_op jit(solution)/shard_map/ppermute | solution.py:488
  53.2 3.7 %collective-permute-start.20 = (f32[4,3,128]{2,1,0:T(4,128)S(1)}, f32[4,3,128]{2,1,0:T(4,128)S(1)}, u32[]{:S(2)}, u32[]{:S(2)}) collective-permute-start(f32[4,3,128]{2,1,0:T(4,128)S(1)} %pad_maximum_fusion.2), channel_id=1, source_target_pairs={{0,2},{2,0},{4,6},{6,4},{1,3},{3,1},{5,7},{7,5},{8,10},{10,8},{12,... | collective-permute-start | bytes 18440 | tf_op jit(solution)/shard_map/ppermute | solution.py:488
  56.9 5.8 %collective-permute-start.21 = (f32[8,3,128]{2,1,0:T(4,128)S(1)}, f32[8,3,128]{2,1,0:T(4,128)S(1)}, u32[]{:S(2)}, u32[]{:S(2)}) collective-permute-start(f32[8,3,128]{2,1,0:T(4,128)S(1)} %pad_maximum_fusion.1), channel_id=1, source_target_pairs={{0,6},{2,4},{4,2},{6,0},{1,7},{3,5},{5,3},{7,1},{8,14},{10,12},{12... | collective-permute-start | bytes 36872 | tf_op jit(solution)/shard_map/ppermute | solution.py:488
  73.7 2.3 %collective-permute-start.23 = (bf16[512,256]{1,0:T(8,128)(2,1)S(1)}, bf16[512,256]{1,0:T(8,128)(2,1)S(1)}, u32[]{:S(2)}, u32[]{:S(2)}) collective-permute-start(bf16[512,256]{1,0:T(8,128)(2,1)S(1)} %get-tuple-element.99), channel_id=1, source_target_pairs={{0,8},{8,0},{1,9},{9,1},{2,10},{10,2},{3,11},{11,3},{4,12},{12,4},... | collective-permute-start | bytes 786440 | tf_op jit(solution)/shard_map/ppermute | solution.py:425
  73.7 21.2 %copy-start.1 = (bf16[1,8,256,512]{3,2,1,0:T(8,128)(2,1)S(1)}, bf16[1,8,256,512]{3,2,1,0:T(8,128)(2,1)}, u32[]{:S(2)}) copy-start(bf16[1,8,256,512]{3,2,1,0:T(8,128)(2,1)} %interp.1) | copy-start | bytes 6291460
